TPU v7x, 512 devices: a whole 4x4x16 slice. The times are simulated.
512 devices in a mesh: gx: 32 (over z, core), gy: 4 (over x), gz: 4 (over y).
Axes of the slice: x: 4, y: 4, z: 16, core: 2. Of those that a mesh axis runs over, the one named last changes fastest.
Arguments:
- adjoint_final: float32 [16, 512, 512], P('gz', 'gx', 'gy'), may hold values from -6 to 6
- conductivity: float32 [3, 16, 512, 512], P(None, 'gz', 'gx', 'gy'), may hold values from 0.05 to 1
- step_ratio: float32 [16, 512, 512], P('gz', 'gx', 'gy'), may hold values from 0.04 to 0.16
- refine_rate: float32 [16, 512, 512], P('gz', 'gx', 'gy'), may hold values from 0.05 to 0.24
- residual: float32 [4, 8192], P(None, ('gx', 'gy')), may hold values from -6 to 6
- sensor_tile: int32 [8192], P(('gx', 'gy')), may hold values from 0 to 127, as said below
- sensor_cell: int32 [8192], P(('gx', 'gy')), may hold values from 0 to 32767
- substeps: int32 [32, 4], replicated, may hold values from 1 to 6, as said below
Outputs:
- adjoint_start: float32 [16, 512, 512], P('gz', 'gx', 'gy')
- sensitivity: float32 [16, 512, 512], P('gz', 'gx', 'gy')
Inputs may be any that keep to these rules, and one draw needn't show every extreme that they name: `sensor_tile`: tiles are numbered ix * 4 + iy. Among the 64 sensors of each aligned block at most 4 name one tile, and in every block some tile is named by exactly 4 of them. `substeps`: some tile takes 6 sub-steps in every draw.
All inputs are finite; a program needn't handle non-finite values.
Results may differ from a plain program's by a relative error of at most 0.000079.
Values sent between devices are 32-bit elements; how exact they have to be, the bound alone decides.
No kernel may reach another device: no remote copies, remote signals or barrier semaphores. Data moves between devices by JAX's collectives and lax.ppermute only.
A program may use at most 64 MiB of HBM per device.

v0:
```python
import functools

import jax
import jax.numpy as jnp
from jax import lax
from jax.experimental import pallas as pl
from jax.experimental.pallas import tpu as pltpu
from jax.sharding import PartitionSpec as P


F32 = jnp.float32
BF16 = jnp.bfloat16
LANES = 128
WIDE = 32
QUART = LANES // WIDE
MAXSUB = 6
SLOTS = 4
FIELDS = 6
TINY = 1e-30
LIMIT = 24 * 2**20


def iota(shape, dim):
    return lax.broadcasted_iota(jnp.int32, shape, dim)


def harmonic(first, second):
    return 2.0 * first * second / jnp.maximum(first + second, TINY)


def swap(field):
    return jnp.concatenate([field[:, 1:2], field[:, 0:1]], axis=1)


def call(kernel, outs, cost=20000):
    vmem = pl.BlockSpec(memory_space=pltpu.VMEM)

    def run(*args):
        return pl.pallas_call(
            kernel,
            out_shape=[jax.ShapeDtypeStruct(o, F32) for o in outs],
            in_specs=[vmem] * len(args),
            out_specs=[vmem] * len(outs),
            compiler_params=pltpu.CompilerParams(vmem_limit_bytes=LIMIT),
            cost_estimate=pl.CostEstimate(flops=cost, bytes_accessed=cost, transcendentals=0),
        )(*args)

    return run


def pack(gy, residual_ref, tile_ref, cell_ref, out_ref):
    count = residual_ref.shape[1]
    tiles = out_ref.shape[0]
    eye = iota((count, count), 0) == iota((count, count), 1)

    def column(row):
        return jnp.sum(jnp.where(eye, jnp.broadcast_to(row, (count, count)), 0.0), axis=1, keepdims=True)

    named = tile_ref[...]
    tile_row = named.astype(F32)
    tile_col = column(tile_row)
    same = (tile_col == tile_row) & (iota((count, count), 1) < iota((count, count), 0))
    rank = jnp.sum(same.astype(F32), axis=1, keepdims=True).astype(jnp.int32)
    values = [column(residual_ref[s : s + 1, :]) for s in range(4)]
    values.append(column(cell_ref[...].astype(F32) + 1.0))
    lane = iota((count, LANES), 1)
    within = lane % 8
    spread = jnp.zeros((count, LANES), F32)
    for place, value in enumerate(values):
        spread = jnp.where(within == place, value, spread)
    spread = jnp.where((lane % 32) // 8 == rank, spread, 0.0)
    tile_at = iota((tiles, count), 0)
    total = jnp.zeros((tiles, LANES), F32)
    for group, (step, edge) in enumerate(((0, -1), (-1, 0), (1, gy - 1))):
        hit = (named == tile_at + step) & (tile_at % gy != edge)
        part = jnp.where(lane // 32 == group, spread, 0.0)
        total = total + jnp.dot(hit.astype(F32), part, precision=lax.Precision.HIGHEST, preferred_element_type=F32)
    out_ref[...] = total


def stacked(refs, field, layer):
    each = refs[0].shape[1]
    return refs[layer // each][field, layer % each]


def pack_columns(below_ref, own_ref, above_ref, left_ref, right_ref):
    refs = (below_ref, own_ref, above_ref)
    layers = 3 * own_ref.shape[1]
    rows = own_ref.shape[2]
    quarter = iota((rows, LANES), 1) // WIDE
    for j in range(FIELDS * layers // QUART):
        left = right = None
        for q in range(QUART):
            p = j * QUART + q
            plane = stacked(refs, p // layers, p % layers)
            to_left = plane if q == 0 else pltpu.roll(plane, WIDE * q, 1)
            shift = (WIDE * q + WIDE) % LANES
            to_right = plane if shift == 0 else pltpu.roll(plane, shift, 1)
            left = to_left if q == 0 else jnp.where(quarter == q, to_left, left)
            right = to_right if q == 0 else jnp.where(quarter == q, to_right, right)
        left_ref[j] = left
        right_ref[j] = right


def spread_column(columns, at, shape):
    return jnp.broadcast_to(columns[:, at : at + 1], shape)


def sources(layer_axis, own, layers, rows, sensors_ref, steps):
    got = sensors_ref[...]
    blocks = got.shape[0]
    lane = iota((blocks, LANES), 1)
    lane_at = lane.astype(F32)
    cell = got.astype(jnp.int32) - 1
    row_base = (lax.axis_index(layer_axis) * own - own) * rows
    cell_row = ((cell >> 7) - row_base).astype(F32).T
    cell_col = cell & (LANES - 1)
    half = LANES // 2
    group_of = lane // 32
    cell_col = jnp.where(
        group_of == 0,
        cell_col,
        jnp.where(
            group_of == 1,
            jnp.where(cell_col >= LANES - WIDE, cell_col - half, -LANES),
            jnp.where(cell_col < WIDE, cell_col, -LANES),
        ),
    ).astype(F32)
    row_at = iota((layers * rows, blocks), 0).astype(F32)
    high = got.astype(BF16)
    values = (high, (got - high.astype(F32)).astype(BF16))
    onehots, tables = ([], []), ([], [])
    for group in range(3):
        for slot in range(SLOTS):
            base = group * 32 + slot * 8
            onehots[group > 0].append((cell_row[base + 4 : base + 5, :] == row_at).astype(F32).astype(BF16))
            at = spread_column(cell_col, base + 4, lane.shape)
            pairs = (0, half) if group > 0 and len(steps) > 1 else (0,)
            place = [(at == lane_at - by).astype(F32).astype(BF16) for by in pairs]
            line = []
            for part in range(2):
                cells = [spread_column(values[part], base + s, lane.shape) for s in steps]
                for k in range(0, len(cells), len(place)):
                    line.append(functools.reduce(jnp.add, [m * v for m, v in zip(place, cells[k : k + len(place)])]))
            tables[group > 0].append(jnp.concatenate(line, axis=1))
    sums = []
    for onehot, table in zip(onehots, tables):
        both = jnp.dot(jnp.concatenate(onehot, axis=1), jnp.concatenate(table, axis=0), preferred_element_type=F32)
        width = both.shape[1] // 2
        sums.append(both[:, :width] + both[:, width:])
    centre, side = sums
    lane = iota((layers * rows, LANES), 1)
    out = []
    for s in range(len(steps)):
        tile = side[:, (s // 2) * LANES : (s // 2 + 1) * LANES]
        turned = pltpu.roll(tile, half, 1)
        right, left = (tile, turned) if s % 2 == 0 else (turned, tile)
        beside = jnp.where(lane < WIDE, right, jnp.where(lane >= LANES - WIDE, left, 0.0))
        parts = [m.reshape(layers, 1, rows, LANES) for m in (centre[:, s * LANES : (s + 1) * LANES], beside)]
        out.append(jnp.concatenate(parts, axis=1))
    return out


def prepare(axes, substeps_ref, below_ref, own_ref, above_ref, left_ref, right_ref, state_ref, fixed_ref, edge_ref, counts_ref):
    refs = (below_ref, own_ref, above_ref)
    own = own_ref.shape[1]
    layers = 3 * own
    rows = own_ref.shape[2]
    lane = iota((rows, LANES), 1)

    def field(f):
        planes = []
        for l in range(layers):
            p = f * layers + l
            j, q = p // QUART, p % QUART
            from_left = pltpu.roll(left_ref[j], (LANES - WIDE - WIDE * q) % LANES, 1) if q != QUART - 1 else left_ref[j]
            from_right = pltpu.roll(right_ref[j], LANES - WIDE * q, 1) if q != 0 else right_ref[j]
            side = jnp.where(lane < WIDE, from_right, jnp.where(lane >= LANES - WIDE, from_left, 0.0))
            planes.append(jnp.stack([stacked(refs, f, l), side], axis=0))
        return jnp.stack(planes, axis=0)

    at_x, at_y = (lax.axis_index(axis) for axis in axes)
    n_y, n_x = substeps_ref.shape
    named = jnp.where(iota((n_y, n_x), 1) == at_x, substeps_ref[...].astype(F32), 0.0)

    def count(tile):
        rows_of = jnp.sum(jnp.where(iota((n_y, n_x), 0) == tile, named, 0.0), axis=1, keepdims=True)
        return jnp.broadcast_to(jnp.sum(rows_of, axis=0, keepdims=True), (rows, LANES))

    counts_ref[0] = count(at_y)
    counts_ref[1] = jnp.where(lane < LANES // 2, count(at_y + 1), count(at_y - 1))
    shape = (layers, 2, rows, LANES)
    row = iota(shape, 2)
    col = iota(shape, 3)
    state_ref[...] = field(0)
    along_rows = field(1)
    edge_ref[0] = along_rows[:, :, 0:1, :]
    edge_ref[1] = along_rows[:, :, rows - 1 :, :]
    fixed_ref[0] = harmonic(along_rows, jnp.where(row == rows - 1, 0.0, pltpu.roll(along_rows, rows - 1, 2)))
    along_cols = field(2)
    rolled = pltpu.roll(along_cols, LANES - 1, 3)
    fixed_ref[1] = harmonic(along_cols, jnp.where(col == LANES - 1, swap(rolled), rolled))
    along_layers = field(3)
    fixed_ref[2, : layers - 1] = harmonic(along_layers[: layers - 1], along_layers[1:])
    fixed_ref[2, layers - 1 :] = jnp.zeros((1, 2, rows, LANES), F32)
    fixed_ref[3] = field(4)
    fixed_ref[4] = field(5)


def first_source(layer_axis, own, state_in, fixed_ref, edge_ref, sensors_ref, state_ref, up_ref, down_ref):
    layers, _, rows, _ = state_ref.shape
    (source,) = sources(layer_axis, own, layers, rows, sensors_ref, (3,))
    state = state_in[...] + source
    state_ref[...] = state
    weighted = fixed_ref[3] * state
    up_ref[0] = weighted[:, :, 0:1, :]
    up_ref[1] = edge_ref[0]
    down_ref[0] = weighted[:, :, rows - 1 :, :]
    down_ref[1] = edge_ref[1]


def other_sources(layer_axis, own, sensors_ref, source_ref):
    _, layers, _, rows, _ = source_ref.shape
    for s, source in enumerate(sources(layer_axis, own, layers, rows, sensors_ref, (0, 1, 2))):
        source_ref[s] = source


def step(axis, turn, *refs):
    first, last = turn == 3, turn == 0
    refs = list(refs)
    counts_ref, state_ref, fixed_ref, above_ref, below_ref = refs[:5]
    refs = refs[5:]
    if first:
        own_up_ref, own_down_ref = refs[:2]
    else:
        row_edge_ref, sens_ref = refs[:2]
    refs = refs[2:]
    if not last:
        source_ref = refs[0]
        refs = refs[1:]
    if first:
        state_out, up_out, down_out, sens_out, edge_out = refs
    elif not last:
        state_out, up_out, down_out, sens_out = refs
    else:
        state_out, sens_out = refs
    at_x, n_x = lax.axis_index(axis), lax.axis_size(axis)
    layers, _, rows, _ = state_ref.shape
    total = fixed_ref.shape[1]
    low = (total - layers) // 2
    span = slice(low, low + layers)
    inner = slice(low + 1, low + layers - 1)
    state = state_ref[...]
    weighted = fixed_ref[3, span] * state
    if first:
        edges = []
        for mine, other, there in ((own_up_ref, above_ref, at_x > 0), (own_down_ref, below_ref, at_x < n_x - 1)):
            edges.append(harmonic(mine[1], jnp.where(there, other[1], 0.0)))
        edge_out[0] = edges[0]
        edge_out[1] = edges[1]
        over, under = edges[0][1:-1], edges[1][1:-1]
    else:
        over, under = row_edge_ref[0, inner], row_edge_ref[1, inner]
    shape = (layers - 2, 2, rows, LANES)
    row, col = iota(shape, 2), iota(shape, 3)
    across = weighted[1:-1]
    halo_over = above_ref[0, 1:-1]
    halo_under = below_ref[0, 1:-1]
    flux = fixed_ref[0, inner] * (pltpu.roll(across, rows - 1, 2) - across)
    edge_low = over * (across[:, :, 0:1, :] - halo_over)
    edge_high = under * (halo_under - across[:, :, rows - 1 :, :])
    flux = jnp.where(row == rows - 1, edge_high, flux)
    change = flux - jnp.where(row == 0, edge_low, pltpu.roll(flux, 1, 2))
    rolled = pltpu.roll(across, LANES - 1, 3)
    flux = fixed_ref[1, inner] * (jnp.where(col == LANES - 1, swap(rolled), rolled) - across)
    rolled = pltpu.roll(flux, 1, 3)
    change = change + (flux - jnp.where(col == 0, swap(rolled), rolled))
    flux = fixed_ref[2, low : low + layers - 1] * (weighted[1:] - weighted[:-1])
    change = change + (flux[1:] - flux[:-1])
    state = state[1:-1] + change
    kept = slice(0, 1) if last else slice(0, 2)
    state = state[:, kept]
    rate = fixed_ref[4, inner, kept]
    counts = counts_ref[kept][None]
    keep_own = 1.0 - 4.0 * rate
    half = rows // 2
    part = state.shape[:2] + (half, LANES)
    row, col = iota(part, 2), iota(part, 3)

    def one_turn(at, now):
        top, low_half = (rate[:, :, h : h + half] * now[:, :, h : h + half] for h in (0, half))
        up = pltpu.roll(top, half - 1, 2), pltpu.roll(low_half, half - 1, 2)
        down = pltpu.roll(top, 1, 2), pltpu.roll(low_half, 1, 2)
        near = (
            jnp.where(row == half - 1, up[1], up[0]) + jnp.where(row == 0, top, down[0]),
            jnp.where(row == half - 1, low_half, up[1]) + jnp.where(row == 0, down[0], down[1]),
        )
        parts = []
        for h, (v, rowwise) in enumerate(zip((top, low_half), near)):
            colwise = jnp.where(col == LANES - 1, v, pltpu.roll(v, LANES - 1, 3)) + jnp.where(col == 0, v, pltpu.roll(v, 1, 3))
            here = slice(h * half, (h + 1) * half)
            after = keep_own[:, :, here] * now[:, :, here] + (rowwise + colwise)
            parts.append(after if at == 0 else jnp.where(counts[:, :, here] > at, after, now[:, :, here]))
        return jnp.concatenate(parts, axis=2)

    for at in range(MAXSUB):
        state = one_turn(at, state)
    own = total // 3
    keep = slice((layers - 2 - own) // 2, (layers - 2 - own) // 2 + own)
    addend = fixed_ref[3, own : 2 * own, 0] * state[keep, 0]
    sens_out[...] = addend if first else sens_ref[...] + addend
    if last:
        state_out[...] = state[:, 0]
        return
    state = state + source_ref[turn - 1, inner]
    state_out[...] = state
    weighted = fixed_ref[3, inner] * state
    up_out[0] = weighted[:, :, 0:1, :]
    down_out[0] = weighted[:, :, rows - 1 :, :]


def shift(cells, axis, by, wrap):
    count = lax.axis_size(axis)
    pairs = [(i, (i + by) % count) for i in range(count) if wrap or 0 <= i + by < count]
    return lax.ppermute(cells, axis, pairs)


def body(adjoint_final, conductivity, step_ratio, refine_rate, residual, sensor_tile, sensor_cell, substeps):
    own, rows, cols = adjoint_final.shape
    layers = 3 * own
    n_y = lax.axis_size("gy")
    tiles = lax.axis_size("gx") * n_y
    listed = sensor_tile.shape[0]
    (message,) = call(functools.partial(pack, n_y), [(tiles, LANES)])(
        residual, sensor_tile.reshape(1, listed), sensor_cell.reshape(1, listed)
    )
    sensors = lax.all_to_all(message, ("gx", "gy"), 0, 0, tiled=True)
    fields = jnp.concatenate([adjoint_final[None], conductivity, step_ratio[None], refine_rate[None]], axis=0)
    below = shift(fields, "gz", 1, False)
    above = shift(fields, "gz", -1, False)
    packed = (FIELDS * layers // QUART, rows, LANES)
    to_left, to_right = call(pack_columns, [packed, packed])(below, fields, above)
    from_left = shift(to_right, "gy", 1, False)
    from_right = shift(to_left, "gy", -1, False)
    block = (layers, 2, rows, LANES)
    faces = (2, layers, 2, 1, LANES)
    state, fixed, edges, counts = call(
        functools.partial(prepare, ("gx", "gy")), [block, (5,) + block, faces, (2, rows, LANES)]
    )(substeps.T, below, fields, above, from_left, from_right)
    state, up, down = call(functools.partial(first_source, "gz", own), [block, faces, faces])(state, fixed, edges, sensors)
    (source,) = call(functools.partial(other_sources, "gz", own), [(3,) + block])(sensors)
    sens = edge = None
    for turn in range(3, -1, -1):
        over = shift(down, "gx", 1, True)
        under = shift(up, "gx", -1, True)
        depth = state.shape[0] - 2
        args = [counts, state, fixed]
        args += [over, under] + ([up, down] if turn == 3 else [edge, sens])
        if turn > 0:
            args += [source]
        face = (1, depth, 2, 1, LANES)
        if turn == 0:
            outs = [(own, rows, cols), (own, rows, cols)]
        else:
            outs = [(depth, 2, rows, LANES), face, face, (own, rows, cols)]
            if turn == 3:
                outs += [(2, layers, 2, 1, LANES)]
        got = call(functools.partial(step, "gx", turn), outs)(*args)
        if turn == 3:
            state, up, down, sens, edge = got
        elif turn > 0:
            state, up, down, sens = got
        else:
            return tuple(got)


def solution(mesh):
    return jax.shard_map(
        body,
        mesh=mesh,
        in_specs=(
            P("gz", "gx", "gy"),
            P(None, "gz", "gx", "gy"),
            P("gz", "gx", "gy"),
            P("gz", "gx", "gy"),
            P(None, ("gx", "gy")),
            P(("gx", "gy")),
            P(("gx", "gy")),
            P(),
        ),
        out_specs=(P("gz", "gx", "gy"), P("gz", "gx", "gy")),
        check_vma=False,
    )
```

profile of v0, /device:TPU:8, one launch (start us, length us, event | category | flops | bytes accessed | tf_op | source)
XLA Modules:
  0.0 65.9 jit_solution(4202458892030027611)
XLA Ops:
  0.6 0.9 %pad_maximum_fusion.own_ref = f32[6,4,16,128]{3,2,1,0:T(8,128)S(1)} fusion(f32[1,4,16,128]{3,2,1,0:T(8,128)} %bitcast.15, f32[1,4,16,128]{3,2,1,0:T(8,128)} %bitcast.16, f32[3,4,16,128]{3,2,1,0:T(8,128)} %param.9, f32[1,4,16,128]{3,2,1,0:T(8,128)} %bitcast.17), kind=kLoop, calls=%fused_computation | loop fusion | flops 147456 | bytes 393216 | tf_op jit(solution)/shard_map/concatenate | solution.py:338
  1.6 0.0 copy-start.1
  1.6 3.5 %collective-permute-start = (f32[6,4,16,128]{3,2,1,0:T(8,128)S(1)}, f32[6,4,16,128]{3,2,1,0:T(8,128)S(1)}, u32[]{:S(2)}, u32[]{:S(2)}) collective-permute-start(f32[6,4,16,128]{3,2,1,0:T(8,128)S(1)} %pad_maximum_fusion.own_ref), channel_id=1, source_target_pairs={{0,1},{1,2},{2,3},{4,5},{5,6},{6,7},{8,9},{9,10},{10,11},{12,13},{... | collective-permute-start | bytes 589832 | tf_op jit(solution)/shard_map/ppermute | solution.py:325
  5.1 5.5 %collective-permute-start.1 = (f32[6,4,16,128]{3,2,1,0:T(8,128)S(1)}, f32[6,4,16,128]{3,2,1,0:T(8,128)S(1)}, u32[]{:S(2)}, u32[]{:S(2)}) collective-permute-start(f32[6,4,16,128]{3,2,1,0:T(8,128)S(1)} %pad_maximum_fusion.own_ref), channel_id=1, source_target_pairs={{1,0},{2,1},{3,2},{5,4},{6,5},{7,6},{9,8},{10,9},{11,10},{13,12},{... | collective-permute-start | bytes 589832 | tf_op jit(solution)/shard_map/ppermute | solution.py:325
  10.6 0.0 copy-start.2
  10.6 0.0 copy-start.3
  10.6 0.0 copy-done.1
  10.6 0.6 copy-done.2
  11.3 0.0 copy-done.3
  11.3 1.1 %shard_map.97 = f32[128,128]{1,0:T(8,128)} custom-call(f32[4,64]{1,0:T(4,128)S(1)} %copy-done.1, s32[1,64]{1,0:T(1,128)S(1)} %bitcast.13, s32[1,64]{1,0:T(1,128)S(1)} %bitcast.14), custom_call_target="tpu_custom_call" | custom-call | flops 20000 | bytes 20000 | tf_op jit(solution)/shard_map/pallas_call | solution.py:39
  12.4 16.6 %all-to-all-start = ((f32[128,1,128]{2,1,0:T(1,128)}), f32[128,1,128]{2,1,0:T(1,128)S(1)}, u32[]{:S(2)}, u32[]{:S(2)}) async-start(f32[128,1,128]{2,1,0:T(1,128)} %bitcast.7), calls=%async_computation | async-start | bytes 131072 | tf_op jit(solution)/shard_map/all_to_all | solution.py:337
  29.0 0.0 collective-permute-done.below_ref
  29.0 0.0 collective-permute-done.1.above_ref
  29.0 0.3 shard_map.95
  29.3 0.0 copy-start
  29.3 3.0 %collective-permute-start.2 = (f32[18,16,128]{2,1,0:T(8,128)S(1)}, f32[18,16,128]{2,1,0:T(8,128)S(1)}, u32[]{:S(2)}, u32[]{:S(2)}) collective-permute-start(f32[18,16,128]{2,1,0:T(8,128)S(1)} %get-tuple-element.24), channel_id=1, source_target_pairs={{0,4},{4,8},{8,12},{1,5},{5,9},{9,13},{2,6},{6,10},{10,14},{3,7},{... | collective-permute-start | bytes 442376 | tf_op jit(solution)/shard_map/ppermute | solution.py:325
  32.4 1.3 %collective-permute-start.3 = (f32[18,16,128]{2,1,0:T(8,128)S(1)}, f32[18,16,128]{2,1,0:T(8,128)S(1)}, u32[]{:S(2)}, u32[]{:S(2)}) collective-permute-start(f32[18,16,128]{2,1,0:T(8,128)S(1)} %get-tuple-element.25), channel_id=1, source_target_pairs={{4,0},{8,4},{12,8},{5,1},{9,5},{13,9},{6,2},{10,6},{14,10},{7,3},{... | collective-permute-start | bytes 442376 | tf_op jit(solution)/shard_map/ppermute | solution.py:325
  33.7 2.3 %collective-permute-done.2.left_ref = f32[18,16,128]{2,1,0:T(8,128)S(1)} collective-permute-done((f32[18,16,128]{2,1,0:T(8,128)S(1)}, f32[18,16,128]{2,1,0:T(8,128)S(1)}, u32[]{:S(2)}, u32[]{:S(2)}) %collective-permute-start.2) | collective-permute-done | bytes 147488 | tf_op jit(solution)/shard_map/ppermute | solution.py:325
  36.0 4.1 %collective-permute-done.3.right_ref = f32[18,16,128]{2,1,0:T(8,128)S(1)} collective-permute-done((f32[18,16,128]{2,1,0:T(8,128)S(1)}, f32[18,16,128]{2,1,0:T(8,128)S(1)}, u32[]{:S(2)}, u32[]{:S(2)}) %collective-permute-start.3) | collective-permute-done | bytes 147488 | tf_op jit(solution)/shard_map/ppermute | solution.py:325
  40.1 0.0 copy-done
  40.1 0.4 shard_map.96
  40.5 3.3 %all-to-all-done = f32[128,1,128]{2,1,0:T(1,128)S(1)} async-done(((f32[128,1,128]{2,1,0:T(1,128)}), f32[128,1,128]{2,1,0:T(1,128)S(1)}, u32[]{:S(2)}, u32[]{:S(2)}) %all-to-all-start) | async-done | bytes 65568 | tf_op jit(solution)/shard_map/all_to_all | solution.py:337
  43.9 0.9 %shard_map.98 = (f32[12,2,16,128]{3,2,1,0:T(8,128)S(1)}, f32[2,12,2,1,128]{4,3,2,1,0:T(1,128)S(1)}, f32[2,12,2,1,128]{4,3,2,1,0:T(1,128)S(1)}) custom-call(f32[12,2,16,128]{3,2,1,0:T(8,128)S(1)} %get-tuple-element.27.state_in, f32[5,12,2,16,128]{4,3,2,1,0:T(8,128)S(1)} %get-tuple-element.28.fixed_ref.refs_2_, ...), custom_call_target="tpu_custom_call" | custom-call | flops 20000 | bytes 20000 | tf_op jit(solution)/shard_map/pallas_call | solution.py:39
  44.7 0.5 collective-permute-start.4
  45.2 2.5 %collective-permute-start.5 = (f32[2,12,2,1,128]{4,3,2,1,0:T(1,128)S(1)}, f32[2,12,2,1,128]{4,3,2,1,0:T(1,128)S(1)}, u32[]{:S(2)}, u32[]{:S(2)}) collective-permute-start(f32[2,12,2,1,128]{4,3,2,1,0:T(1,128)S(1)} %get-tuple-element.32.refs_5_), channel_id=1, source_target_pairs={{0,496},{16,0},{32,16},{48,32},{64,48},{80,64},{96,80},{112,96},{1... | collective-permute-start | bytes 73736 | tf_op jit(solution)/shard_map/ppermute | solution.py:325
  47.7 1.5 %shard_map.99.refs_7_ = f32[3,12,2,16,128]{4,3,2,1,0:T(8,128)S(1)} custom-call(f32[128,128]{1,0:T(8,128)S(1)} %bitcast.11), custom_call_target="tpu_custom_call" | custom-call | flops 20000 | bytes 20000 | tf_op jit(solution)/shard_map/pallas_call | solution.py:39
  49.2 0.0 collective-permute-done.4.refs_3_
  49.2 0.0 collective-permute-done.5.refs_4_
  49.2 0.9 %shard_map.100 = (f32[10,2,16,128]{3,2,1,0:T(8,128)S(1)}, f32[1,10,2,1,128]{4,3,2,1,0:T(1,128)S(1)}, f32[1,10,2,1,128]{4,3,2,1,0:T(1,128)S(1)}, f32[4,16,128]{2,1,0:T(8,128)S(1)}, f32[2,12,2,1,128]{4,3,2,1,0:T(1,128)S(1)}) custom-call(f32[2,16,128]{2,1,0:T(8,128)S(1)} %get-tuple-element.26.refs_0_, f32[12,2,16,128]{3,2,1,0:T(8,128)S(1)} %get-tuple-element.30.refs_1_, ...), custom_call_target="tpu_custom_call" | custom-call | flops 20000 | bytes 20000 | tf_op jit(solution)/shard_map/pallas_call | solution.py:39
  50.1 0.0 collective-permute-start.6
  50.2 3.0 %collective-permute-start.7 = (f32[1,10,2,1,128]{4,3,2,1,0:T(1,128)S(1)}, f32[1,10,2,1,128]{4,3,2,1,0:T(1,128)S(1)}, u32[]{:S(2)}, u32[]{:S(2)}) collective-permute-start(f32[1,10,2,1,128]{4,3,2,1,0:T(1,128)S(1)} %get-tuple-element.35), channel_id=1, source_target_pairs={{0,496},{16,0},{32,16},{48,32},{64,48},{80,64},{96,80},{112,96},{1... | collective-permute-start | bytes 30728 | tf_op jit(solution)/shard_map/ppermute | solution.py:325
  53.1 1.3 %collective-permute-done.6.refs_3_ = f32[1,10,2,1,128]{4,3,2,1,0:T(1,128)S(1)} collective-permute-done((f32[1,10,2,1,128]{4,3,2,1,0:T(1,128)S(1)}, f32[1,10,2,1,128]{4,3,2,1,0:T(1,128)S(1)}, u32[]{:S(2)}, u32[]{:S(2)}) %collective-permute-start.6) | collective-permute-done | bytes 10272 | tf_op jit(solution)/shard_map/ppermute | solution.py:325
  54.5 0.0 collective-permute-done.7.refs_4_
  54.5 0.8 %shard_map.101 = (f32[8,2,16,128]{3,2,1,0:T(8,128)S(1)}, f32[1,8,2,1,128]{4,3,2,1,0:T(1,128)S(1)}, f32[1,8,2,1,128]{4,3,2,1,0:T(1,128)S(1)}, f32[4,16,128]{2,1,0:T(8,128)S(1)}) custom-call(f32[2,16,128]{2,1,0:T(8,128)S(1)} %get-tuple-element.26.refs_0_, f32[10,2,16,128]{3,2,1,0:T(8,128)S(1)} %get-tuple-element.33.refs_1_, ...), custom_call_target="tpu_custom_call" | custom-call | flops 20000 | bytes 20000 | tf_op jit(solution)/shard_map/pallas_call | solution.py:39
  55.3 0.0 collective-permute-start.8
  55.3 2.9 %collective-permute-start.9 = (f32[1,8,2,1,128]{4,3,2,1,0:T(1,128)S(1)}, f32[1,8,2,1,128]{4,3,2,1,0:T(1,128)S(1)}, u32[]{:S(2)}, u32[]{:S(2)}) collective-permute-start(f32[1,8,2,1,128]{4,3,2,1,0:T(1,128)S(1)} %get-tuple-element.40), channel_id=1, source_target_pairs={{0,496},{16,0},{32,16},{48,32},{64,48},{80,64},{96,80},{112,96},{1... | collective-permute-start | bytes 24584 | tf_op jit(solution)/shard_map/ppermute | solution.py:325
  58.3 1.3 %collective-permute-done.8.refs_3_ = f32[1,8,2,1,128]{4,3,2,1,0:T(1,128)S(1)} collective-permute-done((f32[1,8,2,1,128]{4,3,2,1,0:T(1,128)S(1)}, f32[1,8,2,1,128]{4,3,2,1,0:T(1,128)S(1)}, u32[]{:S(2)}, u32[]{:S(2)}) %collective-permute-start.8) | collective-permute-done | bytes 8224 | tf_op jit(solution)/shard_map/ppermute | solution.py:325
  59.6 0.0 collective-permute-done.9.refs_4_
  59.6 0.7 %shard_map.102 = (f32[6,2,16,128]{3,2,1,0:T(8,128)S(1)}, f32[1,6,2,1,128]{4,3,2,1,0:T(1,128)S(1)}, f32[1,6,2,1,128]{4,3,2,1,0:T(1,128)S(1)}, f32[4,16,128]{2,1,0:T(8,128)S(1)}) custom-call(f32[2,16,128]{2,1,0:T(8,128)S(1)} %get-tuple-element.26.refs_0_, f32[8,2,16,128]{3,2,1,0:T(8,128)S(1)} %get-tuple-element.38.refs_1_, ...), custom_call_target="tpu_custom_call" | custom-call | flops 20000 | bytes 20000 | tf_op jit(solution)/shard_map/pallas_call | solution.py:39
  60.4 0.0 collective-permute-start.10
  60.4 2.9 %collective-permute-start.11 = (f32[1,6,2,1,128]{4,3,2,1,0:T(1,128)S(1)}, f32[1,6,2,1,128]{4,3,2,1,0:T(1,128)S(1)}, u32[]{:S(2)}, u32[]{:S(2)}) collective-permute-start(f32[1,6,2,1,128]{4,3,2,1,0:T(1,128)S(1)} %get-tuple-element.44), channel_id=1, source_target_pairs={{0,496},{16,0},{32,16},{48,32},{64,48},{80,64},{96,80},{112,96},{1... | collective-permute-start | bytes 18440 | tf_op jit(solution)/shard_map/ppermute | solution.py:325
  63.3 1.3 %collective-permute-done.10.refs_3_ = f32[1,6,2,1,128]{4,3,2,1,0:T(1,128)S(1)} collective-permute-done((f32[1,6,2,1,128]{4,3,2,1,0:T(1,128)S(1)}, f32[1,6,2,1,128]{4,3,2,1,0:T(1,128)S(1)}, u32[]{:S(2)}, u32[]{:S(2)}) %collective-permute-start.10) | collective-permute-done | bytes 6176 | tf_op jit(solution)/shard_map/ppermute | solution.py:325
  64.6 0.0 collective-permute-done.11.refs_4_
  64.7 1.3 %shard_map.103 = (f32[4,16,128]{2,1,0:T(8,128)}, f32[4,16,128]{2,1,0:T(8,128)}) custom-call(f32[2,16,128]{2,1,0:T(8,128)S(1)} %get-tuple-element.26.refs_0_, f32[6,2,16,128]{3,2,1,0:T(8,128)S(1)} %get-tuple-element.42.refs_1_, f32[5,12,2,16,128]{4,3,2,1,0:T(8,128)S(1)} %get-tuple-element.28.fixed_ref.refs_2_, ...), custom_call_target="tpu_custom_call" | custom-call | flops 20000 | bytes 20000 | tf_op jit(solution)/shard_map/pallas_call | solution.py:39
Async XLA Ops:
  1.6 9.1 %copy-start.1 = (f32[4,64]{1,0:T(4,128)S(1)}, f32[4,64]{1,0:T(4,128)}, u32[]{:S(2)}) copy-start(f32[4,64]{1,0:T(4,128)} %residual_ref.1) | copy-start | bytes 3076
  1.6 27.4 %collective-permute-start = (f32[6,4,16,128]{3,2,1,0:T(8,128)S(1)}, f32[6,4,16,128]{3,2,1,0:T(8,128)S(1)}, u32[]{:S(2)}, u32[]{:S(2)}) collective-permute-start(f32[6,4,16,128]{3,2,1,0:T(8,128)S(1)} %pad_maximum_fusion.own_ref), channel_id=1, source_target_pairs={{0,1},{1,2},{2,3},{4,5},{5,6},{6,7},{8,9},{9,10},{10,11},{12,13},{... | collective-permute-start | bytes 589832 | tf_op jit(solution)/shard_map/ppermute | solution.py:325
  5.1 23.9 %collective-permute-start.1 = (f32[6,4,16,128]{3,2,1,0:T(8,128)S(1)}, f32[6,4,16,128]{3,2,1,0:T(8,128)S(1)}, u32[]{:S(2)}, u32[]{:S(2)}) collective-permute-start(f32[6,4,16,128]{3,2,1,0:T(8,128)S(1)} %pad_maximum_fusion.own_ref), channel_id=1, source_target_pairs={{1,0},{2,1},{3,2},{5,4},{6,5},{7,6},{9,8},{10,9},{11,10},{13,12},{... | collective-permute-start | bytes 589832 | tf_op jit(solution)/shard_map/ppermute | solution.py:325
  10.6 0.7 copy-start.2
  10.6 0.7 %copy-start.3 = (s32[64]{0:T(128)S(1)}, s32[64]{0:T(128)}, u32[]{:S(2)}) copy-start(s32[64]{0:T(128)} %param.14) | copy-start | bytes 772
  12.4 31.5 %all-to-all-start = ((f32[128,1,128]{2,1,0:T(1,128)}), f32[128,1,128]{2,1,0:T(1,128)S(1)}, u32[]{:S(2)}, u32[]{:S(2)}) async-start(f32[128,1,128]{2,1,0:T(1,128)} %bitcast.7), calls=%async_computation | async-start | bytes 131072 | tf_op jit(solution)/shard_map/all_to_all | solution.py:337
  29.3 10.8 %copy-start = (s32[32,4]{0,1:T(4,128)S(1)}, s32[32,4]{0,1:T(4,128)}, u32[]{:S(2)}) copy-start(s32[32,4]{0,1:T(4,128)} %param.15) | copy-start | bytes 1540
  29.3 6.7 %collective-permute-start.2 = (f32[18,16,128]{2,1,0:T(8,128)S(1)}, f32[18,16,128]{2,1,0:T(8,128)S(1)}, u32[]{:S(2)}, u32[]{:S(2)}) collective-permute-start(f32[18,16,128]{2,1,0:T(8,128)S(1)} %get-tuple-element.24), channel_id=1, source_target_pairs={{0,4},{4,8},{8,12},{1,5},{5,9},{9,13},{2,6},{6,10},{10,14},{3,7},{... | collective-permute-start | bytes 442376 | tf_op jit(solution)/shard_map/ppermute | solution.py:325
  32.4 7.7 %collective-permute-start.3 = (f32[18,16,128]{2,1,0:T(8,128)S(1)}, f32[18,16,128]{2,1,0:T(8,128)S(1)}, u32[]{:S(2)}, u32[]{:S(2)}) collective-permute-start(f32[18,16,128]{2,1,0:T(8,128)S(1)} %get-tuple-element.25), channel_id=1, source_target_pairs={{4,0},{8,4},{12,8},{5,1},{9,5},{13,9},{6,2},{10,6},{14,10},{7,3},{... | collective-permute-start | bytes 442376 | tf_op jit(solution)/shard_map/ppermute | solution.py:325
  44.7 4.5 %collective-permute-start.4 = (f32[2,12,2,1,128]{4,3,2,1,0:T(1,128)S(1)}, f32[2,12,2,1,128]{4,3,2,1,0:T(1,128)S(1)}, u32[]{:S(2)}, u32[]{:S(2)}) collective-permute-start(f32[2,12,2,1,128]{4,3,2,1,0:T(1,128)S(1)} %get-tuple-element.31.refs_6_), channel_id=1, source_target_pairs={{0,16},{16,32},{32,48},{48,64},{64,80},{80,96},{96,112},{112,128},... | collective-permute-start | bytes 73736 | tf_op jit(solution)/shard_map/ppermute | solution.py:325
  45.2 4.0 %collective-permute-start.5 = (f32[2,12,2,1,128]{4,3,2,1,0:T(1,128)S(1)}, f32[2,12,2,1,128]{4,3,2,1,0:T(1,128)S(1)}, u32[]{:S(2)}, u32[]{:S(2)}) collective-permute-start(f32[2,12,2,1,128]{4,3,2,1,0:T(1,128)S(1)} %get-tuple-element.32.refs_5_), channel_id=1, source_target_pairs={{0,496},{16,0},{32,16},{48,32},{64,48},{80,64},{96,80},{112,96},{1... | collective-permute-start | bytes 73736 | tf_op jit(solution)/shard_map/ppermute | solution.py:325
  50.1 4.3 %collective-permute-start.6 = (f32[1,10,2,1,128]{4,3,2,1,0:T(1,128)S(1)}, f32[1,10,2,1,128]{4,3,2,1,0:T(1,128)S(1)}, u32[]{:S(2)}, u32[]{:S(2)}) collective-permute-start(f32[1,10,2,1,128]{4,3,2,1,0:T(1,128)S(1)} %get-tuple-element.34), channel_id=1, source_target_pairs={{0,16},{16,32},{32,48},{48,64},{64,80},{80,96},{96,112},{112,128},... | collective-permute-start | bytes 30728 | tf_op jit(solution)/shard_map/ppermute | solution.py:325
  50.2 4.3 %collective-permute-start.7 = (f32[1,10,2,1,128]{4,3,2,1,0:T(1,128)S(1)}, f32[1,10,2,1,128]{4,3,2,1,0:T(1,128)S(1)}, u32[]{:S(2)}, u32[]{:S(2)}) collective-permute-start(f32[1,10,2,1,128]{4,3,2,1,0:T(1,128)S(1)} %get-tuple-element.35), channel_id=1, source_target_pairs={{0,496},{16,0},{32,16},{48,32},{64,48},{80,64},{96,80},{112,96},{1... | collective-permute-start | bytes 30728 | tf_op jit(solution)/shard_map/ppermute | solution.py:325
  55.3 4.3 %collective-permute-start.8 = (f32[1,8,2,1,128]{4,3,2,1,0:T(1,128)S(1)}, f32[1,8,2,1,128]{4,3,2,1,0:T(1,128)S(1)}, u32[]{:S(2)}, u32[]{:S(2)}) collective-permute-start(f32[1,8,2,1,128]{4,3,2,1,0:T(1,128)S(1)} %get-tuple-element.39), channel_id=1, source_target_pairs={{0,16},{16,32},{32,48},{48,64},{64,80},{80,96},{96,112},{112,128},... | collective-permute-start | bytes 24584 | tf_op jit(solution)/shard_map/ppermute | solution.py:325
  55.3 4.3 %collective-permute-start.9 = (f32[1,8,2,1,128]{4,3,2,1,0:T(1,128)S(1)}, f32[1,8,2,1,128]{4,3,2,1,0:T(1,128)S(1)}, u32[]{:S(2)}, u32[]{:S(2)}) collective-permute-start(f32[1,8,2,1,128]{4,3,2,1,0:T(1,128)S(1)} %get-tuple-element.40), channel_id=1, source_target_pairs={{0,496},{16,0},{32,16},{48,32},{64,48},{80,64},{96,80},{112,96},{1... | collective-permute-start | bytes 24584 | tf_op jit(solution)/shard_map/ppermute | solution.py:325
  60.4 4.3 %collective-permute-start.10 = (f32[1,6,2,1,128]{4,3,2,1,0:T(1,128)S(1)}, f32[1,6,2,1,128]{4,3,2,1,0:T(1,128)S(1)}, u32[]{:S(2)}, u32[]{:S(2)}) collective-permute-start(f32[1,6,2,1,128]{4,3,2,1,0:T(1,128)S(1)} %get-tuple-element.43), channel_id=1, source_target_pairs={{0,16},{16,32},{32,48},{48,64},{64,80},{80,96},{96,112},{112,128},... | collective-permute-start | bytes 18440 | tf_op jit(solution)/shard_map/ppermute | solution.py:325
  60.4 4.3 %collective-permute-start.11 = (f32[1,6,2,1,128]{4,3,2,1,0:T(1,128)S(1)}, f32[1,6,2,1,128]{4,3,2,1,0:T(1,128)S(1)}, u32[]{:S(2)}, u32[]{:S(2)}) collective-permute-start(f32[1,6,2,1,128]{4,3,2,1,0:T(1,128)S(1)} %get-tuple-element.44), channel_id=1, source_target_pairs={{0,496},{16,0},{32,16},{48,32},{64,48},{80,64},{96,80},{112,96},{1... | collective-permute-start | bytes 18440 | tf_op jit(solution)/shard_map/ppermute | solution.py:325
where the time goes:
time: 66.2 us; the launch traced here: 65.9 us
  starting transfers between devices  41.8 us (63%)
  waiting for transfers between devices  13.9 us (21%)
  Pallas kernels  7.79 us (12%)
  other arithmetic  0.95 us (1%)
  between operations  0.81 us (1%)
    ppermute x12, starting transfers between devices, shift(): return lax.ppermute(cells, axis, pairs)  25.2 us
    all_to_all x1, starting transfers between devices, body(): sensors = lax.all_to_all(message, ('gx', 'gy'), 0, 0, tiled=True)  16.6 us
    ppermute x12, waiting for transfers between devices, shift(): return lax.ppermute(cells, axis, pairs)  10.6 us
    pallas_call x9, Pallas kernels, run(): pl.pallas_call(kernel, out_shape=[jax.ShapeDtypeStruct(o, F32) for o in o...  7.79 us
    all_to_all x1, waiting for transfers between devices, body(): sensors = lax.all_to_all(message, ('gx', 'gy'), 0, 0, tiled=True)  3.33 us
  transfers between devices with their start and end apart: 13, of which 6 were waited for; matrix products, arithmetic and copies ran while one was open for 0% of the time, Pallas kernels for 5%

commit v1 on v0

--- a/solution.py
+++ b/solution.py
@@ -11,8 +11,8 @@
 F32 = jnp.float32
 BF16 = jnp.bfloat16
 LANES = 128
-WIDE = 32
-QUART = LANES // WIDE
+WIDE = 24
+PIECES = LANES // WIDE
 MAXSUB = 6
 SLOTS = 4
 FIELDS = 6
@@ -78,6 +78,10 @@
     out_ref[...] = total
 
 
+def needed(layers):
+    return [(f, l) for f in range(FIELDS) for l in range(layers) if f in (0, 3, 4) or 0 < l < layers - 1]
+
+
 def stacked(refs, field, layer):
     each = refs[0].shape[1]
     return refs[layer // each][field, layer % each]
@@ -87,17 +91,16 @@
     refs = (below_ref, own_ref, above_ref)
     layers = 3 * own_ref.shape[1]
     rows = own_ref.shape[2]
-    quarter = iota((rows, LANES), 1) // WIDE
-    for j in range(FIELDS * layers // QUART):
+    piece = iota((rows, LANES), 1) // WIDE
+    planes = needed(layers)
+    for j in range(left_ref.shape[0]):
         left = right = None
-        for q in range(QUART):
-            p = j * QUART + q
-            plane = stacked(refs, p // layers, p % layers)
+        for q, (f, l) in enumerate(planes[j * PIECES : (j + 1) * PIECES]):
+            plane = stacked(refs, f, l)
             to_left = plane if q == 0 else pltpu.roll(plane, WIDE * q, 1)
-            shift = (WIDE * q + WIDE) % LANES
-            to_right = plane if shift == 0 else pltpu.roll(plane, shift, 1)
-            left = to_left if q == 0 else jnp.where(quarter == q, to_left, left)
-            right = to_right if q == 0 else jnp.where(quarter == q, to_right, right)
+            to_right = pltpu.roll(plane, WIDE * q + WIDE, 1)
+            left = to_left if q == 0 else jnp.where(piece == q, to_left, left)
+            right = to_right if q == 0 else jnp.where(piece == q, to_right, right)
         left_ref[j] = left
         right_ref[j] = right
 
@@ -168,14 +171,18 @@
     rows = own_ref.shape[2]
     lane = iota((rows, LANES), 1)
 
+    listed = {plane: at for at, plane in enumerate(needed(layers))}
+
     def field(f):
         planes = []
         for l in range(layers):
-            p = f * layers + l
-            j, q = p // QUART, p % QUART
-            from_left = pltpu.roll(left_ref[j], (LANES - WIDE - WIDE * q) % LANES, 1) if q != QUART - 1 else left_ref[j]
-            from_right = pltpu.roll(right_ref[j], LANES - WIDE * q, 1) if q != 0 else right_ref[j]
-            side = jnp.where(lane < WIDE, from_right, jnp.where(lane >= LANES - WIDE, from_left, 0.0))
+            if (f, l) in listed:
+                j, q = divmod(listed[f, l], PIECES)
+                from_left = pltpu.roll(left_ref[j], (LANES - WIDE - WIDE * q) % LANES, 1)
+                from_right = pltpu.roll(right_ref[j], LANES - WIDE * q, 1) if q != 0 else right_ref[j]
+                side = jnp.where(lane < WIDE, from_right, jnp.where(lane >= LANES - WIDE, from_left, 0.0))
+            else:
+                side = jnp.zeros((rows, LANES), F32)
             planes.append(jnp.stack([stacked(refs, f, l), side], axis=0))
         return jnp.stack(planes, axis=0)
 
@@ -338,7 +345,7 @@
     fields = jnp.concatenate([adjoint_final[None], conductivity, step_ratio[None], refine_rate[None]], axis=0)
     below = shift(fields, "gz", 1, False)
     above = shift(fields, "gz", -1, False)
-    packed = (FIELDS * layers // QUART, rows, LANES)
+    packed = (pl.cdiv(len(needed(layers)), PIECES), rows, LANES)
     to_left, to_right = call(pack_columns, [packed, packed])(below, fields, above)
     from_left = shift(to_right, "gy", 1, False)
     from_right = shift(to_left, "gy", -1, False)

time: 66.2 us -> 66.2 us (level)
  the two profiles are of different devices: /device:TPU:8 before, /device:TPU:16 now
where the time goes in v1:
time: 66.2 us; the launch traced here: 65.9 us
  starting transfers between devices  41.8 us (63%)
  waiting for transfers between devices  13.9 us (21%)
  Pallas kernels  7.82 us (12%)
  other arithmetic  0.95 us (1%)
  between operations  0.81 us (1%)
    ppermute x12, starting transfers between devices, shift(): return lax.ppermute(cells, axis, pairs)  22.1 us
    all_to_all x1, starting transfers between devices, body(): sensors = lax.all_to_all(message, ('gx', 'gy'), 0, 0, tiled=True)  19.8 us
    ppermute x12, waiting for transfers between devices, shift(): return lax.ppermute(cells, axis, pairs)  9.8 us
    pallas_call x9, Pallas kernels, run(): pl.pallas_call(kernel, out_shape=[jax.ShapeDtypeStruct(o, F32) for o in o...  7.82 us
    all_to_all x1, waiting for transfers between devices, body(): sensors = lax.all_to_all(message, ('gx', 'gy'), 0, 0, tiled=True)  4.06 us
  transfers between devices with their start and end apart: 13, of which 6 were waited for; matrix products, arithmetic and copies ran while one was open for 0% of the time, Pallas kernels for 5%

profile of v1, /device:TPU:16, one launch (start us, length us, event | category | flops | bytes accessed | tf_op | source)
XLA Modules:
  0.0 65.9 jit_solution(8697461345812638454)
XLA Ops:
  0.6 0.9 %pad_maximum_fusion.own_ref = f32[6,4,16,128]{3,2,1,0:T(8,128)S(1)} fusion(f32[1,4,16,128]{3,2,1,0:T(8,128)} %bitcast.15, f32[1,4,16,128]{3,2,1,0:T(8,128)} %bitcast.16, f32[3,4,16,128]{3,2,1,0:T(8,128)} %param.9, f32[1,4,16,128]{3,2,1,0:T(8,128)} %bitcast.17), kind=kLoop, calls=%fused_computation | loop fusion | flops 147456 | bytes 393216 | tf_op jit(solution)/shard_map/concatenate | solution.py:345
  1.6 0.0 copy-start.1
  1.6 2.4 %collective-permute-start.1 = (f32[6,4,16,128]{3,2,1,0:T(8,128)S(1)}, f32[6,4,16,128]{3,2,1,0:T(8,128)S(1)}, u32[]{:S(2)}, u32[]{:S(2)}) collective-permute-start(f32[6,4,16,128]{3,2,1,0:T(8,128)S(1)} %pad_maximum_fusion.own_ref), channel_id=1, source_target_pairs={{1,0},{2,1},{3,2},{5,4},{6,5},{7,6},{9,8},{10,9},{11,10},{13,12},{... | collective-permute-start | bytes 589832 | tf_op jit(solution)/shard_map/ppermute | solution.py:332
  4.0 3.5 %collective-permute-start = (f32[6,4,16,128]{3,2,1,0:T(8,128)S(1)}, f32[6,4,16,128]{3,2,1,0:T(8,128)S(1)}, u32[]{:S(2)}, u32[]{:S(2)}) collective-permute-start(f32[6,4,16,128]{3,2,1,0:T(8,128)S(1)} %pad_maximum_fusion.own_ref), channel_id=1, source_target_pairs={{0,1},{1,2},{2,3},{4,5},{5,6},{6,7},{8,9},{9,10},{10,11},{12,13},{... | collective-permute-start | bytes 589832 | tf_op jit(solution)/shard_map/ppermute | solution.py:332
  7.5 0.0 copy-start.2
  7.5 0.0 copy-start.3
  7.5 0.0 copy-done.1
  7.5 0.6 copy-done.2
  8.1 0.0 copy-done.3
  8.1 1.1 %shard_map.97 = f32[128,128]{1,0:T(8,128)} custom-call(f32[4,64]{1,0:T(4,128)S(1)} %copy-done.1, s32[1,64]{1,0:T(1,128)S(1)} %bitcast.13, s32[1,64]{1,0:T(1,128)S(1)} %bitcast.14), custom_call_target="tpu_custom_call" | custom-call | flops 20000 | bytes 20000 | tf_op jit(solution)/shard_map/pallas_call | solution.py:39
  9.2 19.8 %all-to-all-start = ((f32[128,1,128]{2,1,0:T(1,128)}), f32[128,1,128]{2,1,0:T(1,128)S(1)}, u32[]{:S(2)}, u32[]{:S(2)}) async-start(f32[128,1,128]{2,1,0:T(1,128)} %bitcast.7), calls=%async_computation | async-start | bytes 131072 | tf_op jit(solution)/shard_map/all_to_all | solution.py:344
  29.0 0.0 collective-permute-done.1.above_ref
  29.0 0.0 collective-permute-done.below_ref
  29.0 0.3 shard_map.95
  29.3 0.0 copy-start
  29.4 3.0 %collective-permute-start.2 = (f32[14,16,128]{2,1,0:T(8,128)S(1)}, f32[14,16,128]{2,1,0:T(8,128)S(1)}, u32[]{:S(2)}, u32[]{:S(2)}) collective-permute-start(f32[14,16,128]{2,1,0:T(8,128)S(1)} %get-tuple-element.24), channel_id=1, source_target_pairs={{0,4},{4,8},{8,12},{1,5},{5,9},{9,13},{2,6},{6,10},{10,14},{3,7},{... | collective-permute-start | bytes 344072 | tf_op jit(solution)/shard_map/ppermute | solution.py:332
  32.4 1.3 %collective-permute-start.3 = (f32[14,16,128]{2,1,0:T(8,128)S(1)}, f32[14,16,128]{2,1,0:T(8,128)S(1)}, u32[]{:S(2)}, u32[]{:S(2)}) collective-permute-start(f32[14,16,128]{2,1,0:T(8,128)S(1)} %get-tuple-element.25), channel_id=1, source_target_pairs={{4,0},{8,4},{12,8},{5,1},{9,5},{13,9},{6,2},{10,6},{14,10},{7,3},{... | collective-permute-start | bytes 344072 | tf_op jit(solution)/shard_map/ppermute | solution.py:332
  33.7 1.6 %collective-permute-done.2.left_ref = f32[14,16,128]{2,1,0:T(8,128)S(1)} collective-permute-done((f32[14,16,128]{2,1,0:T(8,128)S(1)}, f32[14,16,128]{2,1,0:T(8,128)S(1)}, u32[]{:S(2)}, u32[]{:S(2)}) %collective-permute-start.2) | collective-permute-done | bytes 114720 | tf_op jit(solution)/shard_map/ppermute | solution.py:332
  35.3 4.1 %collective-permute-done.3.right_ref = f32[14,16,128]{2,1,0:T(8,128)S(1)} collective-permute-done((f32[14,16,128]{2,1,0:T(8,128)S(1)}, f32[14,16,128]{2,1,0:T(8,128)S(1)}, u32[]{:S(2)}, u32[]{:S(2)}) %collective-permute-start.3) | collective-permute-done | bytes 114720 | tf_op jit(solution)/shard_map/ppermute | solution.py:332
  39.4 0.0 copy-done
  39.4 0.4 shard_map.96
  39.8 4.1 %all-to-all-done = f32[128,1,128]{2,1,0:T(1,128)S(1)} async-done(((f32[128,1,128]{2,1,0:T(1,128)}), f32[128,1,128]{2,1,0:T(1,128)S(1)}, u32[]{:S(2)}, u32[]{:S(2)}) %all-to-all-start) | async-done | bytes 65568 | tf_op jit(solution)/shard_map/all_to_all | solution.py:344
  43.9 0.9 %shard_map.98 = (f32[12,2,16,128]{3,2,1,0:T(8,128)S(1)}, f32[2,12,2,1,128]{4,3,2,1,0:T(1,128)S(1)}, f32[2,12,2,1,128]{4,3,2,1,0:T(1,128)S(1)}) custom-call(f32[12,2,16,128]{3,2,1,0:T(8,128)S(1)} %get-tuple-element.27.state_in, f32[5,12,2,16,128]{4,3,2,1,0:T(8,128)S(1)} %get-tuple-element.28.fixed_ref.refs_2_, ...), custom_call_target="tpu_custom_call" | custom-call | flops 20000 | bytes 20000 | tf_op jit(solution)/shard_map/pallas_call | solution.py:39
  44.7 0.5 collective-permute-start.4
  45.2 2.5 %collective-permute-start.5 = (f32[2,12,2,1,128]{4,3,2,1,0:T(1,128)S(1)}, f32[2,12,2,1,128]{4,3,2,1,0:T(1,128)S(1)}, u32[]{:S(2)}, u32[]{:S(2)}) collective-permute-start(f32[2,12,2,1,128]{4,3,2,1,0:T(1,128)S(1)} %get-tuple-element.32.refs_5_), channel_id=1, source_target_pairs={{0,496},{16,0},{32,16},{48,32},{64,48},{80,64},{96,80},{112,96},{1... | collective-permute-start | bytes 73736 | tf_op jit(solution)/shard_map/ppermute | solution.py:332
  47.7 1.5 %shard_map.99.refs_7_ = f32[3,12,2,16,128]{4,3,2,1,0:T(8,128)S(1)} custom-call(f32[128,128]{1,0:T(8,128)S(1)} %bitcast.11), custom_call_target="tpu_custom_call" | custom-call | flops 20000 | bytes 20000 | tf_op jit(solution)/shard_map/pallas_call | solution.py:39
  49.2 0.0 collective-permute-done.4.refs_3_
  49.2 0.0 collective-permute-done.5.refs_4_
  49.2 0.9 %shard_map.100 = (f32[10,2,16,128]{3,2,1,0:T(8,128)S(1)}, f32[1,10,2,1,128]{4,3,2,1,0:T(1,128)S(1)}, f32[1,10,2,1,128]{4,3,2,1,0:T(1,128)S(1)}, f32[4,16,128]{2,1,0:T(8,128)S(1)}, f32[2,12,2,1,128]{4,3,2,1,0:T(1,128)S(1)}) custom-call(f32[2,16,128]{2,1,0:T(8,128)S(1)} %get-tuple-element.26.refs_0_, f32[12,2,16,128]{3,2,1,0:T(8,128)S(1)} %get-tuple-element.30.refs_1_, ...), custom_call_target="tpu_custom_call" | custom-call | flops 20000 | bytes 20000 | tf_op jit(solution)/shard_map/pallas_call | solution.py:39
  50.1 0.0 collective-permute-start.6
  50.2 3.0 %collective-permute-start.7 = (f32[1,10,2,1,128]{4,3,2,1,0:T(1,128)S(1)}, f32[1,10,2,1,128]{4,3,2,1,0:T(1,128)S(1)}, u32[]{:S(2)}, u32[]{:S(2)}) collective-permute-start(f32[1,10,2,1,128]{4,3,2,1,0:T(1,128)S(1)} %get-tuple-element.35), channel_id=1, source_target_pairs={{0,496},{16,0},{32,16},{48,32},{64,48},{80,64},{96,80},{112,96},{1... | collective-permute-start | bytes 30728 | tf_op jit(solution)/shard_map/ppermute | solution.py:332
  53.1 1.3 %collective-permute-done.6.refs_3_ = f32[1,10,2,1,128]{4,3,2,1,0:T(1,128)S(1)} collective-permute-done((f32[1,10,2,1,128]{4,3,2,1,0:T(1,128)S(1)}, f32[1,10,2,1,128]{4,3,2,1,0:T(1,128)S(1)}, u32[]{:S(2)}, u32[]{:S(2)}) %collective-permute-start.6) | collective-permute-done | bytes 10272 | tf_op jit(solution)/shard_map/ppermute | solution.py:332
  54.5 0.0 collective-permute-done.7.refs_4_
  54.5 0.8 %shard_map.101 = (f32[8,2,16,128]{3,2,1,0:T(8,128)S(1)}, f32[1,8,2,1,128]{4,3,2,1,0:T(1,128)S(1)}, f32[1,8,2,1,128]{4,3,2,1,0:T(1,128)S(1)}, f32[4,16,128]{2,1,0:T(8,128)S(1)}) custom-call(f32[2,16,128]{2,1,0:T(8,128)S(1)} %get-tuple-element.26.refs_0_, f32[10,2,16,128]{3,2,1,0:T(8,128)S(1)} %get-tuple-element.33.refs_1_, ...), custom_call_target="tpu_custom_call" | custom-call | flops 20000 | bytes 20000 | tf_op jit(solution)/shard_map/pallas_call | solution.py:39
  55.3 0.0 collective-permute-start.8
  55.3 2.9 %collective-permute-start.9 = (f32[1,8,2,1,128]{4,3,2,1,0:T(1,128)S(1)}, f32[1,8,2,1,128]{4,3,2,1,0:T(1,128)S(1)}, u32[]{:S(2)}, u32[]{:S(2)}) collective-permute-start(f32[1,8,2,1,128]{4,3,2,1,0:T(1,128)S(1)} %get-tuple-element.40), channel_id=1, source_target_pairs={{0,496},{16,0},{32,16},{48,32},{64,48},{80,64},{96,80},{112,96},{1... | collective-permute-start | bytes 24584 | tf_op jit(solution)/shard_map/ppermute | solution.py:332
  58.3 1.3 %collective-permute-done.8.refs_3_ = f32[1,8,2,1,128]{4,3,2,1,0:T(1,128)S(1)} collective-permute-done((f32[1,8,2,1,128]{4,3,2,1,0:T(1,128)S(1)}, f32[1,8,2,1,128]{4,3,2,1,0:T(1,128)S(1)}, u32[]{:S(2)}, u32[]{:S(2)}) %collective-permute-start.8) | collective-permute-done | bytes 8224 | tf_op jit(solution)/shard_map/ppermute | solution.py:332
  59.6 0.0 collective-permute-done.9.refs_4_
  59.6 0.7 %shard_map.102 = (f32[6,2,16,128]{3,2,1,0:T(8,128)S(1)}, f32[1,6,2,1,128]{4,3,2,1,0:T(1,128)S(1)}, f32[1,6,2,1,128]{4,3,2,1,0:T(1,128)S(1)}, f32[4,16,128]{2,1,0:T(8,128)S(1)}) custom-call(f32[2,16,128]{2,1,0:T(8,128)S(1)} %get-tuple-element.26.refs_0_, f32[8,2,16,128]{3,2,1,0:T(8,128)S(1)} %get-tuple-element.38.refs_1_, ...), custom_call_target="tpu_custom_call" | custom-call | flops 20000 | bytes 20000 | tf_op jit(solution)/shard_map/pallas_call | solution.py:39
  60.4 0.0 collective-permute-start.10
  60.4 2.9 %collective-permute-start.11 = (f32[1,6,2,1,128]{4,3,2,1,0:T(1,128)S(1)}, f32[1,6,2,1,128]{4,3,2,1,0:T(1,128)S(1)}, u32[]{:S(2)}, u32[]{:S(2)}) collective-permute-start(f32[1,6,2,1,128]{4,3,2,1,0:T(1,128)S(1)} %get-tuple-element.44), channel_id=1, source_target_pairs={{0,496},{16,0},{32,16},{48,32},{64,48},{80,64},{96,80},{112,96},{1... | collective-permute-start | bytes 18440 | tf_op jit(solution)/shard_map/ppermute | solution.py:332
  63.3 1.3 %collective-permute-done.10.refs_3_ = f32[1,6,2,1,128]{4,3,2,1,0:T(1,128)S(1)} collective-permute-done((f32[1,6,2,1,128]{4,3,2,1,0:T(1,128)S(1)}, f32[1,6,2,1,128]{4,3,2,1,0:T(1,128)S(1)}, u32[]{:S(2)}, u32[]{:S(2)}) %collective-permute-start.10) | collective-permute-done | bytes 6176 | tf_op jit(solution)/shard_map/ppermute | solution.py:332
  64.6 0.0 collective-permute-done.11.refs_4_
  64.7 1.3 %shard_map.103 = (f32[4,16,128]{2,1,0:T(8,128)}, f32[4,16,128]{2,1,0:T(8,128)}) custom-call(f32[2,16,128]{2,1,0:T(8,128)S(1)} %get-tuple-element.26.refs_0_, f32[6,2,16,128]{3,2,1,0:T(8,128)S(1)} %get-tuple-element.42.refs_1_, f32[5,12,2,16,128]{4,3,2,1,0:T(8,128)S(1)} %get-tuple-element.28.fixed_ref.refs_2_, ...), custom_call_target="tpu_custom_call" | custom-call | flops 20000 | bytes 20000 | tf_op jit(solution)/shard_map/pallas_call | solution.py:39
Async XLA Ops:
  1.6 5.9 %copy-start.1 = (f32[4,64]{1,0:T(4,128)S(1)}, f32[4,64]{1,0:T(4,128)}, u32[]{:S(2)}) copy-start(f32[4,64]{1,0:T(4,128)} %residual_ref.1) | copy-start | bytes 3076
  1.6 27.4 %collective-permute-start.1 = (f32[6,4,16,128]{3,2,1,0:T(8,128)S(1)}, f32[6,4,16,128]{3,2,1,0:T(8,128)S(1)}, u32[]{:S(2)}, u32[]{:S(2)}) collective-permute-start(f32[6,4,16,128]{3,2,1,0:T(8,128)S(1)} %pad_maximum_fusion.own_ref), channel_id=1, source_target_pairs={{1,0},{2,1},{3,2},{5,4},{6,5},{7,6},{9,8},{10,9},{11,10},{13,12},{... | collective-permute-start | bytes 589832 | tf_op jit(solution)/shard_map/ppermute | solution.py:332
  4.0 25.1 %collective-permute-start = (f32[6,4,16,128]{3,2,1,0:T(8,128)S(1)}, f32[6,4,16,128]{3,2,1,0:T(8,128)S(1)}, u32[]{:S(2)}, u32[]{:S(2)}) collective-permute-start(f32[6,4,16,128]{3,2,1,0:T(8,128)S(1)} %pad_maximum_fusion.own_ref), channel_id=1, source_target_pairs={{0,1},{1,2},{2,3},{4,5},{5,6},{6,7},{8,9},{9,10},{10,11},{12,13},{... | collective-permute-start | bytes 589832 | tf_op jit(solution)/shard_map/ppermute | solution.py:332
  7.5 0.7 copy-start.2
  7.5 0.7 %copy-start.3 = (s32[64]{0:T(128)S(1)}, s32[64]{0:T(128)}, u32[]{:S(2)}) copy-start(s32[64]{0:T(128)} %param.14) | copy-start | bytes 772
  9.2 34.7 %all-to-all-start = ((f32[128,1,128]{2,1,0:T(1,128)}), f32[128,1,128]{2,1,0:T(1,128)S(1)}, u32[]{:S(2)}, u32[]{:S(2)}) async-start(f32[128,1,128]{2,1,0:T(1,128)} %bitcast.7), calls=%async_computation | async-start | bytes 131072 | tf_op jit(solution)/shard_map/all_to_all | solution.py:344
  29.3 10.0 %copy-start = (s32[32,4]{0,1:T(4,128)S(1)}, s32[32,4]{0,1:T(4,128)}, u32[]{:S(2)}) copy-start(s32[32,4]{0,1:T(4,128)} %param.15) | copy-start | bytes 1540
  29.4 5.9 %collective-permute-start.2 = (f32[14,16,128]{2,1,0:T(8,128)S(1)}, f32[14,16,128]{2,1,0:T(8,128)S(1)}, u32[]{:S(2)}, u32[]{:S(2)}) collective-permute-start(f32[14,16,128]{2,1,0:T(8,128)S(1)} %get-tuple-element.24), channel_id=1, source_target_pairs={{0,4},{4,8},{8,12},{1,5},{5,9},{9,13},{2,6},{6,10},{10,14},{3,7},{... | collective-permute-start | bytes 344072 | tf_op jit(solution)/shard_map/ppermute | solution.py:332
  32.4 7.0 %collective-permute-start.3 = (f32[14,16,128]{2,1,0:T(8,128)S(1)}, f32[14,16,128]{2,1,0:T(8,128)S(1)}, u32[]{:S(2)}, u32[]{:S(2)}) collective-permute-start(f32[14,16,128]{2,1,0:T(8,128)S(1)} %get-tuple-element.25), channel_id=1, source_target_pairs={{4,0},{8,4},{12,8},{5,1},{9,5},{13,9},{6,2},{10,6},{14,10},{7,3},{... | collective-permute-start | bytes 344072 | tf_op jit(solution)/shard_map/ppermute | solution.py:332
  44.7 4.5 %collective-permute-start.4 = (f32[2,12,2,1,128]{4,3,2,1,0:T(1,128)S(1)}, f32[2,12,2,1,128]{4,3,2,1,0:T(1,128)S(1)}, u32[]{:S(2)}, u32[]{:S(2)}) collective-permute-start(f32[2,12,2,1,128]{4,3,2,1,0:T(1,128)S(1)} %get-tuple-element.31.refs_6_), channel_id=1, source_target_pairs={{0,16},{16,32},{32,48},{48,64},{64,80},{80,96},{96,112},{112,128},... | collective-permute-start | bytes 73736 | tf_op jit(solution)/shard_map/ppermute | solution.py:332
  45.2 4.0 %collective-permute-start.5 = (f32[2,12,2,1,128]{4,3,2,1,0:T(1,128)S(1)}, f32[2,12,2,1,128]{4,3,2,1,0:T(1,128)S(1)}, u32[]{:S(2)}, u32[]{:S(2)}) collective-permute-start(f32[2,12,2,1,128]{4,3,2,1,0:T(1,128)S(1)} %get-tuple-element.32.refs_5_), channel_id=1, source_target_pairs={{0,496},{16,0},{32,16},{48,32},{64,48},{80,64},{96,80},{112,96},{1... | collective-permute-start | bytes 73736 | tf_op jit(solution)/shard_map/ppermute | solution.py:332
  50.1 4.3 %collective-permute-start.6 = (f32[1,10,2,1,128]{4,3,2,1,0:T(1,128)S(1)}, f32[1,10,2,1,128]{4,3,2,1,0:T(1,128)S(1)}, u32[]{:S(2)}, u32[]{:S(2)}) collective-permute-start(f32[1,10,2,1,128]{4,3,2,1,0:T(1,128)S(1)} %get-tuple-element.34), channel_id=1, source_target_pairs={{0,16},{16,32},{32,48},{48,64},{64,80},{80,96},{96,112},{112,128},... | collective-permute-start | bytes 30728 | tf_op jit(solution)/shard_map/ppermute | solution.py:332
  50.2 4.3 %collective-permute-start.7 = (f32[1,10,2,1,128]{4,3,2,1,0:T(1,128)S(1)}, f32[1,10,2,1,128]{4,3,2,1,0:T(1,128)S(1)}, u32[]{:S(2)}, u32[]{:S(2)}) collective-permute-start(f32[1,10,2,1,128]{4,3,2,1,0:T(1,128)S(1)} %get-tuple-element.35), channel_id=1, source_target_pairs={{0,496},{16,0},{32,16},{48,32},{64,48},{80,64},{96,80},{112,96},{1... | collective-permute-start | bytes 30728 | tf_op jit(solution)/shard_map/ppermute | solution.py:332
  55.3 4.3 %collective-permute-start.8 = (f32[1,8,2,1,128]{4,3,2,1,0:T(1,128)S(1)}, f32[1,8,2,1,128]{4,3,2,1,0:T(1,128)S(1)}, u32[]{:S(2)}, u32[]{:S(2)}) collective-permute-start(f32[1,8,2,1,128]{4,3,2,1,0:T(1,128)S(1)} %get-tuple-element.39), channel_id=1, source_target_pairs={{0,16},{16,32},{32,48},{48,64},{64,80},{80,96},{96,112},{112,128},... | collective-permute-start | bytes 24584 | tf_op jit(solution)/shard_map/ppermute | solution.py:332
  55.3 4.3 %collective-permute-start.9 = (f32[1,8,2,1,128]{4,3,2,1,0:T(1,128)S(1)}, f32[1,8,2,1,128]{4,3,2,1,0:T(1,128)S(1)}, u32[]{:S(2)}, u32[]{:S(2)}) collective-permute-start(f32[1,8,2,1,128]{4,3,2,1,0:T(1,128)S(1)} %get-tuple-element.40), channel_id=1, source_target_pairs={{0,496},{16,0},{32,16},{48,32},{64,48},{80,64},{96,80},{112,96},{1... | collective-permute-start | bytes 24584 | tf_op jit(solution)/shard_map/ppermute | solution.py:332
  60.4 4.3 %collective-permute-start.10 = (f32[1,6,2,1,128]{4,3,2,1,0:T(1,128)S(1)}, f32[1,6,2,1,128]{4,3,2,1,0:T(1,128)S(1)}, u32[]{:S(2)}, u32[]{:S(2)}) collective-permute-start(f32[1,6,2,1,128]{4,3,2,1,0:T(1,128)S(1)} %get-tuple-element.43), channel_id=1, source_target_pairs={{0,16},{16,32},{32,48},{48,64},{64,80},{80,96},{96,112},{112,128},... | collective-permute-start | bytes 18440 | tf_op jit(solution)/shard_map/ppermute | solution.py:332
  60.4 4.3 %collective-permute-start.11 = (f32[1,6,2,1,128]{4,3,2,1,0:T(1,128)S(1)}, f32[1,6,2,1,128]{4,3,2,1,0:T(1,128)S(1)}, u32[]{:S(2)}, u32[]{:S(2)}) collective-permute-start(f32[1,6,2,1,128]{4,3,2,1,0:T(1,128)S(1)} %get-tuple-element.44), channel_id=1, source_target_pairs={{0,496},{16,0},{32,16},{48,32},{64,48},{80,64},{96,80},{112,96},{1... | collective-permute-start | bytes 18440 | tf_op jit(solution)/shard_map/ppermute | solution.py:332

commit v2 on v1

--- a/solution.py
+++ b/solution.py
@@ -18,6 +18,7 @@
 FIELDS = 6
 TINY = 1e-30
 LIMIT = 24 * 2**20
+WHOLE = 66_800_000
 
 
 def iota(shape, dim):
@@ -32,7 +33,7 @@
     return jnp.concatenate([field[:, 1:2], field[:, 0:1]], axis=1)
 
 
-def call(kernel, outs, cost=20000):
+def call(kernel, outs, cost=20000, grant=LIMIT):
     vmem = pl.BlockSpec(memory_space=pltpu.VMEM)
 
     def run(*args):
@@ -41,14 +42,18 @@
             out_shape=[jax.ShapeDtypeStruct(o, F32) for o in outs],
             in_specs=[vmem] * len(args),
             out_specs=[vmem] * len(outs),
-            compiler_params=pltpu.CompilerParams(vmem_limit_bytes=LIMIT),
+            compiler_params=pltpu.CompilerParams(vmem_limit_bytes=grant),
             cost_estimate=pl.CostEstimate(flops=cost, bytes_accessed=cost, transcendentals=0),
         )(*args)
 
     return run
 
 
-def pack(gy, residual_ref, tile_ref, cell_ref, out_ref):
+def pack(gy, residual_ref, tile_ref, cell_ref, adjoint_ref, conductivity_ref, ratio_ref, rate_ref, fields_ref, out_ref):
+    fields_ref[0] = adjoint_ref[...]
+    fields_ref[1:4] = conductivity_ref[...]
+    fields_ref[4] = ratio_ref[...]
+    fields_ref[5] = rate_ref[...]
     count = residual_ref.shape[1]
     tiles = out_ref.shape[0]
     eye = iota((count, count), 0) == iota((count, count), 1)
@@ -338,13 +343,18 @@
     n_y = lax.axis_size("gy")
     tiles = lax.axis_size("gx") * n_y
     listed = sensor_tile.shape[0]
-    (message,) = call(functools.partial(pack, n_y), [(tiles, LANES)])(
-        residual, sensor_tile.reshape(1, listed), sensor_cell.reshape(1, listed)
+    fields, message = call(functools.partial(pack, n_y), [(FIELDS, own, rows, cols), (tiles, LANES)], grant=WHOLE)(
+        residual,
+        sensor_tile.reshape(1, listed),
+        sensor_cell.reshape(1, listed),
+        adjoint_final,
+        conductivity,
+        step_ratio,
+        refine_rate,
     )
-    sensors = lax.all_to_all(message, ("gx", "gy"), 0, 0, tiled=True)
-    fields = jnp.concatenate([adjoint_final[None], conductivity, step_ratio[None], refine_rate[None]], axis=0)
     below = shift(fields, "gz", 1, False)
     above = shift(fields, "gz", -1, False)
+    sensors = lax.all_to_all(message, ("gx", "gy"), 0, 0, tiled=True)
     packed = (pl.cdiv(len(needed(layers)), PIECES), rows, LANES)
     to_left, to_right = call(pack_columns, [packed, packed])(below, fields, above)
     from_left = shift(to_right, "gy", 1, False)

time: 66.2 us -> 65.6 us (level)
  Pallas kernels: 7.82 us -> 8.82 us
  waiting for transfers between devices: 13.9 us -> 12.9 us
  other arithmetic: 0.95 us -> 0 us
    pallas_call x9, Pallas kernels: 7.82 us -> 8.82 us  [run(): pl.pallas_call(kernel, out_shape=[jax.ShapeDtypeStruct(o, F32) for o in o...]
    concatenate x1 -> x0, other arithmetic: 0.95 us -> none  [body(): jnp.concatenate([adjoint_final[None], conductivity, step_ratio[None], ref...]
    all_to_all x1, waiting for transfers between devices: 4.06 us -> 3.11 us  [body(): sensors = lax.all_to_all(message, ('gx', 'gy'), 0, 0, tiled=True)]
  transfers between devices with their start and end apart: 13 -> 13, of which waited for: 6 -> 6; matrix products, arithmetic and copies ran while one was open for 0% -> 0% of each run, Pallas kernels for 5% -> 3%
where the time goes in v2:
time: 65.6 us; the launch traced here: 65.3 us
  starting transfers between devices  41.8 us (64%)
  waiting for transfers between devices  12.9 us (20%)
  Pallas kernels  8.82 us (13%)
  local copies, waits for them, and re-layouts  0.93 us (1%)
  between operations  0.79 us (1%)
    ppermute x12, starting transfers between devices, shift(): return lax.ppermute(cells, axis, pairs)  22 us
    all_to_all x1, starting transfers between devices, body(): sensors = lax.all_to_all(message, ('gx', 'gy'), 0, 0, tiled=True)  19.8 us
    ppermute x12, waiting for transfers between devices, shift(): return lax.ppermute(cells, axis, pairs)  9.83 us
    pallas_call x9, Pallas kernels, run(): pl.pallas_call(kernel, out_shape=[jax.ShapeDtypeStruct(o, F32) for o in o...  8.82 us
    all_to_all x1, waiting for transfers between devices, body(): sensors = lax.all_to_all(message, ('gx', 'gy'), 0, 0, tiled=True)  3.11 us
  transfers between devices with their start and end apart: 13, of which 6 were waited for; matrix products, arithmetic and copies ran while one was open for 0% of the time, Pallas kernels for 3%

profile of v2, /device:TPU:16, one launch (start us, length us, event | category | flops | bytes accessed | tf_op | source)
XLA Modules:
  0.0 65.3 jit_solution(10108191630825940638)
XLA Ops:
  0.6 2.1 %shard_map.95 = (f32[6,4,16,128]{3,2,1,0:T(8,128)}, f32[128,128]{1,0:T(8,128)}) custom-call(f32[4,64]{1,0:T(4,128)} %residual_ref.1, s32[1,64]{1,0:T(1,128)} %bitcast.11, s32[1,64]{1,0:T(1,128)} %bitcast.12, f32[4,16,128]{2,1,0:T(8,128)} %adjoint_ref.1, f32[3,4,16,128]{3,2,1,0:T(8,128)} %conductivity_ref.1, f32[4,16,128]{2,1,0:T(8,128)} %ratio_ref.1, ...), custom_call_target="tpu_custom_call" | custom-call | flops 20000 | bytes 20000 | tf_op jit(solution)/shard_map/pallas_call | solution.py:40
  2.7 2.3 %collective-permute-start.1 = (f32[6,4,16,128]{3,2,1,0:T(8,128)}, f32[6,4,16,128]{3,2,1,0:T(8,128)S(1)}, u32[]{:S(2)}, u32[]{:S(2)}) collective-permute-start(f32[6,4,16,128]{3,2,1,0:T(8,128)} %get-tuple-element.26.own_ref), channel_id=1, source_target_pairs={{1,0},{2,1},{3,2},{5,4},{6,5},{7,6},{9,8},{10,9},{11,10},{13,12},{... | collective-permute-start | bytes 589832 | tf_op jit(solution)/shard_map/ppermute | solution.py:337
  5.1 3.5 %collective-permute-start = (f32[6,4,16,128]{3,2,1,0:T(8,128)}, f32[6,4,16,128]{3,2,1,0:T(8,128)S(1)}, u32[]{:S(2)}, u32[]{:S(2)}) collective-permute-start(f32[6,4,16,128]{3,2,1,0:T(8,128)} %get-tuple-element.26.own_ref), channel_id=1, source_target_pairs={{0,1},{1,2},{2,3},{4,5},{5,6},{6,7},{8,9},{9,10},{10,11},{12,13},{... | collective-permute-start | bytes 589832 | tf_op jit(solution)/shard_map/ppermute | solution.py:337
  8.6 19.8 %all-to-all-start = ((f32[128,1,128]{2,1,0:T(1,128)}), f32[128,1,128]{2,1,0:T(1,128)S(1)}, u32[]{:S(2)}, u32[]{:S(2)}) async-start(f32[128,1,128]{2,1,0:T(1,128)} %bitcast.10), calls=%async_computation | async-start | bytes 131072 | tf_op jit(solution)/shard_map/all_to_all | solution.py:357
  28.4 0.0 collective-permute-done.1.above_ref
  28.4 0.0 collective-permute-done.below_ref
  28.4 0.0 copy-start
  28.4 0.9 %copy-done = f32[6,4,16,128]{3,2,1,0:T(8,128)S(1)} copy-done((f32[6,4,16,128]{3,2,1,0:T(8,128)S(1)}, f32[6,4,16,128]{3,2,1,0:T(8,128)}, u32[]{:S(2)}) %copy-start) | copy-done | bytes 196632
  29.3 0.3 shard_map.96
  29.6 0.0 copy-start.1
  29.6 3.0 %collective-permute-start.2 = (f32[14,16,128]{2,1,0:T(8,128)S(1)}, f32[14,16,128]{2,1,0:T(8,128)S(1)}, u32[]{:S(2)}, u32[]{:S(2)}) collective-permute-start(f32[14,16,128]{2,1,0:T(8,128)S(1)} %get-tuple-element.27), channel_id=1, source_target_pairs={{0,4},{4,8},{8,12},{1,5},{5,9},{9,13},{2,6},{6,10},{10,14},{3,7},{... | collective-permute-start | bytes 344072 | tf_op jit(solution)/shard_map/ppermute | solution.py:337
  32.7 1.3 %collective-permute-start.3 = (f32[14,16,128]{2,1,0:T(8,128)S(1)}, f32[14,16,128]{2,1,0:T(8,128)S(1)}, u32[]{:S(2)}, u32[]{:S(2)}) collective-permute-start(f32[14,16,128]{2,1,0:T(8,128)S(1)} %get-tuple-element.28), channel_id=1, source_target_pairs={{4,0},{8,4},{12,8},{5,1},{9,5},{13,9},{6,2},{10,6},{14,10},{7,3},{... | collective-permute-start | bytes 344072 | tf_op jit(solution)/shard_map/ppermute | solution.py:337
  34.0 1.6 %collective-permute-done.2.left_ref = f32[14,16,128]{2,1,0:T(8,128)S(1)} collective-permute-done((f32[14,16,128]{2,1,0:T(8,128)S(1)}, f32[14,16,128]{2,1,0:T(8,128)S(1)}, u32[]{:S(2)}, u32[]{:S(2)}) %collective-permute-start.2) | collective-permute-done | bytes 114720 | tf_op jit(solution)/shard_map/ppermute | solution.py:337
  35.6 4.1 %collective-permute-done.3.right_ref = f32[14,16,128]{2,1,0:T(8,128)S(1)} collective-permute-done((f32[14,16,128]{2,1,0:T(8,128)S(1)}, f32[14,16,128]{2,1,0:T(8,128)S(1)}, u32[]{:S(2)}, u32[]{:S(2)}) %collective-permute-start.3) | collective-permute-done | bytes 114720 | tf_op jit(solution)/shard_map/ppermute | solution.py:337
  39.7 0.0 copy-done.1
  39.7 0.4 shard_map.97
  40.1 3.1 %all-to-all-done = f32[128,1,128]{2,1,0:T(1,128)S(1)} async-done(((f32[128,1,128]{2,1,0:T(1,128)}), f32[128,1,128]{2,1,0:T(1,128)S(1)}, u32[]{:S(2)}, u32[]{:S(2)}) %all-to-all-start) | async-done | bytes 65568 | tf_op jit(solution)/shard_map/all_to_all | solution.py:357
  43.2 0.9 %shard_map.98 = (f32[12,2,16,128]{3,2,1,0:T(8,128)S(1)}, f32[2,12,2,1,128]{4,3,2,1,0:T(1,128)S(1)}, f32[2,12,2,1,128]{4,3,2,1,0:T(1,128)S(1)}) custom-call(f32[12,2,16,128]{3,2,1,0:T(8,128)S(1)} %get-tuple-element.30.state_in, f32[5,12,2,16,128]{4,3,2,1,0:T(8,128)S(1)} %get-tuple-element.31.fixed_ref.refs_2_, ...), custom_call_target="tpu_custom_call" | custom-call | flops 20000 | bytes 20000 | tf_op jit(solution)/shard_map/pallas_call | solution.py:40
  44.1 0.5 collective-permute-start.4
  44.6 2.5 %collective-permute-start.5 = (f32[2,12,2,1,128]{4,3,2,1,0:T(1,128)S(1)}, f32[2,12,2,1,128]{4,3,2,1,0:T(1,128)S(1)}, u32[]{:S(2)}, u32[]{:S(2)}) collective-permute-start(f32[2,12,2,1,128]{4,3,2,1,0:T(1,128)S(1)} %get-tuple-element.36.refs_5_), channel_id=1, source_target_pairs={{0,496},{16,0},{32,16},{48,32},{64,48},{80,64},{96,80},{112,96},{1... | collective-permute-start | bytes 73736 | tf_op jit(solution)/shard_map/ppermute | solution.py:337
  47.1 1.5 %shard_map.99.refs_7_ = f32[3,12,2,16,128]{4,3,2,1,0:T(8,128)S(1)} custom-call(f32[128,128]{1,0:T(8,128)S(1)} %bitcast.8), custom_call_target="tpu_custom_call" | custom-call | flops 20000 | bytes 20000 | tf_op jit(solution)/shard_map/pallas_call | solution.py:40
  48.6 0.0 collective-permute-done.4.refs_3_
  48.6 0.0 collective-permute-done.5.refs_4_
  48.6 0.9 %shard_map.100 = (f32[10,2,16,128]{3,2,1,0:T(8,128)S(1)}, f32[1,10,2,1,128]{4,3,2,1,0:T(1,128)S(1)}, f32[1,10,2,1,128]{4,3,2,1,0:T(1,128)S(1)}, f32[4,16,128]{2,1,0:T(8,128)S(1)}, f32[2,12,2,1,128]{4,3,2,1,0:T(1,128)S(1)}) custom-call(f32[2,16,128]{2,1,0:T(8,128)S(1)} %get-tuple-element.29.refs_0_, f32[12,2,16,128]{3,2,1,0:T(8,128)S(1)} %get-tuple-element.34.refs_1_, ...), custom_call_target="tpu_custom_call" | custom-call | flops 20000 | bytes 20000 | tf_op jit(solution)/shard_map/pallas_call | solution.py:40
  49.5 0.0 collective-permute-start.6
  49.5 3.0 %collective-permute-start.7 = (f32[1,10,2,1,128]{4,3,2,1,0:T(1,128)S(1)}, f32[1,10,2,1,128]{4,3,2,1,0:T(1,128)S(1)}, u32[]{:S(2)}, u32[]{:S(2)}) collective-permute-start(f32[1,10,2,1,128]{4,3,2,1,0:T(1,128)S(1)} %get-tuple-element.39), channel_id=1, source_target_pairs={{0,496},{16,0},{32,16},{48,32},{64,48},{80,64},{96,80},{112,96},{1... | collective-permute-start | bytes 30728 | tf_op jit(solution)/shard_map/ppermute | solution.py:337
  52.5 1.3 %collective-permute-done.6.refs_3_ = f32[1,10,2,1,128]{4,3,2,1,0:T(1,128)S(1)} collective-permute-done((f32[1,10,2,1,128]{4,3,2,1,0:T(1,128)S(1)}, f32[1,10,2,1,128]{4,3,2,1,0:T(1,128)S(1)}, u32[]{:S(2)}, u32[]{:S(2)}) %collective-permute-start.6) | collective-permute-done | bytes 10272 | tf_op jit(solution)/shard_map/ppermute | solution.py:337
  53.8 0.0 collective-permute-done.7.refs_4_
  53.9 0.8 %shard_map.101 = (f32[8,2,16,128]{3,2,1,0:T(8,128)S(1)}, f32[1,8,2,1,128]{4,3,2,1,0:T(1,128)S(1)}, f32[1,8,2,1,128]{4,3,2,1,0:T(1,128)S(1)}, f32[4,16,128]{2,1,0:T(8,128)S(1)}) custom-call(f32[2,16,128]{2,1,0:T(8,128)S(1)} %get-tuple-element.29.refs_0_, f32[10,2,16,128]{3,2,1,0:T(8,128)S(1)} %get-tuple-element.37.refs_1_, ...), custom_call_target="tpu_custom_call" | custom-call | flops 20000 | bytes 20000 | tf_op jit(solution)/shard_map/pallas_call | solution.py:40
  54.7 0.0 collective-permute-start.8
  54.7 2.9 %collective-permute-start.9 = (f32[1,8,2,1,128]{4,3,2,1,0:T(1,128)S(1)}, f32[1,8,2,1,128]{4,3,2,1,0:T(1,128)S(1)}, u32[]{:S(2)}, u32[]{:S(2)}) collective-permute-start(f32[1,8,2,1,128]{4,3,2,1,0:T(1,128)S(1)} %get-tuple-element.44), channel_id=1, source_target_pairs={{0,496},{16,0},{32,16},{48,32},{64,48},{80,64},{96,80},{112,96},{1... | collective-permute-start | bytes 24584 | tf_op jit(solution)/shard_map/ppermute | solution.py:337
  57.6 1.3 %collective-permute-done.8.refs_3_ = f32[1,8,2,1,128]{4,3,2,1,0:T(1,128)S(1)} collective-permute-done((f32[1,8,2,1,128]{4,3,2,1,0:T(1,128)S(1)}, f32[1,8,2,1,128]{4,3,2,1,0:T(1,128)S(1)}, u32[]{:S(2)}, u32[]{:S(2)}) %collective-permute-start.8) | collective-permute-done | bytes 8224 | tf_op jit(solution)/shard_map/ppermute | solution.py:337
  59.0 0.0 collective-permute-done.9.refs_4_
  59.0 0.7 %shard_map.102 = (f32[6,2,16,128]{3,2,1,0:T(8,128)S(1)}, f32[1,6,2,1,128]{4,3,2,1,0:T(1,128)S(1)}, f32[1,6,2,1,128]{4,3,2,1,0:T(1,128)S(1)}, f32[4,16,128]{2,1,0:T(8,128)S(1)}) custom-call(f32[2,16,128]{2,1,0:T(8,128)S(1)} %get-tuple-element.29.refs_0_, f32[8,2,16,128]{3,2,1,0:T(8,128)S(1)} %get-tuple-element.42.refs_1_, ...), custom_call_target="tpu_custom_call" | custom-call | flops 20000 | bytes 20000 | tf_op jit(solution)/shard_map/pallas_call | solution.py:40
  59.7 0.0 collective-permute-start.10
  59.7 2.9 %collective-permute-start.11 = (f32[1,6,2,1,128]{4,3,2,1,0:T(1,128)S(1)}, f32[1,6,2,1,128]{4,3,2,1,0:T(1,128)S(1)}, u32[]{:S(2)}, u32[]{:S(2)}) collective-permute-start(f32[1,6,2,1,128]{4,3,2,1,0:T(1,128)S(1)} %get-tuple-element.48), channel_id=1, source_target_pairs={{0,496},{16,0},{32,16},{48,32},{64,48},{80,64},{96,80},{112,96},{1... | collective-permute-start | bytes 18440 | tf_op jit(solution)/shard_map/ppermute | solution.py:337
  62.7 1.3 %collective-permute-done.10.refs_3_ = f32[1,6,2,1,128]{4,3,2,1,0:T(1,128)S(1)} collective-permute-done((f32[1,6,2,1,128]{4,3,2,1,0:T(1,128)S(1)}, f32[1,6,2,1,128]{4,3,2,1,0:T(1,128)S(1)}, u32[]{:S(2)}, u32[]{:S(2)}) %collective-permute-start.10) | collective-permute-done | bytes 6176 | tf_op jit(solution)/shard_map/ppermute | solution.py:337
  64.0 0.0 collective-permute-done.11.refs_4_
  64.0 1.3 %shard_map.103 = (f32[4,16,128]{2,1,0:T(8,128)}, f32[4,16,128]{2,1,0:T(8,128)}) custom-call(f32[2,16,128]{2,1,0:T(8,128)S(1)} %get-tuple-element.29.refs_0_, f32[6,2,16,128]{3,2,1,0:T(8,128)S(1)} %get-tuple-element.46.refs_1_, f32[5,12,2,16,128]{4,3,2,1,0:T(8,128)S(1)} %get-tuple-element.31.fixed_ref.refs_2_, ...), custom_call_target="tpu_custom_call" | custom-call | flops 20000 | bytes 20000 | tf_op jit(solution)/shard_map/pallas_call | solution.py:40
Async XLA Ops:
  2.7 25.7 %collective-permute-start.1 = (f32[6,4,16,128]{3,2,1,0:T(8,128)}, f32[6,4,16,128]{3,2,1,0:T(8,128)S(1)}, u32[]{:S(2)}, u32[]{:S(2)}) collective-permute-start(f32[6,4,16,128]{3,2,1,0:T(8,128)} %get-tuple-element.26.own_ref), channel_id=1, source_target_pairs={{1,0},{2,1},{3,2},{5,4},{6,5},{7,6},{9,8},{10,9},{11,10},{13,12},{... | collective-permute-start | bytes 589832 | tf_op jit(solution)/shard_map/ppermute | solution.py:337
  5.1 23.3 %collective-permute-start = (f32[6,4,16,128]{3,2,1,0:T(8,128)}, f32[6,4,16,128]{3,2,1,0:T(8,128)S(1)}, u32[]{:S(2)}, u32[]{:S(2)}) collective-permute-start(f32[6,4,16,128]{3,2,1,0:T(8,128)} %get-tuple-element.26.own_ref), channel_id=1, source_target_pairs={{0,1},{1,2},{2,3},{4,5},{5,6},{6,7},{8,9},{9,10},{10,11},{12,13},{... | collective-permute-start | bytes 589832 | tf_op jit(solution)/shard_map/ppermute | solution.py:337
  8.6 34.7 %all-to-all-start = ((f32[128,1,128]{2,1,0:T(1,128)}), f32[128,1,128]{2,1,0:T(1,128)S(1)}, u32[]{:S(2)}, u32[]{:S(2)}) async-start(f32[128,1,128]{2,1,0:T(1,128)} %bitcast.10), calls=%async_computation | async-start | bytes 131072 | tf_op jit(solution)/shard_map/all_to_all | solution.py:357
  28.4 0.9 %copy-start = (f32[6,4,16,128]{3,2,1,0:T(8,128)S(1)}, f32[6,4,16,128]{3,2,1,0:T(8,128)}, u32[]{:S(2)}) copy-start(f32[6,4,16,128]{3,2,1,0:T(8,128)} %get-tuple-element.26.own_ref) | copy-start | bytes 589828
  29.6 10.1 %copy-start.1 = (s32[32,4]{0,1:T(4,128)S(1)}, s32[32,4]{0,1:T(4,128)}, u32[]{:S(2)}) copy-start(s32[32,4]{0,1:T(4,128)} %param.15) | copy-start | bytes 1540
  29.6 5.9 %collective-permute-start.2 = (f32[14,16,128]{2,1,0:T(8,128)S(1)}, f32[14,16,128]{2,1,0:T(8,128)S(1)}, u32[]{:S(2)}, u32[]{:S(2)}) collective-permute-start(f32[14,16,128]{2,1,0:T(8,128)S(1)} %get-tuple-element.27), channel_id=1, source_target_pairs={{0,4},{4,8},{8,12},{1,5},{5,9},{9,13},{2,6},{6,10},{10,14},{3,7},{... | collective-permute-start | bytes 344072 | tf_op jit(solution)/shard_map/ppermute | solution.py:337
  32.7 7.0 %collective-permute-start.3 = (f32[14,16,128]{2,1,0:T(8,128)S(1)}, f32[14,16,128]{2,1,0:T(8,128)S(1)}, u32[]{:S(2)}, u32[]{:S(2)}) collective-permute-start(f32[14,16,128]{2,1,0:T(8,128)S(1)} %get-tuple-element.28), channel_id=1, source_target_pairs={{4,0},{8,4},{12,8},{5,1},{9,5},{13,9},{6,2},{10,6},{14,10},{7,3},{... | collective-permute-start | bytes 344072 | tf_op jit(solution)/shard_map/ppermute | solution.py:337
  44.1 4.5 %collective-permute-start.4 = (f32[2,12,2,1,128]{4,3,2,1,0:T(1,128)S(1)}, f32[2,12,2,1,128]{4,3,2,1,0:T(1,128)S(1)}, u32[]{:S(2)}, u32[]{:S(2)}) collective-permute-start(f32[2,12,2,1,128]{4,3,2,1,0:T(1,128)S(1)} %get-tuple-element.35.refs_6_), channel_id=1, source_target_pairs={{0,16},{16,32},{32,48},{48,64},{64,80},{80,96},{96,112},{112,128},... | collective-permute-start | bytes 73736 | tf_op jit(solution)/shard_map/ppermute | solution.py:337
  44.6 4.0 %collective-permute-start.5 = (f32[2,12,2,1,128]{4,3,2,1,0:T(1,128)S(1)}, f32[2,12,2,1,128]{4,3,2,1,0:T(1,128)S(1)}, u32[]{:S(2)}, u32[]{:S(2)}) collective-permute-start(f32[2,12,2,1,128]{4,3,2,1,0:T(1,128)S(1)} %get-tuple-element.36.refs_5_), channel_id=1, source_target_pairs={{0,496},{16,0},{32,16},{48,32},{64,48},{80,64},{96,80},{112,96},{1... | collective-permute-start | bytes 73736 | tf_op jit(solution)/shard_map/ppermute | solution.py:337
  49.5 4.3 %collective-permute-start.6 = (f32[1,10,2,1,128]{4,3,2,1,0:T(1,128)S(1)}, f32[1,10,2,1,128]{4,3,2,1,0:T(1,128)S(1)}, u32[]{:S(2)}, u32[]{:S(2)}) collective-permute-start(f32[1,10,2,1,128]{4,3,2,1,0:T(1,128)S(1)} %get-tuple-element.38), channel_id=1, source_target_pairs={{0,16},{16,32},{32,48},{48,64},{64,80},{80,96},{96,112},{112,128},... | collective-permute-start | bytes 30728 | tf_op jit(solution)/shard_map/ppermute | solution.py:337
  49.5 4.3 %collective-permute-start.7 = (f32[1,10,2,1,128]{4,3,2,1,0:T(1,128)S(1)}, f32[1,10,2,1,128]{4,3,2,1,0:T(1,128)S(1)}, u32[]{:S(2)}, u32[]{:S(2)}) collective-permute-start(f32[1,10,2,1,128]{4,3,2,1,0:T(1,128)S(1)} %get-tuple-element.39), channel_id=1, source_target_pairs={{0,496},{16,0},{32,16},{48,32},{64,48},{80,64},{96,80},{112,96},{1... | collective-permute-start | bytes 30728 | tf_op jit(solution)/shard_map/ppermute | solution.py:337
  54.7 4.3 %collective-permute-start.8 = (f32[1,8,2,1,128]{4,3,2,1,0:T(1,128)S(1)}, f32[1,8,2,1,128]{4,3,2,1,0:T(1,128)S(1)}, u32[]{:S(2)}, u32[]{:S(2)}) collective-permute-start(f32[1,8,2,1,128]{4,3,2,1,0:T(1,128)S(1)} %get-tuple-element.43), channel_id=1, source_target_pairs={{0,16},{16,32},{32,48},{48,64},{64,80},{80,96},{96,112},{112,128},... | collective-permute-start | bytes 24584 | tf_op jit(solution)/shard_map/ppermute | solution.py:337
  54.7 4.3 %collective-permute-start.9 = (f32[1,8,2,1,128]{4,3,2,1,0:T(1,128)S(1)}, f32[1,8,2,1,128]{4,3,2,1,0:T(1,128)S(1)}, u32[]{:S(2)}, u32[]{:S(2)}) collective-permute-start(f32[1,8,2,1,128]{4,3,2,1,0:T(1,128)S(1)} %get-tuple-element.44), channel_id=1, source_target_pairs={{0,496},{16,0},{32,16},{48,32},{64,48},{80,64},{96,80},{112,96},{1... | collective-permute-start | bytes 24584 | tf_op jit(solution)/shard_map/ppermute | solution.py:337
  59.7 4.3 %collective-permute-start.10 = (f32[1,6,2,1,128]{4,3,2,1,0:T(1,128)S(1)}, f32[1,6,2,1,128]{4,3,2,1,0:T(1,128)S(1)}, u32[]{:S(2)}, u32[]{:S(2)}) collective-permute-start(f32[1,6,2,1,128]{4,3,2,1,0:T(1,128)S(1)} %get-tuple-element.47), channel_id=1, source_target_pairs={{0,16},{16,32},{32,48},{48,64},{64,80},{80,96},{96,112},{112,128},... | collective-permute-start | bytes 18440 | tf_op jit(solution)/shard_map/ppermute | solution.py:337
  59.7 4.3 %collective-permute-start.11 = (f32[1,6,2,1,128]{4,3,2,1,0:T(1,128)S(1)}, f32[1,6,2,1,128]{4,3,2,1,0:T(1,128)S(1)}, u32[]{:S(2)}, u32[]{:S(2)}) collective-permute-start(f32[1,6,2,1,128]{4,3,2,1,0:T(1,128)S(1)} %get-tuple-element.48), channel_id=1, source_target_pairs={{0,496},{16,0},{32,16},{48,32},{64,48},{80,64},{96,80},{112,96},{1... | collective-permute-start | bytes 18440 | tf_op jit(solution)/shard_map/ppermute | solution.py:337

commit v3 on v2

--- a/solution.py
+++ b/solution.py
@@ -169,7 +169,7 @@
     return out
 
 
-def prepare(axes, substeps_ref, below_ref, own_ref, above_ref, left_ref, right_ref, state_ref, fixed_ref, edge_ref, counts_ref):
+def prepare(axes, substeps_ref, below_ref, own_ref, above_ref, left_ref, right_ref, state_ref, fixed_ref, up_ref, down_ref, counts_ref):
     refs = (below_ref, own_ref, above_ref)
     own = own_ref.shape[1]
     layers = 3 * own
@@ -193,142 +193,158 @@
 
     at_x, at_y = (lax.axis_index(axis) for axis in axes)
     n_y, n_x = substeps_ref.shape
-    named = jnp.where(iota((n_y, n_x), 1) == at_x, substeps_ref[...].astype(F32), 0.0)
-
-    def count(tile):
-        rows_of = jnp.sum(jnp.where(iota((n_y, n_x), 0) == tile, named, 0.0), axis=1, keepdims=True)
-        return jnp.broadcast_to(jnp.sum(rows_of, axis=0, keepdims=True), (rows, LANES))
-
-    counts_ref[0] = count(at_y)
-    counts_ref[1] = jnp.where(lane < LANES // 2, count(at_y + 1), count(at_y - 1))
-    shape = (layers, 2, rows, LANES)
+    named = substeps_ref[...].astype(F32)
+
+    def count(x, y):
+        hit = (iota((n_y, n_x), 1) == x) & (iota((n_y, n_x), 0) == y)
+        found = jnp.sum(jnp.where(hit, named, 0.0), axis=1, keepdims=True)
+        return jnp.broadcast_to(jnp.sum(found, axis=0, keepdims=True), (rows // 2, LANES))
+
+    for part, x in enumerate((at_x - 1, at_x, at_x, at_x + 1)):
+        at_rows = slice(part * (rows // 2), (part + 1) * (rows // 2))
+        counts_ref[0, at_rows] = count(x, at_y)
+        counts_ref[1, at_rows] = jnp.where(lane[: rows // 2] < LANES // 2, count(x, at_y + 1), count(x, at_y - 1))
+    state_ref[...] = field(0)
+    half = rows // 2
+    for f in range(1, FIELDS):
+        values = field(f)
+        fixed_ref[f - 1] = values
+        up_ref[f - 1] = values[:, :, :half]
+        down_ref[f - 1] = values[:, :, half:]
+
+
+def conduct(axis, own_ref, over_ref, under_ref, fixed_ref):
+    at_x, n_x = lax.axis_index(axis), lax.axis_size(axis)
+
+    def deep(f, masked=False):
+        over, under = over_ref[f], under_ref[f]
+        if masked:
+            over = jnp.where(at_x > 0, over, 0.0)
+            under = jnp.where(at_x < n_x - 1, under, 0.0)
+        return jnp.concatenate([over, own_ref[f], under], axis=2)
+
+    along_rows = deep(0, True)
+    shape = along_rows.shape
+    layers, _, rows, _ = shape
     row = iota(shape, 2)
     col = iota(shape, 3)
-    state_ref[...] = field(0)
-    along_rows = field(1)
-    edge_ref[0] = along_rows[:, :, 0:1, :]
-    edge_ref[1] = along_rows[:, :, rows - 1 :, :]
     fixed_ref[0] = harmonic(along_rows, jnp.where(row == rows - 1, 0.0, pltpu.roll(along_rows, rows - 1, 2)))
-    along_cols = field(2)
+    along_cols = deep(1)
     rolled = pltpu.roll(along_cols, LANES - 1, 3)
     fixed_ref[1] = harmonic(along_cols, jnp.where(col == LANES - 1, swap(rolled), rolled))
-    along_layers = field(3)
+    along_layers = deep(2)
     fixed_ref[2, : layers - 1] = harmonic(along_layers[: layers - 1], along_layers[1:])
-    fixed_ref[2, layers - 1 :] = jnp.zeros((1, 2, rows, LANES), F32)
-    fixed_ref[3] = field(4)
-    fixed_ref[4] = field(5)
-
-
-def first_source(layer_axis, own, state_in, fixed_ref, edge_ref, sensors_ref, state_ref, up_ref, down_ref):
+    fixed_ref[2, layers - 1 :] = jnp.zeros((1,) + shape[1:], F32)
+    fixed_ref[3] = deep(3)
+    fixed_ref[4] = deep(4)
+
+
+def send_rows(state, source, up_ref, down_ref):
+    half = state.shape[2] // 2
+    up_ref[0] = state[:, :, :half]
+    up_ref[1] = source[:, :, :half]
+    down_ref[0] = state[:, :, half:]
+    down_ref[1] = source[:, :, half:]
+
+
+def first_sources(layer_axis, own, state_in, sensors_ref, state_ref, source_ref, up_ref, down_ref):
     layers, _, rows, _ = state_ref.shape
-    (source,) = sources(layer_axis, own, layers, rows, sensors_ref, (3,))
-    state = state_in[...] + source
+    second, first = sources(layer_axis, own, layers, rows, sensors_ref, (2, 3))
+    state = state_in[...] + first
     state_ref[...] = state
-    weighted = fixed_ref[3] * state
-    up_ref[0] = weighted[:, :, 0:1, :]
-    up_ref[1] = edge_ref[0]
-    down_ref[0] = weighted[:, :, rows - 1 :, :]
-    down_ref[1] = edge_ref[1]
+    source_ref[...] = second
+    send_rows(state, second, up_ref, down_ref)
 
 
 def other_sources(layer_axis, own, sensors_ref, source_ref):
     _, layers, _, rows, _ = source_ref.shape
-    for s, source in enumerate(sources(layer_axis, own, layers, rows, sensors_ref, (0, 1, 2))):
+    for s, source in enumerate(sources(layer_axis, own, layers, rows, sensors_ref, (0, 1))):
         source_ref[s] = source
 
 
-def step(axis, turn, *refs):
-    first, last = turn == 3, turn == 0
-    refs = list(refs)
-    counts_ref, state_ref, fixed_ref, above_ref, below_ref = refs[:5]
-    refs = refs[5:]
-    if first:
-        own_up_ref, own_down_ref = refs[:2]
+def diffuse(fixed_ref, low, state, kept):
+    layers = state.shape[0]
+    span, inner = slice(low, low + layers), slice(low + 1, low + layers - 1)
+    weighted = fixed_ref[3, span] * state
+    across = weighted[1:-1]
+    flux = fixed_ref[0, inner] * (pltpu.roll(across, across.shape[2] - 1, 2) - across)
+    change = (flux - pltpu.roll(flux, 1, 2))[:, :, kept]
+    weighted, across = weighted[:, :, kept], across[:, :, kept]
+    col = iota(across.shape, 3)
+    rolled = pltpu.roll(across, LANES - 1, 3)
+    flux = fixed_ref[1, inner, :, kept] * (jnp.where(col == LANES - 1, swap(rolled), rolled) - across)
+    rolled = pltpu.roll(flux, 1, 3)
+    change = change + (flux - jnp.where(col == 0, swap(rolled), rolled))
+    flux = fixed_ref[2, low : low + layers - 1, :, kept] * (weighted[1:] - weighted[:-1])
+    change = change + (flux[1:] - flux[:-1])
+    return state[1:-1, :, kept] + change
+
+
+def refine(state, rate, counts, tiles):
+    size = 8
+    shape = state.shape[:2] + (size, LANES)
+    row, col = iota(shape, 2), iota(shape, 3)
+    pieces = range(state.shape[2] // size)
+    at_rows = [slice(p * size, (p + 1) * size) for p in pieces]
+    rates = [rate[:, :, r] for r in at_rows]
+    keeps = [1.0 - 4.0 * r for r in rates]
+    limits = [counts[:, :, r] for r in at_rows]
+    now = [state[:, :, r] for r in at_rows]
+    for turn in range(MAXSUB):
+        scaled = [rates[p] * now[p] for p in pieces]
+        later = list(now)
+        for tile in tiles:
+            ups = {p: pltpu.roll(scaled[p], size - 1, 2) for p in tile}
+            downs = {p: pltpu.roll(scaled[p], 1, 2) for p in tile}
+            for p in tile:
+                v = scaled[p]
+                near = jnp.where(row == size - 1, ups[p + 1] if p + 1 in tile else v, ups[p])
+                near = near + jnp.where(row == 0, downs[p - 1] if p - 1 in tile else v, downs[p])
+                near = near + jnp.where(col == LANES - 1, v, pltpu.roll(v, LANES - 1, 3))
+                near = near + jnp.where(col == 0, v, pltpu.roll(v, 1, 3))
+                after = keeps[p] * now[p] + near
+                later[p] = after if turn == 0 else jnp.where(limits[p] > turn, after, now[p])
+        now = later
+    return jnp.concatenate(now, axis=2)
+
+
+def two_steps(last, counts_ref, state_ref, fixed_ref, over_ref, under_ref, between_ref, *refs):
+    if last:
+        sens_ref, state_out, sens_out = refs
     else:
-        row_edge_ref, sens_ref = refs[:2]
-    refs = refs[2:]
-    if not last:
-        source_ref = refs[0]
-        refs = refs[1:]
-    if first:
-        state_out, up_out, down_out, sens_out, edge_out = refs
-    elif not last:
-        state_out, up_out, down_out, sens_out = refs
-    else:
-        state_out, sens_out = refs
-    at_x, n_x = lax.axis_index(axis), lax.axis_size(axis)
+        rest_ref, state_out, up_out, down_out, sens_out = refs
     layers, _, rows, _ = state_ref.shape
     total = fixed_ref.shape[1]
+    own = total // 3
     low = (total - layers) // 2
-    span = slice(low, low + layers)
-    inner = slice(low + 1, low + layers - 1)
-    state = state_ref[...]
-    weighted = fixed_ref[3, span] * state
-    if first:
-        edges = []
-        for mine, other, there in ((own_up_ref, above_ref, at_x > 0), (own_down_ref, below_ref, at_x < n_x - 1)):
-            edges.append(harmonic(mine[1], jnp.where(there, other[1], 0.0)))
-        edge_out[0] = edges[0]
-        edge_out[1] = edges[1]
-        over, under = edges[0][1:-1], edges[1][1:-1]
-    else:
-        over, under = row_edge_ref[0, inner], row_edge_ref[1, inner]
-    shape = (layers - 2, 2, rows, LANES)
-    row, col = iota(shape, 2), iota(shape, 3)
-    across = weighted[1:-1]
-    halo_over = above_ref[0, 1:-1]
-    halo_under = below_ref[0, 1:-1]
-    flux = fixed_ref[0, inner] * (pltpu.roll(across, rows - 1, 2) - across)
-    edge_low = over * (across[:, :, 0:1, :] - halo_over)
-    edge_high = under * (halo_under - across[:, :, rows - 1 :, :])
-    flux = jnp.where(row == rows - 1, edge_high, flux)
-    change = flux - jnp.where(row == 0, edge_low, pltpu.roll(flux, 1, 2))
-    rolled = pltpu.roll(across, LANES - 1, 3)
-    flux = fixed_ref[1, inner] * (jnp.where(col == LANES - 1, swap(rolled), rolled) - across)
-    rolled = pltpu.roll(flux, 1, 3)
-    change = change + (flux - jnp.where(col == 0, swap(rolled), rolled))
-    flux = fixed_ref[2, low : low + layers - 1] * (weighted[1:] - weighted[:-1])
-    change = change + (flux[1:] - flux[:-1])
-    state = state[1:-1] + change
-    kept = slice(0, 1) if last else slice(0, 2)
-    state = state[:, kept]
-    rate = fixed_ref[4, inner, kept]
-    counts = counts_ref[kept][None]
-    keep_own = 1.0 - 4.0 * rate
     half = rows // 2
-    part = state.shape[:2] + (half, LANES)
-    row, col = iota(part, 2), iota(part, 3)
-
-    def one_turn(at, now):
-        top, low_half = (rate[:, :, h : h + half] * now[:, :, h : h + half] for h in (0, half))
-        up = pltpu.roll(top, half - 1, 2), pltpu.roll(low_half, half - 1, 2)
-        down = pltpu.roll(top, 1, 2), pltpu.roll(low_half, 1, 2)
-        near = (
-            jnp.where(row == half - 1, up[1], up[0]) + jnp.where(row == 0, top, down[0]),
-            jnp.where(row == half - 1, low_half, up[1]) + jnp.where(row == 0, down[0], down[1]),
-        )
-        parts = []
-        for h, (v, rowwise) in enumerate(zip((top, low_half), near)):
-            colwise = jnp.where(col == LANES - 1, v, pltpu.roll(v, LANES - 1, 3)) + jnp.where(col == 0, v, pltpu.roll(v, 1, 3))
-            here = slice(h * half, (h + 1) * half)
-            after = keep_own[:, :, here] * now[:, :, here] + (rowwise + colwise)
-            parts.append(after if at == 0 else jnp.where(counts[:, :, here] > at, after, now[:, :, here]))
-        return jnp.concatenate(parts, axis=2)
-
-    for at in range(MAXSUB):
-        state = one_turn(at, state)
-    own = total // 3
-    keep = slice((layers - 2 - own) // 2, (layers - 2 - own) // 2 + own)
-    addend = fixed_ref[3, own : 2 * own, 0] * state[keep, 0]
-    sens_out[...] = addend if first else sens_ref[...] + addend
+    mine = slice(half, half + rows)
+    everything = slice(0, 2 * rows)
+
+    def deep(field, at):
+        return jnp.concatenate([over_ref[at], field, under_ref[at]], axis=2)
+
+    def sensed(state, first_row):
+        keep = slice((state.shape[0] - own) // 2, (state.shape[0] - own) // 2 + own)
+        return fixed_ref[3, own : 2 * own, 0, mine] * state[keep, 0, first_row : first_row + rows]
+
+    state = diffuse(fixed_ref, low, deep(state_ref[...], 0), everything)
+    state = refine(state, fixed_ref[4, low + 1 : low + layers - 1], counts_ref[...][None], ((0,), (1, 2), (3,)))
+    sens = sensed(state, half)
+    if last:
+        sens = sens_ref[...] + sens
+    state = state + deep(between_ref[low : low + layers], 1)[1:-1]
+    state = diffuse(fixed_ref, low + 1, state, mine)
+    halves = slice(0, 1) if last else slice(0, 2)
+    inner = slice(low + 2, low + layers - 2)
+    state = refine(state[:, halves], fixed_ref[4, inner, halves, mine], counts_ref[halves, mine][None], ((0, 1),))
+    sens_out[...] = sens + sensed(state, 0)
     if last:
         state_out[...] = state[:, 0]
         return
-    state = state + source_ref[turn - 1, inner]
+    state = state + rest_ref[1, inner]
     state_out[...] = state
-    weighted = fixed_ref[3, inner] * state
-    up_out[0] = weighted[:, :, 0:1, :]
-    down_out[0] = weighted[:, :, rows - 1 :, :]
+    send_rows(state, rest_ref[0, inner], up_out, down_out)
 
 
 def shift(cells, axis, by, wrap):
@@ -360,35 +376,31 @@
     from_left = shift(to_right, "gy", 1, False)
     from_right = shift(to_left, "gy", -1, False)
     block = (layers, 2, rows, LANES)
-    faces = (2, layers, 2, 1, LANES)
-    state, fixed, edges, counts = call(
-        functools.partial(prepare, ("gx", "gy")), [block, (5,) + block, faces, (2, rows, LANES)]
+    halo = (layers, 2, rows // 2, LANES)
+    state, fixed, up, down, counts = call(
+        functools.partial(prepare, ("gx", "gy")), [block, (5,) + block, (5,) + halo, (5,) + halo, (2, 2 * rows, LANES)]
     )(substeps.T, below, fields, above, from_left, from_right)
-    state, up, down = call(functools.partial(first_source, "gz", own), [block, faces, faces])(state, fixed, edges, sensors)
-    (source,) = call(functools.partial(other_sources, "gz", own), [(3,) + block])(sensors)
-    sens = edge = None
-    for turn in range(3, -1, -1):
-        over = shift(down, "gx", 1, True)
-        under = shift(up, "gx", -1, True)
-        depth = state.shape[0] - 2
-        args = [counts, state, fixed]
-        args += [over, under] + ([up, down] if turn == 3 else [edge, sens])
-        if turn > 0:
-            args += [source]
-        face = (1, depth, 2, 1, LANES)
-        if turn == 0:
-            outs = [(own, rows, cols), (own, rows, cols)]
-        else:
-            outs = [(depth, 2, rows, LANES), face, face, (own, rows, cols)]
-            if turn == 3:
-                outs += [(2, layers, 2, 1, LANES)]
-        got = call(functools.partial(step, "gx", turn), outs)(*args)
-        if turn == 3:
-            state, up, down, sens, edge = got
-        elif turn > 0:
-            state, up, down, sens = got
-        else:
-            return tuple(got)
+    over = shift(down, "gx", 1, True)
+    under = shift(up, "gx", -1, True)
+    first_state, second, up, down = call(
+        functools.partial(first_sources, "gz", own), [block, block, (2,) + halo, (2,) + halo]
+    )(state, sensors)
+    (fixed,) = call(functools.partial(conduct, "gx"), [(5, layers, 2, 2 * rows, LANES)])(fixed, over, under)
+    (rest,) = call(functools.partial(other_sources, "gz", own), [(2,) + block])(sensors)
+    over = shift(down, "gx", 1, True)
+    under = shift(up, "gx", -1, True)
+    depth = layers - 4
+    halo = (2, depth, 2, rows // 2, LANES)
+    state, up, down, sens = call(
+        functools.partial(two_steps, False), [(depth, 2, rows, LANES), halo, halo, (own, rows, cols)]
+    )(counts, first_state, fixed, over, under, second, rest)
+    over = shift(down, "gx", 1, True)
+    under = shift(up, "gx", -1, True)
+    return tuple(
+        call(functools.partial(two_steps, True), [(own, rows, cols), (own, rows, cols)])(
+            counts, state, fixed, over, under, rest[0], sens
+        )
+    )
 
 
 def solution(mesh):

time: 65.6 us -> 81.9 us (1.25)
  the two profiles are of different devices: /device:TPU:16 before, /device:TPU:8 now
where the time goes in v3:
time: 81.9 us; the launch traced here: 81.5 us
  blocking collectives  31 us (38%)
  starting transfers between devices  25.5 us (31%)
  waiting for transfers between devices  13.2 us (16%)
  Pallas kernels  9.41 us (11%)
  local copies, waits for them, and re-layouts  1.62 us (2%)
    all_to_all x1, blocking collectives, body(): sensors = lax.all_to_all(message, ('gx', 'gy'), 0, 0, tiled=True)  31 us
    ppermute x10, starting transfers between devices, shift(): return lax.ppermute(cells, axis, pairs)  25.5 us
    ppermute x10, waiting for transfers between devices, shift(): return lax.ppermute(cells, axis, pairs)  13.2 us
    pallas_call x8, Pallas kernels, run(): pl.pallas_call(kernel, out_shape=[jax.ShapeDtypeStruct(o, F32) for o in o...  9.41 us
  transfers between devices with their start and end apart: 10, of which 6 were waited for; matrix products, arithmetic and copies ran while one was open for 0% of the time, Pallas kernels for 3%

profile of v3, /device:TPU:8, one launch (start us, length us, event | category | flops | bytes accessed | tf_op | source)
XLA Modules:
  0.0 81.5 jit_solution(7246612205053268667)
XLA Ops:
  0.6 2.1 %shard_map.95 = (f32[6,4,16,128]{3,2,1,0:T(8,128)}, f32[128,128]{1,0:T(8,128)}) custom-call(f32[4,64]{1,0:T(4,128)} %residual_ref.1, s32[1,64]{1,0:T(1,128)} %bitcast.13, s32[1,64]{1,0:T(1,128)} %bitcast.14, f32[4,16,128]{2,1,0:T(8,128)} %adjoint_ref.1, f32[3,4,16,128]{3,2,1,0:T(8,128)} %conductivity_ref.1, f32[4,16,128]{2,1,0:T(8,128)} %ratio_ref.1, ...), custom_call_target="tpu_custom_call" | custom-call | flops 20000 | bytes 20000 | tf_op jit(solution)/shard_map/pallas_call | solution.py:40
  2.7 3.5 %collective-permute-start = (f32[6,4,16,128]{3,2,1,0:T(8,128)}, f32[6,4,16,128]{3,2,1,0:T(8,128)S(1)}, u32[]{:S(2)}, u32[]{:S(2)}) collective-permute-start(f32[6,4,16,128]{3,2,1,0:T(8,128)} %get-tuple-element.19.own_ref), channel_id=1, source_target_pairs={{0,1},{1,2},{2,3},{4,5},{5,6},{6,7},{8,9},{9,10},{10,11},{12,13},{... | collective-permute-start | bytes 589832 | tf_op jit(solution)/shard_map/ppermute | solution.py:353
  6.2 5.5 %collective-permute-start.1 = (f32[6,4,16,128]{3,2,1,0:T(8,128)}, f32[6,4,16,128]{3,2,1,0:T(8,128)S(1)}, u32[]{:S(2)}, u32[]{:S(2)}) collective-permute-start(f32[6,4,16,128]{3,2,1,0:T(8,128)} %get-tuple-element.19.own_ref), channel_id=1, source_target_pairs={{1,0},{2,1},{3,2},{5,4},{6,5},{7,6},{9,8},{10,9},{11,10},{13,12},{... | collective-permute-start | bytes 589832 | tf_op jit(solution)/shard_map/ppermute | solution.py:353
  11.7 1.9 %collective-permute-done.below_ref = f32[6,4,16,128]{3,2,1,0:T(8,128)S(1)} collective-permute-done((f32[6,4,16,128]{3,2,1,0:T(8,128)}, f32[6,4,16,128]{3,2,1,0:T(8,128)S(1)}, u32[]{:S(2)}, u32[]{:S(2)}) %collective-permute-start) | collective-permute-done | bytes 196640 | tf_op jit(solution)/shard_map/ppermute | solution.py:353
  13.6 1.6 %collective-permute-done.1.above_ref = f32[6,4,16,128]{3,2,1,0:T(8,128)S(1)} collective-permute-done((f32[6,4,16,128]{3,2,1,0:T(8,128)}, f32[6,4,16,128]{3,2,1,0:T(8,128)S(1)}, u32[]{:S(2)}, u32[]{:S(2)}) %collective-permute-start.1) | collective-permute-done | bytes 196640 | tf_op jit(solution)/shard_map/ppermute | solution.py:353
  15.2 0.0 copy-start
  15.2 0.9 %copy-done = f32[6,4,16,128]{3,2,1,0:T(8,128)S(1)} copy-done((f32[6,4,16,128]{3,2,1,0:T(8,128)S(1)}, f32[6,4,16,128]{3,2,1,0:T(8,128)}, u32[]{:S(2)}) %copy-start) | copy-done | bytes 196632
  16.1 0.3 shard_map.96
  16.4 2.9 %collective-permute-start.2 = (f32[14,16,128]{2,1,0:T(8,128)S(1)}, f32[14,16,128]{2,1,0:T(8,128)S(1)}, u32[]{:S(2)}, u32[]{:S(2)}) collective-permute-start(f32[14,16,128]{2,1,0:T(8,128)S(1)} %get-tuple-element.20), channel_id=1, source_target_pairs={{0,4},{4,8},{8,12},{1,5},{5,9},{9,13},{2,6},{6,10},{10,14},{3,7},{... | collective-permute-start | bytes 344072 | tf_op jit(solution)/shard_map/ppermute | solution.py:353
  19.3 1.3 %collective-permute-start.3 = (f32[14,16,128]{2,1,0:T(8,128)S(1)}, f32[14,16,128]{2,1,0:T(8,128)S(1)}, u32[]{:S(2)}, u32[]{:S(2)}) collective-permute-start(f32[14,16,128]{2,1,0:T(8,128)S(1)} %get-tuple-element.21), channel_id=1, source_target_pairs={{4,0},{8,4},{12,8},{5,1},{9,5},{13,9},{6,2},{10,6},{14,10},{7,3},{... | collective-permute-start | bytes 344072 | tf_op jit(solution)/shard_map/ppermute | solution.py:353
  20.6 1.0 %collective-permute-done.2.left_ref = f32[14,16,128]{2,1,0:T(8,128)S(1)} collective-permute-done((f32[14,16,128]{2,1,0:T(8,128)S(1)}, f32[14,16,128]{2,1,0:T(8,128)S(1)}, u32[]{:S(2)}, u32[]{:S(2)}) %collective-permute-start.2) | collective-permute-done | bytes 114720 | tf_op jit(solution)/shard_map/ppermute | solution.py:353
  21.7 4.3 %collective-permute-done.3.right_ref = f32[14,16,128]{2,1,0:T(8,128)S(1)} collective-permute-done((f32[14,16,128]{2,1,0:T(8,128)S(1)}, f32[14,16,128]{2,1,0:T(8,128)S(1)}, u32[]{:S(2)}, u32[]{:S(2)}) %collective-permute-start.3) | collective-permute-done | bytes 114720 | tf_op jit(solution)/shard_map/ppermute | solution.py:353
  26.0 0.0 copy-start.1
  26.0 0.7 copy-done.1
  26.7 0.4 shard_map.97
  27.0 0.0 collective-permute-start.4
  27.1 6.4 %collective-permute-start.5 = (f32[5,12,2,8,128]{4,3,2,1,0:T(8,128)S(1)}, f32[5,12,2,8,128]{4,3,2,1,0:T(8,128)S(1)}, u32[]{:S(2)}, u32[]{:S(2)}) collective-permute-start(f32[5,12,2,8,128]{4,3,2,1,0:T(8,128)S(1)} %get-tuple-element.28), channel_id=1, source_target_pairs={{0,496},{16,0},{32,16},{48,32},{64,48},{80,64},{96,80},{112,96},{1... | collective-permute-start | bytes 1474568 | tf_op jit(solution)/shard_map/ppermute | solution.py:353
  33.4 31.0 %all_to_all.11 = f32[128,1,128]{2,1,0:T(1,128)S(1)} all-to-all(f32[128,1,128]{2,1,0:T(1,128)} %bitcast.12), channel_id=1, replica_groups=mesh['gx'=32,'gy'=4,'gz'=4] {'gx','gy'}, dimensions={0} | all-to-all | bytes 131072 | tf_op jit(solution)/shard_map/all_to_all | solution.py:373
  64.5 1.1 %shard_map.98 = (f32[12,2,16,128]{3,2,1,0:T(8,128)S(1)}, f32[12,2,16,128]{3,2,1,0:T(8,128)S(1)}, f32[2,12,2,8,128]{4,3,2,1,0:T(8,128)S(1)}, f32[2,12,2,8,128]{4,3,2,1,0:T(8,128)S(1)}) custom-call(f32[12,2,16,128]{3,2,1,0:T(8,128)S(1)} %get-tuple-element.23.state_in, f32[128,128]{1,0:T(8,128)S(1)} %bitcast.9), custom_call_target="tpu_custom_call" | custom-call | flops 20000 | bytes 20000 | tf_op jit(solution)/shard_map/pallas_call | solution.py:40
  65.6 0.4 collective-permute-start.6
  66.0 2.6 %collective-permute-start.7 = (f32[2,12,2,8,128]{4,3,2,1,0:T(8,128)S(1)}, f32[2,12,2,8,128]{4,3,2,1,0:T(8,128)S(1)}, u32[]{:S(2)}, u32[]{:S(2)}) collective-permute-start(f32[2,12,2,8,128]{4,3,2,1,0:T(8,128)S(1)} %get-tuple-element.30), channel_id=1, source_target_pairs={{0,496},{16,0},{32,16},{48,32},{64,48},{80,64},{96,80},{112,96},{1... | collective-permute-start | bytes 589832 | tf_op jit(solution)/shard_map/ppermute | solution.py:353
  68.6 1.1 %shard_map.100.refs_0_ = f32[2,12,2,16,128]{4,3,2,1,0:T(8,128)S(1)} custom-call(f32[128,128]{1,0:T(8,128)S(1)} %bitcast.10), custom_call_target="tpu_custom_call" | custom-call | flops 20000 | bytes 20000 | tf_op jit(solution)/shard_map/pallas_call | solution.py:40
  69.7 0.0 collective-permute-done.4.over_ref
  69.7 0.0 collective-permute-done.5.under_ref
  69.7 0.5 shard_map.99.fixed_ref
  70.2 1.7 %collective-permute-done.6.over_ref = f32[2,12,2,8,128]{4,3,2,1,0:T(8,128)S(1)} collective-permute-done((f32[2,12,2,8,128]{4,3,2,1,0:T(8,128)S(1)}, f32[2,12,2,8,128]{4,3,2,1,0:T(8,128)S(1)}, u32[]{:S(2)}, u32[]{:S(2)}) %collective-permute-start.6) | collective-permute-done | bytes 196640 | tf_op jit(solution)/shard_map/ppermute | solution.py:353
  71.9 0.0 collective-permute-done.7.under_ref
  71.9 2.0 %shard_map.101 = (f32[8,2,16,128]{3,2,1,0:T(8,128)S(1)}, f32[2,8,2,8,128]{4,3,2,1,0:T(8,128)S(1)}, f32[2,8,2,8,128]{4,3,2,1,0:T(8,128)S(1)}, f32[4,16,128]{2,1,0:T(8,128)S(1)}) custom-call(f32[2,32,128]{2,1,0:T(8,128)S(1)} %get-tuple-element.22.counts_ref, f32[12,2,16,128]{3,2,1,0:T(8,128)S(1)} %get-tuple-element.25.state_ref, ...), custom_call_target="tpu_custom_call" | custom-call | flops 20000 | bytes 20000 | tf_op jit(solution)/shard_map/pallas_call | solution.py:40
  73.9 0.0 collective-permute-start.8
  74.0 3.0 %collective-permute-start.9 = (f32[2,8,2,8,128]{4,3,2,1,0:T(8,128)S(1)}, f32[2,8,2,8,128]{4,3,2,1,0:T(8,128)S(1)}, u32[]{:S(2)}, u32[]{:S(2)}) collective-permute-start(f32[2,8,2,8,128]{4,3,2,1,0:T(8,128)S(1)} %get-tuple-element.34), channel_id=1, source_target_pairs={{0,496},{16,0},{32,16},{48,32},{64,48},{80,64},{96,80},{112,96},{1... | collective-permute-start | bytes 393224 | tf_op jit(solution)/shard_map/ppermute | solution.py:353
  76.9 2.6 %collective-permute-done.8.over_ref = f32[2,8,2,8,128]{4,3,2,1,0:T(8,128)S(1)} collective-permute-done((f32[2,8,2,8,128]{4,3,2,1,0:T(8,128)S(1)}, f32[2,8,2,8,128]{4,3,2,1,0:T(8,128)S(1)}, u32[]{:S(2)}, u32[]{:S(2)}) %collective-permute-start.8) | collective-permute-done | bytes 131104 | tf_op jit(solution)/shard_map/ppermute | solution.py:353
  79.6 0.0 collective-permute-done.9.under_ref
  79.6 2.0 %shard_map.102 = (f32[4,16,128]{2,1,0:T(8,128)}, f32[4,16,128]{2,1,0:T(8,128)}) custom-call(f32[2,32,128]{2,1,0:T(8,128)S(1)} %get-tuple-element.22.counts_ref, f32[8,2,16,128]{3,2,1,0:T(8,128)S(1)} %get-tuple-element.32.state_ref, f32[5,12,2,32,128]{4,3,2,1,0:T(8,128)S(1)} %shard_map.99.fixed_ref, f32[2,8,2,8,128]{4,3,2,1,0:T(8,128)S(1)} %collective-permute-done.8.over_ref, ...), custom_call_target="tpu_custom_call" | custom-call | flops 20000 | bytes 20000 | tf_op jit(solution)/shard_map/pallas_call | solution.py:40
  (1 shorter events, 0.0 us)
Async XLA Ops:
  2.7 10.9 %collective-permute-start = (f32[6,4,16,128]{3,2,1,0:T(8,128)}, f32[6,4,16,128]{3,2,1,0:T(8,128)S(1)}, u32[]{:S(2)}, u32[]{:S(2)}) collective-permute-start(f32[6,4,16,128]{3,2,1,0:T(8,128)} %get-tuple-element.19.own_ref), channel_id=1, source_target_pairs={{0,1},{1,2},{2,3},{4,5},{5,6},{6,7},{8,9},{9,10},{10,11},{12,13},{... | collective-permute-start | bytes 589832 | tf_op jit(solution)/shard_map/ppermute | solution.py:353
  6.2 9.0 %collective-permute-start.1 = (f32[6,4,16,128]{3,2,1,0:T(8,128)}, f32[6,4,16,128]{3,2,1,0:T(8,128)S(1)}, u32[]{:S(2)}, u32[]{:S(2)}) collective-permute-start(f32[6,4,16,128]{3,2,1,0:T(8,128)} %get-tuple-element.19.own_ref), channel_id=1, source_target_pairs={{1,0},{2,1},{3,2},{5,4},{6,5},{7,6},{9,8},{10,9},{11,10},{13,12},{... | collective-permute-start | bytes 589832 | tf_op jit(solution)/shard_map/ppermute | solution.py:353
  15.2 0.9 %copy-start = (f32[6,4,16,128]{3,2,1,0:T(8,128)S(1)}, f32[6,4,16,128]{3,2,1,0:T(8,128)}, u32[]{:S(2)}) copy-start(f32[6,4,16,128]{3,2,1,0:T(8,128)} %get-tuple-element.19.own_ref) | copy-start | bytes 589828
  16.4 5.2 %collective-permute-start.2 = (f32[14,16,128]{2,1,0:T(8,128)S(1)}, f32[14,16,128]{2,1,0:T(8,128)S(1)}, u32[]{:S(2)}, u32[]{:S(2)}) collective-permute-start(f32[14,16,128]{2,1,0:T(8,128)S(1)} %get-tuple-element.20), channel_id=1, source_target_pairs={{0,4},{4,8},{8,12},{1,5},{5,9},{9,13},{2,6},{6,10},{10,14},{3,7},{... | collective-permute-start | bytes 344072 | tf_op jit(solution)/shard_map/ppermute | solution.py:353
  19.3 6.7 %collective-permute-start.3 = (f32[14,16,128]{2,1,0:T(8,128)S(1)}, f32[14,16,128]{2,1,0:T(8,128)S(1)}, u32[]{:S(2)}, u32[]{:S(2)}) collective-permute-start(f32[14,16,128]{2,1,0:T(8,128)S(1)} %get-tuple-element.21), channel_id=1, source_target_pairs={{4,0},{8,4},{12,8},{5,1},{9,5},{13,9},{6,2},{10,6},{14,10},{7,3},{... | collective-permute-start | bytes 344072 | tf_op jit(solution)/shard_map/ppermute | solution.py:353
  26.0 0.7 copy-start.1
  27.0 42.6 %collective-permute-start.4 = (f32[5,12,2,8,128]{4,3,2,1,0:T(8,128)S(1)}, f32[5,12,2,8,128]{4,3,2,1,0:T(8,128)S(1)}, u32[]{:S(2)}, u32[]{:S(2)}) collective-permute-start(f32[5,12,2,8,128]{4,3,2,1,0:T(8,128)S(1)} %get-tuple-element.27), channel_id=1, source_target_pairs={{0,16},{16,32},{32,48},{48,64},{64,80},{80,96},{96,112},{112,128},... | collective-permute-start | bytes 1474568 | tf_op jit(solution)/shard_map/ppermute | solution.py:353
  27.1 42.6 %collective-permute-start.5 = (f32[5,12,2,8,128]{4,3,2,1,0:T(8,128)S(1)}, f32[5,12,2,8,128]{4,3,2,1,0:T(8,128)S(1)}, u32[]{:S(2)}, u32[]{:S(2)}) collective-permute-start(f32[5,12,2,8,128]{4,3,2,1,0:T(8,128)S(1)} %get-tuple-element.28), channel_id=1, source_target_pairs={{0,496},{16,0},{32,16},{48,32},{64,48},{80,64},{96,80},{112,96},{1... | collective-permute-start | bytes 1474568 | tf_op jit(solution)/shard_map/ppermute | solution.py:353
  65.6 6.3 %collective-permute-start.6 = (f32[2,12,2,8,128]{4,3,2,1,0:T(8,128)S(1)}, f32[2,12,2,8,128]{4,3,2,1,0:T(8,128)S(1)}, u32[]{:S(2)}, u32[]{:S(2)}) collective-permute-start(f32[2,12,2,8,128]{4,3,2,1,0:T(8,128)S(1)} %get-tuple-element.29), channel_id=1, source_target_pairs={{0,16},{16,32},{32,48},{48,64},{64,80},{80,96},{96,112},{112,128},... | collective-permute-start | bytes 589832 | tf_op jit(solution)/shard_map/ppermute | solution.py:353
  66.0 5.9 %collective-permute-start.7 = (f32[2,12,2,8,128]{4,3,2,1,0:T(8,128)S(1)}, f32[2,12,2,8,128]{4,3,2,1,0:T(8,128)S(1)}, u32[]{:S(2)}, u32[]{:S(2)}) collective-permute-start(f32[2,12,2,8,128]{4,3,2,1,0:T(8,128)S(1)} %get-tuple-element.30), channel_id=1, source_target_pairs={{0,496},{16,0},{32,16},{48,32},{64,48},{80,64},{96,80},{112,96},{1... | collective-permute-start | bytes 589832 | tf_op jit(solution)/shard_map/ppermute | solution.py:353
  73.9 5.6 %collective-permute-start.8 = (f32[2,8,2,8,128]{4,3,2,1,0:T(8,128)S(1)}, f32[2,8,2,8,128]{4,3,2,1,0:T(8,128)S(1)}, u32[]{:S(2)}, u32[]{:S(2)}) collective-permute-start(f32[2,8,2,8,128]{4,3,2,1,0:T(8,128)S(1)} %get-tuple-element.33), channel_id=1, source_target_pairs={{0,16},{16,32},{32,48},{48,64},{64,80},{80,96},{96,112},{112,128},... | collective-permute-start | bytes 393224 | tf_op jit(solution)/shard_map/ppermute | solution.py:353
  74.0 5.6 %collective-permute-start.9 = (f32[2,8,2,8,128]{4,3,2,1,0:T(8,128)S(1)}, f32[2,8,2,8,128]{4,3,2,1,0:T(8,128)S(1)}, u32[]{:S(2)}, u32[]{:S(2)}) collective-permute-start(f32[2,8,2,8,128]{4,3,2,1,0:T(8,128)S(1)} %get-tuple-element.34), channel_id=1, source_target_pairs={{0,496},{16,0},{32,16},{48,32},{64,48},{80,64},{96,80},{112,96},{1... | collective-permute-start | bytes 393224 | tf_op jit(solution)/shard_map/ppermute | solution.py:353

commit v4 on v3

--- a/solution.py
+++ b/solution.py
@@ -169,7 +169,7 @@
     return out
 
 
-def prepare(axes, substeps_ref, below_ref, own_ref, above_ref, left_ref, right_ref, state_ref, fixed_ref, up_ref, down_ref, counts_ref):
+def prepare(below_ref, own_ref, above_ref, left_ref, right_ref, state_ref, fixed_ref, up_ref, down_ref):
     refs = (below_ref, own_ref, above_ref)
     own = own_ref.shape[1]
     layers = 3 * own
@@ -191,33 +191,51 @@
             planes.append(jnp.stack([stacked(refs, f, l), side], axis=0))
         return jnp.stack(planes, axis=0)
 
-    at_x, at_y = (lax.axis_index(axis) for axis in axes)
-    n_y, n_x = substeps_ref.shape
-    named = substeps_ref[...].astype(F32)
-
-    def count(x, y):
-        hit = (iota((n_y, n_x), 1) == x) & (iota((n_y, n_x), 0) == y)
-        found = jnp.sum(jnp.where(hit, named, 0.0), axis=1, keepdims=True)
-        return jnp.broadcast_to(jnp.sum(found, axis=0, keepdims=True), (rows // 2, LANES))
-
-    for part, x in enumerate((at_x - 1, at_x, at_x, at_x + 1)):
-        at_rows = slice(part * (rows // 2), (part + 1) * (rows // 2))
-        counts_ref[0, at_rows] = count(x, at_y)
-        counts_ref[1, at_rows] = jnp.where(lane[: rows // 2] < LANES // 2, count(x, at_y + 1), count(x, at_y - 1))
     state_ref[...] = field(0)
     half = rows // 2
     for f in range(1, FIELDS):
         values = field(f)
         fixed_ref[f - 1] = values
-        up_ref[f - 1] = values[:, :, :half]
-        down_ref[f - 1] = values[:, :, half:]
-
-
-def conduct(axis, own_ref, over_ref, under_ref, fixed_ref):
-    at_x, n_x = lax.axis_index(axis), lax.axis_size(axis)
+        up_ref[f - 1] = fold(values[:, :, :half])
+        down_ref[f - 1] = fold(values[:, :, half:])
+
+
+def fold(block):
+    half = block.shape[0] // 2
+    lane = iota((half,) + block.shape[2:], 2)
+    used = (lane < WIDE) | (lane >= LANES - WIDE)
+    low, high = (jnp.where(used, part, 0.0) for part in (block[:half, 1], block[half:, 1]))
+    return jnp.concatenate([block[:, 0], low + pltpu.roll(high, LANES // 2, 2)], axis=0)
+
+
+def unfold(folded):
+    layers = folded.shape[0] * 2 // 3
+    shared = folded[layers:]
+    lane = iota(shared.shape, 2)
+    used = (lane < WIDE) | (lane >= LANES - WIDE)
+    parts = [jnp.where(used, part, 0.0) for part in (shared, pltpu.roll(shared, LANES // 2, 2))]
+    return jnp.stack([folded[:layers], jnp.concatenate(parts, axis=0)], axis=1)
+
+
+def conduct(axes, substeps_ref, own_ref, over_ref, under_ref, fixed_ref, counts_ref):
+    at_x, at_y = (lax.axis_index(axis) for axis in axes)
+    n_y, n_x = substeps_ref.shape
+    named = substeps_ref[...].astype(F32)
+    size = own_ref.shape[3] // 2
+    lane = iota((size, LANES), 1)
+
+    def count(x, y):
+        hit = (iota((n_y, n_x), 1) == x) & (iota((n_y, n_x), 0) == y)
+        found = jnp.sum(jnp.where(hit, named, 0.0), axis=1, keepdims=True)
+        return jnp.broadcast_to(jnp.sum(found, axis=0, keepdims=True), (size, LANES))
+
+    for part, x in enumerate((at_x - 1, at_x, at_x, at_x + 1)):
+        at_rows = slice(part * size, (part + 1) * size)
+        counts_ref[0, at_rows] = count(x, at_y)
+        counts_ref[1, at_rows] = jnp.where(lane < LANES // 2, count(x, at_y + 1), count(x, at_y - 1))
 
     def deep(f, masked=False):
-        over, under = over_ref[f], under_ref[f]
+        over, under = unfold(over_ref[f]), unfold(under_ref[f])
         if masked:
             over = jnp.where(at_x > 0, over, 0.0)
             under = jnp.where(at_x < n_x - 1, under, 0.0)
@@ -241,10 +259,10 @@
 
 def send_rows(state, source, up_ref, down_ref):
     half = state.shape[2] // 2
-    up_ref[0] = state[:, :, :half]
-    up_ref[1] = source[:, :, :half]
-    down_ref[0] = state[:, :, half:]
-    down_ref[1] = source[:, :, half:]
+    up_ref[0] = fold(state[:, :, :half])
+    up_ref[1] = fold(source[:, :, :half])
+    down_ref[0] = fold(state[:, :, half:])
+    down_ref[1] = fold(source[:, :, half:])
 
 
 def first_sources(layer_axis, own, state_in, sensors_ref, state_ref, source_ref, up_ref, down_ref):
@@ -322,7 +340,7 @@
     everything = slice(0, 2 * rows)
 
     def deep(field, at):
-        return jnp.concatenate([over_ref[at], field, under_ref[at]], axis=2)
+        return jnp.concatenate([unfold(over_ref[at]), field, unfold(under_ref[at])], axis=2)
 
     def sensed(state, first_row):
         keep = slice((state.shape[0] - own) // 2, (state.shape[0] - own) // 2 + own)
@@ -376,21 +394,23 @@
     from_left = shift(to_right, "gy", 1, False)
     from_right = shift(to_left, "gy", -1, False)
     block = (layers, 2, rows, LANES)
-    halo = (layers, 2, rows // 2, LANES)
-    state, fixed, up, down, counts = call(
-        functools.partial(prepare, ("gx", "gy")), [block, (5,) + block, (5,) + halo, (5,) + halo, (2, 2 * rows, LANES)]
-    )(substeps.T, below, fields, above, from_left, from_right)
+    halo = (layers + layers // 2, rows // 2, LANES)
+    state, fixed, up, down = call(prepare, [block, (5,) + block, (5,) + halo, (5,) + halo])(
+        below, fields, above, from_left, from_right
+    )
     over = shift(down, "gx", 1, True)
     under = shift(up, "gx", -1, True)
     first_state, second, up, down = call(
         functools.partial(first_sources, "gz", own), [block, block, (2,) + halo, (2,) + halo]
     )(state, sensors)
-    (fixed,) = call(functools.partial(conduct, "gx"), [(5, layers, 2, 2 * rows, LANES)])(fixed, over, under)
+    fixed, counts = call(
+        functools.partial(conduct, ("gx", "gy")), [(5, layers, 2, 2 * rows, LANES), (2, 2 * rows, LANES)]
+    )(substeps.T, fixed, over, under)
     (rest,) = call(functools.partial(other_sources, "gz", own), [(2,) + block])(sensors)
     over = shift(down, "gx", 1, True)
     under = shift(up, "gx", -1, True)
     depth = layers - 4
-    halo = (2, depth, 2, rows // 2, LANES)
+    halo = (2, depth + depth // 2, rows // 2, LANES)
     state, up, down, sens = call(
         functools.partial(two_steps, False), [(depth, 2, rows, LANES), halo, halo, (own, rows, cols)]
     )(counts, first_state, fixed, over, under, second, rest)

time: 81.9 us -> 73.3 us (0.89)
  blocking collectives: 31 us -> 0 us
  starting transfers between devices: 25.5 us -> 43 us
  waiting for transfers between devices: 13.2 us -> 17.4 us
    all_to_all x1 -> x0, blocking collectives: 31 us -> none  [body(): sensors = lax.all_to_all(message, ('gx', 'gy'), 0, 0, tiled=True)]
    all_to_all x0 -> x1, starting transfers between devices: none -> 20.9 us  [body(): sensors = lax.all_to_all(message, ('gx', 'gy'), 0, 0, tiled=True)]
    all_to_all x0 -> x1, waiting for transfers between devices: none -> 10.4 us  [body(): sensors = lax.all_to_all(message, ('gx', 'gy'), 0, 0, tiled=True)]
    ppermute x10, waiting for transfers between devices: 13.2 us -> 7.03 us  [shift(): return lax.ppermute(cells, axis, pairs)]
    ppermute x10, starting transfers between devices: 25.5 us -> 22.1 us  [shift(): return lax.ppermute(cells, axis, pairs)]
    unnamed x4 -> x6, local copies, waits for them, and re-layouts: 1.61 us -> 1.85 us
  transfers between devices with their start and end apart: 10 -> 11, of which waited for: 6 -> 5; matrix products, arithmetic and copies ran while one was open for 0% -> 0% of each run, Pallas kernels for 3% -> 5%
where the time goes in v4:
time: 73.3 us; the launch traced here: 73 us
  starting transfers between devices  43 us (59%)
  waiting for transfers between devices  17.4 us (24%)
  Pallas kernels  9.94 us (14%)
  local copies, waits for them, and re-layouts  1.86 us (3%)
  between operations  0.8 us (1%)
    ppermute x10, starting transfers between devices, shift(): return lax.ppermute(cells, axis, pairs)  22.1 us
    all_to_all x1, starting transfers between devices, body(): sensors = lax.all_to_all(message, ('gx', 'gy'), 0, 0, tiled=True)  20.9 us
    all_to_all x1, waiting for transfers between devices, body(): sensors = lax.all_to_all(message, ('gx', 'gy'), 0, 0, tiled=True)  10.4 us
    pallas_call x8, Pallas kernels, run(): pl.pallas_call(kernel, out_shape=[jax.ShapeDtypeStruct(o, F32) for o in o...  9.94 us
    ppermute x10, waiting for transfers between devices, shift(): return lax.ppermute(cells, axis, pairs)  7.03 us
    unnamed x6, local copies, waits for them, and re-layouts  1.85 us
  transfers between devices with their start and end apart: 11, of which 5 were waited for; matrix products, arithmetic and copies ran while one was open for 0% of the time, Pallas kernels for 5%

profile of v4, /device:TPU:8, one launch (start us, length us, event | category | flops | bytes accessed | tf_op | source)
XLA Modules:
  0.0 73.0 jit_solution(14363911681967431848)
XLA Ops:
  0.6 0.0 copy-start.2
  0.6 2.1 %shard_map.95 = (f32[6,4,16,128]{3,2,1,0:T(8,128)}, f32[128,128]{1,0:T(8,128)}) custom-call(f32[4,64]{1,0:T(4,128)} %residual_ref.1, s32[1,64]{1,0:T(1,128)} %bitcast.13, s32[1,64]{1,0:T(1,128)} %bitcast.14, f32[4,16,128]{2,1,0:T(8,128)} %adjoint_ref.1, f32[3,4,16,128]{3,2,1,0:T(8,128)} %conductivity_ref.1, f32[4,16,128]{2,1,0:T(8,128)} %ratio_ref.1, ...), custom_call_target="tpu_custom_call" | custom-call | flops 20000 | bytes 20000 | tf_op jit(solution)/shard_map/pallas_call | solution.py:40
  2.7 3.5 %collective-permute-start = (f32[6,4,16,128]{3,2,1,0:T(8,128)}, f32[6,4,16,128]{3,2,1,0:T(8,128)S(1)}, u32[]{:S(2)}, u32[]{:S(2)}) collective-permute-start(f32[6,4,16,128]{3,2,1,0:T(8,128)} %get-tuple-element.20.own_ref), channel_id=1, source_target_pairs={{0,1},{1,2},{2,3},{4,5},{5,6},{6,7},{8,9},{9,10},{10,11},{12,13},{... | collective-permute-start | bytes 589832 | tf_op jit(solution)/shard_map/ppermute | solution.py:371
  6.2 5.5 %collective-permute-start.1 = (f32[6,4,16,128]{3,2,1,0:T(8,128)}, f32[6,4,16,128]{3,2,1,0:T(8,128)S(1)}, u32[]{:S(2)}, u32[]{:S(2)}) collective-permute-start(f32[6,4,16,128]{3,2,1,0:T(8,128)} %get-tuple-element.20.own_ref), channel_id=1, source_target_pairs={{1,0},{2,1},{3,2},{5,4},{6,5},{7,6},{9,8},{10,9},{11,10},{13,12},{... | collective-permute-start | bytes 589832 | tf_op jit(solution)/shard_map/ppermute | solution.py:371
  11.7 1.9 %collective-permute-done.below_ref = f32[6,4,16,128]{3,2,1,0:T(8,128)S(1)} collective-permute-done((f32[6,4,16,128]{3,2,1,0:T(8,128)}, f32[6,4,16,128]{3,2,1,0:T(8,128)S(1)}, u32[]{:S(2)}, u32[]{:S(2)}) %collective-permute-start) | collective-permute-done | bytes 196640 | tf_op jit(solution)/shard_map/ppermute | solution.py:371
  13.6 1.6 %collective-permute-done.1.above_ref = f32[6,4,16,128]{3,2,1,0:T(8,128)S(1)} collective-permute-done((f32[6,4,16,128]{3,2,1,0:T(8,128)}, f32[6,4,16,128]{3,2,1,0:T(8,128)S(1)}, u32[]{:S(2)}, u32[]{:S(2)}) %collective-permute-start.1) | collective-permute-done | bytes 196640 | tf_op jit(solution)/shard_map/ppermute | solution.py:371
  15.2 0.0 copy-start
  15.2 0.9 %copy-done = f32[6,4,16,128]{3,2,1,0:T(8,128)S(1)} copy-done((f32[6,4,16,128]{3,2,1,0:T(8,128)S(1)}, f32[6,4,16,128]{3,2,1,0:T(8,128)}, u32[]{:S(2)}) %copy-start) | copy-done | bytes 196632
  16.1 0.3 shard_map.96
  16.5 2.9 %collective-permute-start.2 = (f32[14,16,128]{2,1,0:T(8,128)S(1)}, f32[14,16,128]{2,1,0:T(8,128)S(1)}, u32[]{:S(2)}, u32[]{:S(2)}) collective-permute-start(f32[14,16,128]{2,1,0:T(8,128)S(1)} %get-tuple-element.21), channel_id=1, source_target_pairs={{0,4},{4,8},{8,12},{1,5},{5,9},{9,13},{2,6},{6,10},{10,14},{3,7},{... | collective-permute-start | bytes 344072 | tf_op jit(solution)/shard_map/ppermute | solution.py:371
  19.3 1.3 %collective-permute-start.3 = (f32[14,16,128]{2,1,0:T(8,128)S(1)}, f32[14,16,128]{2,1,0:T(8,128)S(1)}, u32[]{:S(2)}, u32[]{:S(2)}) collective-permute-start(f32[14,16,128]{2,1,0:T(8,128)S(1)} %get-tuple-element.22), channel_id=1, source_target_pairs={{4,0},{8,4},{12,8},{5,1},{9,5},{13,9},{6,2},{10,6},{14,10},{7,3},{... | collective-permute-start | bytes 344072 | tf_op jit(solution)/shard_map/ppermute | solution.py:371
  20.6 20.9 %all-to-all-start = ((f32[128,1,128]{2,1,0:T(1,128)}), f32[128,1,128]{2,1,0:T(1,128)S(1)}, u32[]{:S(2)}, u32[]{:S(2)}) async-start(f32[128,1,128]{2,1,0:T(1,128)} %bitcast.12), calls=%async_computation | async-start | bytes 131072 | tf_op jit(solution)/shard_map/all_to_all | solution.py:391
  41.6 0.0 collective-permute-done.2.left_ref
  41.6 0.0 collective-permute-done.3.right_ref
  41.6 0.0 copy-start.1
  41.6 0.9 %copy-done.1 = f32[6,4,16,128]{3,2,1,0:T(8,128)S(1)} copy-done((f32[6,4,16,128]{3,2,1,0:T(8,128)S(1)}, f32[6,4,16,128]{3,2,1,0:T(8,128)}, u32[]{:S(2)}) %copy-start.1) | copy-done | bytes 196632
  42.5 0.6 shard_map.97
  43.2 0.0 collective-permute-start.4
  43.2 2.9 %collective-permute-start.5 = (f32[5,18,8,128]{3,2,1,0:T(8,128)S(1)}, f32[5,18,8,128]{3,2,1,0:T(8,128)S(1)}, u32[]{:S(2)}, u32[]{:S(2)}) collective-permute-start(f32[5,18,8,128]{3,2,1,0:T(8,128)S(1)} %get-tuple-element.25), channel_id=1, source_target_pairs={{0,496},{16,0},{32,16},{48,32},{64,48},{80,64},{96,80},{112,96},{1... | collective-permute-start | bytes 1105928 | tf_op jit(solution)/shard_map/ppermute | solution.py:371
  46.1 10.4 %all-to-all-done = f32[128,1,128]{2,1,0:T(1,128)S(1)} async-done(((f32[128,1,128]{2,1,0:T(1,128)}), f32[128,1,128]{2,1,0:T(1,128)S(1)}, u32[]{:S(2)}, u32[]{:S(2)}) %all-to-all-start) | async-done | bytes 65568 | tf_op jit(solution)/shard_map/all_to_all | solution.py:391
  56.5 1.2 %shard_map.99 = (f32[12,2,16,128]{3,2,1,0:T(8,128)S(1)}, f32[12,2,16,128]{3,2,1,0:T(8,128)S(1)}, f32[2,18,8,128]{3,2,1,0:T(8,128)S(1)}, f32[2,18,8,128]{3,2,1,0:T(8,128)S(1)}) custom-call(f32[12,2,16,128]{3,2,1,0:T(8,128)S(1)} %get-tuple-element.27.state_in, f32[128,128]{1,0:T(8,128)S(1)} %bitcast.9), custom_call_target="tpu_custom_call" | custom-call | flops 20000 | bytes 20000 | tf_op jit(solution)/shard_map/pallas_call | solution.py:40
  57.7 0.5 collective-permute-start.6
  58.2 2.5 %collective-permute-start.7 = (f32[2,18,8,128]{3,2,1,0:T(8,128)S(1)}, f32[2,18,8,128]{3,2,1,0:T(8,128)S(1)}, u32[]{:S(2)}, u32[]{:S(2)}) collective-permute-start(f32[2,18,8,128]{3,2,1,0:T(8,128)S(1)} %get-tuple-element.32), channel_id=1, source_target_pairs={{0,496},{16,0},{32,16},{48,32},{64,48},{80,64},{96,80},{112,96},{1... | collective-permute-start | bytes 442376 | tf_op jit(solution)/shard_map/ppermute | solution.py:371
  60.7 1.1 %shard_map.100.refs_0_ = f32[2,12,2,16,128]{4,3,2,1,0:T(8,128)S(1)} custom-call(f32[128,128]{1,0:T(8,128)S(1)} %bitcast.10), custom_call_target="tpu_custom_call" | custom-call | flops 20000 | bytes 20000 | tf_op jit(solution)/shard_map/pallas_call | solution.py:40
  61.8 0.0 collective-permute-done.4.over_ref
  61.8 0.0 collective-permute-done.5.under_ref
  61.8 0.0 copy-done.2
  61.8 0.4 shard_map.98
  62.2 1.3 %collective-permute-done.6.over_ref = f32[2,18,8,128]{3,2,1,0:T(8,128)S(1)} collective-permute-done((f32[2,18,8,128]{3,2,1,0:T(8,128)S(1)}, f32[2,18,8,128]{3,2,1,0:T(8,128)S(1)}, u32[]{:S(2)}, u32[]{:S(2)}) %collective-permute-start.6) | collective-permute-done | bytes 147488 | tf_op jit(solution)/shard_map/ppermute | solution.py:371
  63.5 0.0 collective-permute-done.7.under_ref
  63.5 2.2 %shard_map.101 = (f32[8,2,16,128]{3,2,1,0:T(8,128)S(1)}, f32[2,12,8,128]{3,2,1,0:T(8,128)S(1)}, f32[2,12,8,128]{3,2,1,0:T(8,128)S(1)}, f32[4,16,128]{2,1,0:T(8,128)S(1)}) custom-call(f32[2,32,128]{2,1,0:T(8,128)S(1)} %get-tuple-element.26.counts_ref, f32[12,2,16,128]{3,2,1,0:T(8,128)S(1)} %get-tuple-element.29.state_ref, ...), custom_call_target="tpu_custom_call" | custom-call | flops 20000 | bytes 20000 | tf_op jit(solution)/shard_map/pallas_call | solution.py:40
  65.7 0.0 collective-permute-start.8
  65.7 3.0 %collective-permute-start.9 = (f32[2,12,8,128]{3,2,1,0:T(8,128)S(1)}, f32[2,12,8,128]{3,2,1,0:T(8,128)S(1)}, u32[]{:S(2)}, u32[]{:S(2)}) collective-permute-start(f32[2,12,8,128]{3,2,1,0:T(8,128)S(1)} %get-tuple-element.36), channel_id=1, source_target_pairs={{0,496},{16,0},{32,16},{48,32},{64,48},{80,64},{96,80},{112,96},{1... | collective-permute-start | bytes 294920 | tf_op jit(solution)/shard_map/ppermute | solution.py:371
  68.7 2.3 %collective-permute-done.8.over_ref = f32[2,12,8,128]{3,2,1,0:T(8,128)S(1)} collective-permute-done((f32[2,12,8,128]{3,2,1,0:T(8,128)S(1)}, f32[2,12,8,128]{3,2,1,0:T(8,128)S(1)}, u32[]{:S(2)}, u32[]{:S(2)}) %collective-permute-start.8) | collective-permute-done | bytes 98336 | tf_op jit(solution)/shard_map/ppermute | solution.py:371
  71.0 0.0 collective-permute-done.9.under_ref
  71.0 2.0 %shard_map.102 = (f32[4,16,128]{2,1,0:T(8,128)}, f32[4,16,128]{2,1,0:T(8,128)}) custom-call(f32[2,32,128]{2,1,0:T(8,128)S(1)} %get-tuple-element.26.counts_ref, f32[8,2,16,128]{3,2,1,0:T(8,128)S(1)} %get-tuple-element.34.state_ref, f32[5,12,2,32,128]{4,3,2,1,0:T(8,128)S(1)} %get-tuple-element.30.fixed_ref, ...), custom_call_target="tpu_custom_call" | custom-call | flops 20000 | bytes 20000 | tf_op jit(solution)/shard_map/pallas_call | solution.py:40
  (1 shorter events, 0.0 us)
Async XLA Ops:
  0.6 61.2 %copy-start.2 = (s32[32,4]{0,1:T(4,128)S(1)}, s32[32,4]{0,1:T(4,128)}, u32[]{:S(2)}) copy-start(s32[32,4]{0,1:T(4,128)} %param.15) | copy-start | bytes 1540
  2.7 10.9 %collective-permute-start = (f32[6,4,16,128]{3,2,1,0:T(8,128)}, f32[6,4,16,128]{3,2,1,0:T(8,128)S(1)}, u32[]{:S(2)}, u32[]{:S(2)}) collective-permute-start(f32[6,4,16,128]{3,2,1,0:T(8,128)} %get-tuple-element.20.own_ref), channel_id=1, source_target_pairs={{0,1},{1,2},{2,3},{4,5},{5,6},{6,7},{8,9},{9,10},{10,11},{12,13},{... | collective-permute-start | bytes 589832 | tf_op jit(solution)/shard_map/ppermute | solution.py:371
  6.2 9.0 %collective-permute-start.1 = (f32[6,4,16,128]{3,2,1,0:T(8,128)}, f32[6,4,16,128]{3,2,1,0:T(8,128)S(1)}, u32[]{:S(2)}, u32[]{:S(2)}) collective-permute-start(f32[6,4,16,128]{3,2,1,0:T(8,128)} %get-tuple-element.20.own_ref), channel_id=1, source_target_pairs={{1,0},{2,1},{3,2},{5,4},{6,5},{7,6},{9,8},{10,9},{11,10},{13,12},{... | collective-permute-start | bytes 589832 | tf_op jit(solution)/shard_map/ppermute | solution.py:371
  15.2 0.9 %copy-start = (f32[6,4,16,128]{3,2,1,0:T(8,128)S(1)}, f32[6,4,16,128]{3,2,1,0:T(8,128)}, u32[]{:S(2)}) copy-start(f32[6,4,16,128]{3,2,1,0:T(8,128)} %get-tuple-element.20.own_ref) | copy-start | bytes 589828
  16.5 25.1 %collective-permute-start.2 = (f32[14,16,128]{2,1,0:T(8,128)S(1)}, f32[14,16,128]{2,1,0:T(8,128)S(1)}, u32[]{:S(2)}, u32[]{:S(2)}) collective-permute-start(f32[14,16,128]{2,1,0:T(8,128)S(1)} %get-tuple-element.21), channel_id=1, source_target_pairs={{0,4},{4,8},{8,12},{1,5},{5,9},{9,13},{2,6},{6,10},{10,14},{3,7},{... | collective-permute-start | bytes 344072 | tf_op jit(solution)/shard_map/ppermute | solution.py:371
  19.3 22.3 %collective-permute-start.3 = (f32[14,16,128]{2,1,0:T(8,128)S(1)}, f32[14,16,128]{2,1,0:T(8,128)S(1)}, u32[]{:S(2)}, u32[]{:S(2)}) collective-permute-start(f32[14,16,128]{2,1,0:T(8,128)S(1)} %get-tuple-element.22), channel_id=1, source_target_pairs={{4,0},{8,4},{12,8},{5,1},{9,5},{13,9},{6,2},{10,6},{14,10},{7,3},{... | collective-permute-start | bytes 344072 | tf_op jit(solution)/shard_map/ppermute | solution.py:371
  20.6 35.9 %all-to-all-start = ((f32[128,1,128]{2,1,0:T(1,128)}), f32[128,1,128]{2,1,0:T(1,128)S(1)}, u32[]{:S(2)}, u32[]{:S(2)}) async-start(f32[128,1,128]{2,1,0:T(1,128)} %bitcast.12), calls=%async_computation | async-start | bytes 131072 | tf_op jit(solution)/shard_map/all_to_all | solution.py:391
  41.6 0.9 %copy-start.1 = (f32[6,4,16,128]{3,2,1,0:T(8,128)S(1)}, f32[6,4,16,128]{3,2,1,0:T(8,128)}, u32[]{:S(2)}) copy-start(f32[6,4,16,128]{3,2,1,0:T(8,128)} %get-tuple-element.20.own_ref) | copy-start | bytes 589828
  43.2 18.6 %collective-permute-start.4 = (f32[5,18,8,128]{3,2,1,0:T(8,128)S(1)}, f32[5,18,8,128]{3,2,1,0:T(8,128)S(1)}, u32[]{:S(2)}, u32[]{:S(2)}) collective-permute-start(f32[5,18,8,128]{3,2,1,0:T(8,128)S(1)} %get-tuple-element.24), channel_id=1, source_target_pairs={{0,16},{16,32},{32,48},{48,64},{64,80},{80,96},{96,112},{112,128},... | collective-permute-start | bytes 1105928 | tf_op jit(solution)/shard_map/ppermute | solution.py:371
  43.2 18.6 %collective-permute-start.5 = (f32[5,18,8,128]{3,2,1,0:T(8,128)S(1)}, f32[5,18,8,128]{3,2,1,0:T(8,128)S(1)}, u32[]{:S(2)}, u32[]{:S(2)}) collective-permute-start(f32[5,18,8,128]{3,2,1,0:T(8,128)S(1)} %get-tuple-element.25), channel_id=1, source_target_pairs={{0,496},{16,0},{32,16},{48,32},{64,48},{80,64},{96,80},{112,96},{1... | collective-permute-start | bytes 1105928 | tf_op jit(solution)/shard_map/ppermute | solution.py:371
  57.7 5.8 %collective-permute-start.6 = (f32[2,18,8,128]{3,2,1,0:T(8,128)S(1)}, f32[2,18,8,128]{3,2,1,0:T(8,128)S(1)}, u32[]{:S(2)}, u32[]{:S(2)}) collective-permute-start(f32[2,18,8,128]{3,2,1,0:T(8,128)S(1)} %get-tuple-element.31), channel_id=1, source_target_pairs={{0,16},{16,32},{32,48},{48,64},{64,80},{80,96},{96,112},{112,128},... | collective-permute-start | bytes 442376 | tf_op jit(solution)/shard_map/ppermute | solution.py:371
  58.2 5.3 %collective-permute-start.7 = (f32[2,18,8,128]{3,2,1,0:T(8,128)S(1)}, f32[2,18,8,128]{3,2,1,0:T(8,128)S(1)}, u32[]{:S(2)}, u32[]{:S(2)}) collective-permute-start(f32[2,18,8,128]{3,2,1,0:T(8,128)S(1)} %get-tuple-element.32), channel_id=1, source_target_pairs={{0,496},{16,0},{32,16},{48,32},{64,48},{80,64},{96,80},{112,96},{1... | collective-permute-start | bytes 442376 | tf_op jit(solution)/shard_map/ppermute | solution.py:371
  65.7 5.3 %collective-permute-start.8 = (f32[2,12,8,128]{3,2,1,0:T(8,128)S(1)}, f32[2,12,8,128]{3,2,1,0:T(8,128)S(1)}, u32[]{:S(2)}, u32[]{:S(2)}) collective-permute-start(f32[2,12,8,128]{3,2,1,0:T(8,128)S(1)} %get-tuple-element.35), channel_id=1, source_target_pairs={{0,16},{16,32},{32,48},{48,64},{64,80},{80,96},{96,112},{112,128},... | collective-permute-start | bytes 294920 | tf_op jit(solution)/shard_map/ppermute | solution.py:371
  65.7 5.2 %collective-permute-start.9 = (f32[2,12,8,128]{3,2,1,0:T(8,128)S(1)}, f32[2,12,8,128]{3,2,1,0:T(8,128)S(1)}, u32[]{:S(2)}, u32[]{:S(2)}) collective-permute-start(f32[2,12,8,128]{3,2,1,0:T(8,128)S(1)} %get-tuple-element.36), channel_id=1, source_target_pairs={{0,496},{16,0},{32,16},{48,32},{64,48},{80,64},{96,80},{112,96},{1... | collective-permute-start | bytes 294920 | tf_op jit(solution)/shard_map/ppermute | solution.py:371

commit v5 on v4

--- a/solution.py
+++ b/solution.py
@@ -92,7 +92,7 @@
     return refs[layer // each][field, layer % each]
 
 
-def pack_columns(below_ref, own_ref, above_ref, left_ref, right_ref):
+def pack_columns(below_ref, own_ref, above_ref, left_ref, right_ref, up_ref, down_ref):
     refs = (below_ref, own_ref, above_ref)
     layers = 3 * own_ref.shape[1]
     rows = own_ref.shape[2]
@@ -108,6 +108,11 @@
             right = to_right if q == 0 else jnp.where(piece == q, to_right, right)
         left_ref[j] = left
         right_ref[j] = right
+    for f in range(1, FIELDS):
+        for l in range(layers):
+            plane = stacked(refs, f, l)
+            up_ref[f - 1, l] = plane[: rows // 2]
+            down_ref[f - 1, l] = plane[rows // 2 :]
 
 
 def spread_column(columns, at, shape):
@@ -196,28 +201,35 @@
     for f in range(1, FIELDS):
         values = field(f)
         fixed_ref[f - 1] = values
-        up_ref[f - 1] = fold(values[:, :, :half])
-        down_ref[f - 1] = fold(values[:, :, half:])
-
-
-def fold(block):
-    half = block.shape[0] // 2
-    lane = iota((half,) + block.shape[2:], 2)
+        up_ref[f - 1] = fold_side(values[:, 1, :half])
+        down_ref[f - 1] = fold_side(values[:, 1, half:])
+
+
+def fold_side(side):
+    half = side.shape[0] // 2
+    lane = iota((half,) + side.shape[1:], 2)
     used = (lane < WIDE) | (lane >= LANES - WIDE)
-    low, high = (jnp.where(used, part, 0.0) for part in (block[:half, 1], block[half:, 1]))
-    return jnp.concatenate([block[:, 0], low + pltpu.roll(high, LANES // 2, 2)], axis=0)
-
-
-def unfold(folded):
-    layers = folded.shape[0] * 2 // 3
-    shared = folded[layers:]
+    low, high = (jnp.where(used, part, 0.0) for part in (side[:half], side[half:]))
+    return low + pltpu.roll(high, LANES // 2, 2)
+
+
+def unfold_side(shared):
     lane = iota(shared.shape, 2)
     used = (lane < WIDE) | (lane >= LANES - WIDE)
     parts = [jnp.where(used, part, 0.0) for part in (shared, pltpu.roll(shared, LANES // 2, 2))]
-    return jnp.stack([folded[:layers], jnp.concatenate(parts, axis=0)], axis=1)
-
-
-def conduct(axes, substeps_ref, own_ref, over_ref, under_ref, fixed_ref, counts_ref):
+    return jnp.concatenate(parts, axis=0)
+
+
+def fold(block):
+    return jnp.concatenate([block[:, 0], fold_side(block[:, 1])], axis=0)
+
+
+def unfold(folded):
+    layers = folded.shape[0] * 2 // 3
+    return jnp.stack([folded[:layers], unfold_side(folded[layers:])], axis=1)
+
+
+def conduct(axes, substeps_ref, own_ref, over_ref, under_ref, over_side_ref, under_side_ref, fixed_ref, counts_ref):
     at_x, at_y = (lax.axis_index(axis) for axis in axes)
     n_y, n_x = substeps_ref.shape
     named = substeps_ref[...].astype(F32)
@@ -234,8 +246,14 @@
         counts_ref[0, at_rows] = count(x, at_y)
         counts_ref[1, at_rows] = jnp.where(lane < LANES // 2, count(x, at_y + 1), count(x, at_y - 1))
 
+    pairs = own_ref.shape[1] // 2
+    first = over_side_ref.shape[0] - 5 * pairs
+
     def deep(f, masked=False):
-        over, under = unfold(over_ref[f]), unfold(under_ref[f])
+        over, under = (
+            jnp.stack([centre[f], unfold_side(side[first + f * pairs : first + (f + 1) * pairs])], axis=1)
+            for centre, side in ((over_ref, over_side_ref), (under_ref, under_side_ref))
+        )
         if masked:
             over = jnp.where(at_x > 0, over, 0.0)
             under = jnp.where(at_x < n_x - 1, under, 0.0)
@@ -259,19 +277,24 @@
 
 def send_rows(state, source, up_ref, down_ref):
     half = state.shape[2] // 2
-    up_ref[0] = fold(state[:, :, :half])
-    up_ref[1] = fold(source[:, :, :half])
-    down_ref[0] = fold(state[:, :, half:])
-    down_ref[1] = fold(source[:, :, half:])
-
-
-def first_sources(layer_axis, own, state_in, sensors_ref, state_ref, source_ref, up_ref, down_ref):
+    size = state.shape[0] + state.shape[0] // 2
+    for ref, rows in ((up_ref, slice(0, half)), (down_ref, slice(half, 2 * half))):
+        ref[:size] = fold(state[:, :, rows])
+        ref[size : 2 * size] = fold(source[:, :, rows])
+
+
+def first_sources(layer_axis, own, state_in, sensors_ref, up_side_ref, down_side_ref, state_ref, source_ref, up_ref, down_ref):
     layers, _, rows, _ = state_ref.shape
     second, first = sources(layer_axis, own, layers, rows, sensors_ref, (2, 3))
     state = state_in[...] + first
     state_ref[...] = state
     source_ref[...] = second
     send_rows(state, second, up_ref, down_ref)
+    count, pairs = up_side_ref.shape[:2]
+    base = up_ref.shape[0] - count * pairs
+    for f in range(count):
+        up_ref[base + f * pairs : base + (f + 1) * pairs] = up_side_ref[f]
+        down_ref[base + f * pairs : base + (f + 1) * pairs] = down_side_ref[f]
 
 
 def other_sources(layer_axis, own, sensors_ref, source_ref):
@@ -340,7 +363,9 @@
     everything = slice(0, 2 * rows)
 
     def deep(field, at):
-        return jnp.concatenate([unfold(over_ref[at]), field, unfold(under_ref[at])], axis=2)
+        size = layers + layers // 2
+        over, under = (unfold(ref[at * size : (at + 1) * size]) for ref in (over_ref, under_ref))
+        return jnp.concatenate([over, field, under], axis=2)
 
     def sensed(state, first_row):
         keep = slice((state.shape[0] - own) // 2, (state.shape[0] - own) // 2 + own)
@@ -390,27 +415,30 @@
     above = shift(fields, "gz", -1, False)
     sensors = lax.all_to_all(message, ("gx", "gy"), 0, 0, tiled=True)
     packed = (pl.cdiv(len(needed(layers)), PIECES), rows, LANES)
-    to_left, to_right = call(pack_columns, [packed, packed])(below, fields, above)
+    block = (layers, 2, rows, LANES)
+    lines = (rows // 2, LANES)
+    centre = (5, layers) + lines
+    to_left, to_right, up, down = call(pack_columns, [packed, packed, centre, centre])(below, fields, above)
     from_left = shift(to_right, "gy", 1, False)
     from_right = shift(to_left, "gy", -1, False)
-    block = (layers, 2, rows, LANES)
-    halo = (layers + layers // 2, rows // 2, LANES)
-    state, fixed, up, down = call(prepare, [block, (5,) + block, (5,) + halo, (5,) + halo])(
+    over_fixed = shift(down, "gx", 1, True)
+    under_fixed = shift(up, "gx", -1, True)
+    side = (5, layers // 2) + lines
+    state, fixed, up, down = call(prepare, [block, (5,) + block, side, side])(
         below, fields, above, from_left, from_right
     )
-    over = shift(down, "gx", 1, True)
-    under = shift(up, "gx", -1, True)
+    halo = (2 * (layers + layers // 2) + 5 * (layers // 2),) + lines
     first_state, second, up, down = call(
-        functools.partial(first_sources, "gz", own), [block, block, (2,) + halo, (2,) + halo]
-    )(state, sensors)
-    fixed, counts = call(
-        functools.partial(conduct, ("gx", "gy")), [(5, layers, 2, 2 * rows, LANES), (2, 2 * rows, LANES)]
-    )(substeps.T, fixed, over, under)
+        functools.partial(first_sources, "gz", own), [block, block, halo, halo]
+    )(state, sensors, up, down)
     (rest,) = call(functools.partial(other_sources, "gz", own), [(2,) + block])(sensors)
     over = shift(down, "gx", 1, True)
     under = shift(up, "gx", -1, True)
+    fixed, counts = call(
+        functools.partial(conduct, ("gx", "gy")), [(5, layers, 2, 2 * rows, LANES), (2, 2 * rows, LANES)]
+    )(substeps.T, fixed, over_fixed, under_fixed, over, under)
     depth = layers - 4
-    halo = (2, depth + depth // 2, rows // 2, LANES)
+    halo = (2 * (depth + depth // 2),) + lines
     state, up, down, sens = call(
         functools.partial(two_steps, False), [(depth, 2, rows, LANES), halo, halo, (own, rows, cols)]
     )(counts, first_state, fixed, over, under, second, rest)

time: 73.3 us -> 64.4 us (0.88)
  the two profiles are of different devices: /device:TPU:8 before, /device:TPU:24 now
where the time goes in v5:
time: 64.4 us; the launch traced here: 64.1 us
  starting transfers between devices  38.9 us (60%)
  waiting for transfers between devices  13.8 us (21%)
  Pallas kernels  9.74 us (15%)
  local copies, waits for them, and re-layouts  0.94 us (1%)
  between operations  0.77 us (1%)
    all_to_all x1, starting transfers between devices, body(): sensors = lax.all_to_all(message, ('gx', 'gy'), 0, 0, tiled=True)  19.8 us
    ppermute x10, starting transfers between devices, shift(): return lax.ppermute(cells, axis, pairs)  19.1 us
    ppermute x10, waiting for transfers between devices, shift(): return lax.ppermute(cells, axis, pairs)  10.7 us
    pallas_call x8, Pallas kernels, run(): pl.pallas_call(kernel, out_shape=[jax.ShapeDtypeStruct(o, F32) for o in o...  9.74 us
    all_to_all x1, waiting for transfers between devices, body(): sensors = lax.all_to_all(message, ('gx', 'gy'), 0, 0, tiled=True)  3.06 us
  transfers between devices with their start and end apart: 11, of which 5 were waited for; matrix products, arithmetic and copies ran while one was open for 0% of the time, Pallas kernels for 3%

profile of v5, /device:TPU:24, one launch (start us, length us, event | category | flops | bytes accessed | tf_op | source)
XLA Modules:
  0.0 64.1 jit_solution(1865363281210293657)
XLA Ops:
  0.6 0.0 copy-start.1
  0.6 2.1 %shard_map.95 = (f32[6,4,16,128]{3,2,1,0:T(8,128)}, f32[128,128]{1,0:T(8,128)}) custom-call(f32[4,64]{1,0:T(4,128)} %residual_ref.1, s32[1,64]{1,0:T(1,128)} %bitcast.13, s32[1,64]{1,0:T(1,128)} %bitcast.14, f32[4,16,128]{2,1,0:T(8,128)} %adjoint_ref.1, f32[3,4,16,128]{3,2,1,0:T(8,128)} %conductivity_ref.1, f32[4,16,128]{2,1,0:T(8,128)} %ratio_ref.1, ...), custom_call_target="tpu_custom_call" | custom-call | flops 20000 | bytes 20000 | tf_op jit(solution)/shard_map/pallas_call | solution.py:40
  2.7 1.3 %collective-permute-start = (f32[6,4,16,128]{3,2,1,0:T(8,128)}, f32[6,4,16,128]{3,2,1,0:T(8,128)S(1)}, u32[]{:S(2)}, u32[]{:S(2)}) collective-permute-start(f32[6,4,16,128]{3,2,1,0:T(8,128)} %get-tuple-element.22.own_ref), channel_id=1, source_target_pairs={{0,1},{1,2},{2,3},{4,5},{5,6},{6,7},{8,9},{9,10},{10,11},{12,13},{... | collective-permute-start | bytes 589832 | tf_op jit(solution)/shard_map/ppermute | solution.py:396
  4.0 4.6 %collective-permute-start.1 = (f32[6,4,16,128]{3,2,1,0:T(8,128)}, f32[6,4,16,128]{3,2,1,0:T(8,128)S(1)}, u32[]{:S(2)}, u32[]{:S(2)}) collective-permute-start(f32[6,4,16,128]{3,2,1,0:T(8,128)} %get-tuple-element.22.own_ref), channel_id=1, source_target_pairs={{1,0},{2,1},{3,2},{5,4},{6,5},{7,6},{9,8},{10,9},{11,10},{13,12},{... | collective-permute-start | bytes 589832 | tf_op jit(solution)/shard_map/ppermute | solution.py:396
  8.6 19.8 %all-to-all-start = ((f32[128,1,128]{2,1,0:T(1,128)}), f32[128,1,128]{2,1,0:T(1,128)S(1)}, u32[]{:S(2)}, u32[]{:S(2)}) async-start(f32[128,1,128]{2,1,0:T(1,128)} %bitcast.12), calls=%async_computation | async-start | bytes 131072 | tf_op jit(solution)/shard_map/all_to_all | solution.py:416
  28.4 0.0 collective-permute-done.below_ref
  28.4 0.0 collective-permute-done.1.above_ref
  28.4 0.0 copy-start
  28.4 0.9 %copy-done = f32[6,4,16,128]{3,2,1,0:T(8,128)S(1)} copy-done((f32[6,4,16,128]{3,2,1,0:T(8,128)S(1)}, f32[6,4,16,128]{3,2,1,0:T(8,128)}, u32[]{:S(2)}) %copy-start) | copy-done | bytes 196632
  29.3 0.3 shard_map.96
  29.6 3.0 %collective-permute-start.2 = (f32[14,16,128]{2,1,0:T(8,128)S(1)}, f32[14,16,128]{2,1,0:T(8,128)S(1)}, u32[]{:S(2)}, u32[]{:S(2)}) collective-permute-start(f32[14,16,128]{2,1,0:T(8,128)S(1)} %get-tuple-element.23), channel_id=1, source_target_pairs={{0,4},{4,8},{8,12},{1,5},{5,9},{9,13},{2,6},{6,10},{10,14},{3,7},{... | collective-permute-start | bytes 344072 | tf_op jit(solution)/shard_map/ppermute | solution.py:396
  32.7 1.3 %collective-permute-start.3 = (f32[14,16,128]{2,1,0:T(8,128)S(1)}, f32[14,16,128]{2,1,0:T(8,128)S(1)}, u32[]{:S(2)}, u32[]{:S(2)}) collective-permute-start(f32[14,16,128]{2,1,0:T(8,128)S(1)} %get-tuple-element.24), channel_id=1, source_target_pairs={{4,0},{8,4},{12,8},{5,1},{9,5},{13,9},{6,2},{10,6},{14,10},{7,3},{... | collective-permute-start | bytes 344072 | tf_op jit(solution)/shard_map/ppermute | solution.py:396
  34.0 1.6 %collective-permute-done.2.left_ref = f32[14,16,128]{2,1,0:T(8,128)S(1)} collective-permute-done((f32[14,16,128]{2,1,0:T(8,128)S(1)}, f32[14,16,128]{2,1,0:T(8,128)S(1)}, u32[]{:S(2)}, u32[]{:S(2)}) %collective-permute-start.2) | collective-permute-done | bytes 114720 | tf_op jit(solution)/shard_map/ppermute | solution.py:396
  35.6 4.1 %collective-permute-done.3.right_ref = f32[14,16,128]{2,1,0:T(8,128)S(1)} collective-permute-done((f32[14,16,128]{2,1,0:T(8,128)S(1)}, f32[14,16,128]{2,1,0:T(8,128)S(1)}, u32[]{:S(2)}, u32[]{:S(2)}) %collective-permute-start.3) | collective-permute-done | bytes 114720 | tf_op jit(solution)/shard_map/ppermute | solution.py:396
  39.7 0.6 shard_map.97
  40.3 3.1 %all-to-all-done = f32[128,1,128]{2,1,0:T(1,128)S(1)} async-done(((f32[128,1,128]{2,1,0:T(1,128)}), f32[128,1,128]{2,1,0:T(1,128)S(1)}, u32[]{:S(2)}, u32[]{:S(2)}) %all-to-all-start) | async-done | bytes 65568 | tf_op jit(solution)/shard_map/all_to_all | solution.py:416
  43.3 1.2 %shard_map.98 = (f32[12,2,16,128]{3,2,1,0:T(8,128)S(1)}, f32[12,2,16,128]{3,2,1,0:T(8,128)S(1)}, f32[66,8,128]{2,1,0:T(8,128)S(1)}, f32[66,8,128]{2,1,0:T(8,128)S(1)}) custom-call(f32[12,2,16,128]{3,2,1,0:T(8,128)S(1)} %get-tuple-element.28.state_in, f32[128,128]{1,0:T(8,128)S(1)} %bitcast.9, f32[5,6,8,128]{3,2,1,0:T(8,128)S(1)} %get-tuple-element.30.up_side_ref, ...), custom_call_target="tpu_custom_call" | custom-call | flops 20000 | bytes 20000 | tf_op jit(solution)/shard_map/pallas_call | solution.py:40
  44.6 0.4 collective-permute-start.6
  44.9 2.6 %collective-permute-start.7 = (f32[66,8,128]{2,1,0:T(8,128)S(1)}, f32[66,8,128]{2,1,0:T(8,128)S(1)}, u32[]{:S(2)}, u32[]{:S(2)}) collective-permute-start(f32[66,8,128]{2,1,0:T(8,128)S(1)} %get-tuple-element.33), channel_id=1, source_target_pairs={{0,496},{16,0},{32,16},{48,32},{64,48},{80,64},{96,80},{112,96},{1... | collective-permute-start | bytes 811016 | tf_op jit(solution)/shard_map/ppermute | solution.py:396
  47.5 0.0 collective-permute-start.4
  47.5 3.0 %collective-permute-start.5 = (f32[5,12,8,128]{3,2,1,0:T(8,128)S(1)}, f32[5,12,8,128]{3,2,1,0:T(8,128)S(1)}, u32[]{:S(2)}, u32[]{:S(2)}) collective-permute-start(f32[5,12,8,128]{3,2,1,0:T(8,128)S(1)} %get-tuple-element.27), channel_id=1, source_target_pairs={{0,496},{16,0},{32,16},{48,32},{64,48},{80,64},{96,80},{112,96},{1... | collective-permute-start | bytes 737288 | tf_op jit(solution)/shard_map/ppermute | solution.py:396
  50.5 1.1 %shard_map.100.refs_0_ = f32[2,12,2,16,128]{4,3,2,1,0:T(8,128)S(1)} custom-call(f32[128,128]{1,0:T(8,128)S(1)} %bitcast.10), custom_call_target="tpu_custom_call" | custom-call | flops 20000 | bytes 20000 | tf_op jit(solution)/shard_map/pallas_call | solution.py:40
  51.6 2.8 %collective-permute-done.4.over_ref = f32[5,12,8,128]{3,2,1,0:T(8,128)S(1)} collective-permute-done((f32[5,12,8,128]{3,2,1,0:T(8,128)S(1)}, f32[5,12,8,128]{3,2,1,0:T(8,128)S(1)}, u32[]{:S(2)}, u32[]{:S(2)}) %collective-permute-start.4) | collective-permute-done | bytes 245792 | tf_op jit(solution)/shard_map/ppermute | solution.py:396
  54.4 0.0 collective-permute-done.5.under_ref
  54.4 0.0 collective-permute-done.6.over_side_ref.over_ref
  54.4 0.0 collective-permute-done.7.under_side_ref.under_ref
  54.4 0.0 copy-done.1
  54.4 0.4 shard_map.99
  54.8 2.0 %shard_map.101 = (f32[8,2,16,128]{3,2,1,0:T(8,128)S(1)}, f32[24,8,128]{2,1,0:T(8,128)S(1)}, f32[24,8,128]{2,1,0:T(8,128)S(1)}, f32[4,16,128]{2,1,0:T(8,128)S(1)}) custom-call(f32[2,32,128]{2,1,0:T(8,128)S(1)} %get-tuple-element.34.counts_ref, f32[12,2,16,128]{3,2,1,0:T(8,128)S(1)} %get-tuple-element.35.state_ref, ...), custom_call_target="tpu_custom_call" | custom-call | flops 20000 | bytes 20000 | tf_op jit(solution)/shard_map/pallas_call | solution.py:40
  56.8 0.0 collective-permute-start.8
  56.9 3.0 %collective-permute-start.9 = (f32[24,8,128]{2,1,0:T(8,128)S(1)}, f32[24,8,128]{2,1,0:T(8,128)S(1)}, u32[]{:S(2)}, u32[]{:S(2)}) collective-permute-start(f32[24,8,128]{2,1,0:T(8,128)S(1)} %get-tuple-element.40), channel_id=1, source_target_pairs={{0,496},{16,0},{32,16},{48,32},{64,48},{80,64},{96,80},{112,96},{1... | collective-permute-start | bytes 294920 | tf_op jit(solution)/shard_map/ppermute | solution.py:396
  59.8 2.3 %collective-permute-done.8.over_ref = f32[24,8,128]{2,1,0:T(8,128)S(1)} collective-permute-done((f32[24,8,128]{2,1,0:T(8,128)S(1)}, f32[24,8,128]{2,1,0:T(8,128)S(1)}, u32[]{:S(2)}, u32[]{:S(2)}) %collective-permute-start.8) | collective-permute-done | bytes 98336 | tf_op jit(solution)/shard_map/ppermute | solution.py:396
  62.1 0.0 collective-permute-done.9.under_ref
  62.1 2.0 %shard_map.102 = (f32[4,16,128]{2,1,0:T(8,128)}, f32[4,16,128]{2,1,0:T(8,128)}) custom-call(f32[2,32,128]{2,1,0:T(8,128)S(1)} %get-tuple-element.34.counts_ref, f32[8,2,16,128]{3,2,1,0:T(8,128)S(1)} %get-tuple-element.38.state_ref, f32[5,12,2,32,128]{4,3,2,1,0:T(8,128)S(1)} %get-tuple-element.36.fixed_ref, ...), custom_call_target="tpu_custom_call" | custom-call | flops 20000 | bytes 20000 | tf_op jit(solution)/shard_map/pallas_call | solution.py:40
  (1 shorter events, 0.0 us)
Async XLA Ops:
  0.6 53.7 %copy-start.1 = (s32[32,4]{0,1:T(4,128)S(1)}, s32[32,4]{0,1:T(4,128)}, u32[]{:S(2)}) copy-start(s32[32,4]{0,1:T(4,128)} %param.15) | copy-start | bytes 1540
  2.7 25.7 %collective-permute-start = (f32[6,4,16,128]{3,2,1,0:T(8,128)}, f32[6,4,16,128]{3,2,1,0:T(8,128)S(1)}, u32[]{:S(2)}, u32[]{:S(2)}) collective-permute-start(f32[6,4,16,128]{3,2,1,0:T(8,128)} %get-tuple-element.22.own_ref), channel_id=1, source_target_pairs={{0,1},{1,2},{2,3},{4,5},{5,6},{6,7},{8,9},{9,10},{10,11},{12,13},{... | collective-permute-start | bytes 589832 | tf_op jit(solution)/shard_map/ppermute | solution.py:396
  4.0 24.4 %collective-permute-start.1 = (f32[6,4,16,128]{3,2,1,0:T(8,128)}, f32[6,4,16,128]{3,2,1,0:T(8,128)S(1)}, u32[]{:S(2)}, u32[]{:S(2)}) collective-permute-start(f32[6,4,16,128]{3,2,1,0:T(8,128)} %get-tuple-element.22.own_ref), channel_id=1, source_target_pairs={{1,0},{2,1},{3,2},{5,4},{6,5},{7,6},{9,8},{10,9},{11,10},{13,12},{... | collective-permute-start | bytes 589832 | tf_op jit(solution)/shard_map/ppermute | solution.py:396
  8.6 34.8 %all-to-all-start = ((f32[128,1,128]{2,1,0:T(1,128)}), f32[128,1,128]{2,1,0:T(1,128)S(1)}, u32[]{:S(2)}, u32[]{:S(2)}) async-start(f32[128,1,128]{2,1,0:T(1,128)} %bitcast.12), calls=%async_computation | async-start | bytes 131072 | tf_op jit(solution)/shard_map/all_to_all | solution.py:416
  28.4 0.9 %copy-start = (f32[6,4,16,128]{3,2,1,0:T(8,128)S(1)}, f32[6,4,16,128]{3,2,1,0:T(8,128)}, u32[]{:S(2)}) copy-start(f32[6,4,16,128]{3,2,1,0:T(8,128)} %get-tuple-element.22.own_ref) | copy-start | bytes 589828
  29.6 5.9 %collective-permute-start.2 = (f32[14,16,128]{2,1,0:T(8,128)S(1)}, f32[14,16,128]{2,1,0:T(8,128)S(1)}, u32[]{:S(2)}, u32[]{:S(2)}) collective-permute-start(f32[14,16,128]{2,1,0:T(8,128)S(1)} %get-tuple-element.23), channel_id=1, source_target_pairs={{0,4},{4,8},{8,12},{1,5},{5,9},{9,13},{2,6},{6,10},{10,14},{3,7},{... | collective-permute-start | bytes 344072 | tf_op jit(solution)/shard_map/ppermute | solution.py:396
  32.7 7.0 %collective-permute-start.3 = (f32[14,16,128]{2,1,0:T(8,128)S(1)}, f32[14,16,128]{2,1,0:T(8,128)S(1)}, u32[]{:S(2)}, u32[]{:S(2)}) collective-permute-start(f32[14,16,128]{2,1,0:T(8,128)S(1)} %get-tuple-element.24), channel_id=1, source_target_pairs={{4,0},{8,4},{12,8},{5,1},{9,5},{13,9},{6,2},{10,6},{14,10},{7,3},{... | collective-permute-start | bytes 344072 | tf_op jit(solution)/shard_map/ppermute | solution.py:396
  44.6 9.8 %collective-permute-start.6 = (f32[66,8,128]{2,1,0:T(8,128)S(1)}, f32[66,8,128]{2,1,0:T(8,128)S(1)}, u32[]{:S(2)}, u32[]{:S(2)}) collective-permute-start(f32[66,8,128]{2,1,0:T(8,128)S(1)} %get-tuple-element.32), channel_id=1, source_target_pairs={{0,16},{16,32},{32,48},{48,64},{64,80},{80,96},{96,112},{112,128},... | collective-permute-start | bytes 811016 | tf_op jit(solution)/shard_map/ppermute | solution.py:396
  44.9 9.4 %collective-permute-start.7 = (f32[66,8,128]{2,1,0:T(8,128)S(1)}, f32[66,8,128]{2,1,0:T(8,128)S(1)}, u32[]{:S(2)}, u32[]{:S(2)}) collective-permute-start(f32[66,8,128]{2,1,0:T(8,128)S(1)} %get-tuple-element.33), channel_id=1, source_target_pairs={{0,496},{16,0},{32,16},{48,32},{64,48},{80,64},{96,80},{112,96},{1... | collective-permute-start | bytes 811016 | tf_op jit(solution)/shard_map/ppermute | solution.py:396
  47.5 6.8 %collective-permute-start.4 = (f32[5,12,8,128]{3,2,1,0:T(8,128)S(1)}, f32[5,12,8,128]{3,2,1,0:T(8,128)S(1)}, u32[]{:S(2)}, u32[]{:S(2)}) collective-permute-start(f32[5,12,8,128]{3,2,1,0:T(8,128)S(1)} %get-tuple-element.26), channel_id=1, source_target_pairs={{0,16},{16,32},{32,48},{48,64},{64,80},{80,96},{96,112},{112,128},... | collective-permute-start | bytes 737288 | tf_op jit(solution)/shard_map/ppermute | solution.py:396
  47.5 6.8 %collective-permute-start.5 = (f32[5,12,8,128]{3,2,1,0:T(8,128)S(1)}, f32[5,12,8,128]{3,2,1,0:T(8,128)S(1)}, u32[]{:S(2)}, u32[]{:S(2)}) collective-permute-start(f32[5,12,8,128]{3,2,1,0:T(8,128)S(1)} %get-tuple-element.27), channel_id=1, source_target_pairs={{0,496},{16,0},{32,16},{48,32},{64,48},{80,64},{96,80},{112,96},{1... | collective-permute-start | bytes 737288 | tf_op jit(solution)/shard_map/ppermute | solution.py:396
  56.8 5.3 %collective-permute-start.8 = (f32[24,8,128]{2,1,0:T(8,128)S(1)}, f32[24,8,128]{2,1,0:T(8,128)S(1)}, u32[]{:S(2)}, u32[]{:S(2)}) collective-permute-start(f32[24,8,128]{2,1,0:T(8,128)S(1)} %get-tuple-element.39), channel_id=1, source_target_pairs={{0,16},{16,32},{32,48},{48,64},{64,80},{80,96},{96,112},{112,128},... | collective-permute-start | bytes 294920 | tf_op jit(solution)/shard_map/ppermute | solution.py:396
  56.9 5.2 %collective-permute-start.9 = (f32[24,8,128]{2,1,0:T(8,128)S(1)}, f32[24,8,128]{2,1,0:T(8,128)S(1)}, u32[]{:S(2)}, u32[]{:S(2)}) collective-permute-start(f32[24,8,128]{2,1,0:T(8,128)S(1)} %get-tuple-element.40), channel_id=1, source_target_pairs={{0,496},{16,0},{32,16},{48,32},{64,48},{80,64},{96,80},{112,96},{1... | collective-permute-start | bytes 294920 | tf_op jit(solution)/shard_map/ppermute | solution.py:396

commit v6 on v5

--- a/solution.py
+++ b/solution.py
@@ -246,12 +246,9 @@
         counts_ref[0, at_rows] = count(x, at_y)
         counts_ref[1, at_rows] = jnp.where(lane < LANES // 2, count(x, at_y + 1), count(x, at_y - 1))
 
-    pairs = own_ref.shape[1] // 2
-    first = over_side_ref.shape[0] - 5 * pairs
-
     def deep(f, masked=False):
         over, under = (
-            jnp.stack([centre[f], unfold_side(side[first + f * pairs : first + (f + 1) * pairs])], axis=1)
+            jnp.stack([centre[f], unfold_side(side[f])], axis=1)
             for centre, side in ((over_ref, over_side_ref), (under_ref, under_side_ref))
         )
         if masked:
@@ -283,18 +280,13 @@
         ref[size : 2 * size] = fold(source[:, :, rows])
 
 
-def first_sources(layer_axis, own, state_in, sensors_ref, up_side_ref, down_side_ref, state_ref, source_ref, up_ref, down_ref):
+def first_sources(layer_axis, own, state_in, sensors_ref, state_ref, source_ref, up_ref, down_ref):
     layers, _, rows, _ = state_ref.shape
     second, first = sources(layer_axis, own, layers, rows, sensors_ref, (2, 3))
     state = state_in[...] + first
     state_ref[...] = state
     source_ref[...] = second
     send_rows(state, second, up_ref, down_ref)
-    count, pairs = up_side_ref.shape[:2]
-    base = up_ref.shape[0] - count * pairs
-    for f in range(count):
-        up_ref[base + f * pairs : base + (f + 1) * pairs] = up_side_ref[f]
-        down_ref[base + f * pairs : base + (f + 1) * pairs] = down_side_ref[f]
 
 
 def other_sources(layer_axis, own, sensors_ref, source_ref):
@@ -427,16 +419,18 @@
     state, fixed, up, down = call(prepare, [block, (5,) + block, side, side])(
         below, fields, above, from_left, from_right
     )
-    halo = (2 * (layers + layers // 2) + 5 * (layers // 2),) + lines
+    over_side = shift(down, "gx", 1, True)
+    under_side = shift(up, "gx", -1, True)
+    halo = (2 * (layers + layers // 2),) + lines
     first_state, second, up, down = call(
         functools.partial(first_sources, "gz", own), [block, block, halo, halo]
-    )(state, sensors, up, down)
+    )(state, sensors)
+    fixed, counts = call(
+        functools.partial(conduct, ("gx", "gy")), [(5, layers, 2, 2 * rows, LANES), (2, 2 * rows, LANES)]
+    )(substeps.T, fixed, over_fixed, under_fixed, over_side, under_side)
     (rest,) = call(functools.partial(other_sources, "gz", own), [(2,) + block])(sensors)
     over = shift(down, "gx", 1, True)
     under = shift(up, "gx", -1, True)
-    fixed, counts = call(
-        functools.partial(conduct, ("gx", "gy")), [(5, layers, 2, 2 * rows, LANES), (2, 2 * rows, LANES)]
-    )(substeps.T, fixed, over_fixed, under_fixed, over, under)
     depth = layers - 4
     halo = (2 * (depth + depth // 2),) + lines
     state, up, down, sens = call(

time: 64.4 us -> 63.4 us (0.984)
  the two profiles are of different devices: /device:TPU:24 before, /device:TPU:105 now
where the time goes in v6:
time: 63.4 us; the launch traced here: 63.1 us
  starting transfers between devices  35.9 us (57%)
  waiting for transfers between devices  15.6 us (25%)
  Pallas kernels  9.92 us (16%)
  local copies, waits for them, and re-layouts  0.94 us (1%)
  between operations  0.79 us (1%)
    all_to_all x1, starting transfers between devices, body(): sensors = lax.all_to_all(message, ('gx', 'gy'), 0, 0, tiled=True)  19 us
    ppermute x12, starting transfers between devices, shift(): return lax.ppermute(cells, axis, pairs)  16.9 us
    ppermute x12, waiting for transfers between devices, shift(): return lax.ppermute(cells, axis, pairs)  15.6 us
    pallas_call x8, Pallas kernels, run(): pl.pallas_call(kernel, out_shape=[jax.ShapeDtypeStruct(o, F32) for o in o...  9.92 us
  transfers between devices with their start and end apart: 13, of which 5 were waited for; matrix products, arithmetic and copies ran while one was open for 0% of the time, Pallas kernels for 6%

profile of v6, /device:TPU:105, one launch (start us, length us, event | category | flops | bytes accessed | tf_op | source)
XLA Modules:
  0.0 63.1 jit_solution(11202533594216599420)
XLA Ops:
  0.6 0.0 copy-start.1
  0.6 2.1 %shard_map.95 = (f32[6,4,16,128]{3,2,1,0:T(8,128)}, f32[128,128]{1,0:T(8,128)}) custom-call(f32[4,64]{1,0:T(4,128)} %residual_ref.1, s32[1,64]{1,0:T(1,128)} %bitcast.13, s32[1,64]{1,0:T(1,128)} %bitcast.14, f32[4,16,128]{2,1,0:T(8,128)} %adjoint_ref.1, f32[3,4,16,128]{3,2,1,0:T(8,128)} %conductivity_ref.1, f32[4,16,128]{2,1,0:T(8,128)} %ratio_ref.1, ...), custom_call_target="tpu_custom_call" | custom-call | flops 20000 | bytes 20000 | tf_op jit(solution)/shard_map/pallas_call | solution.py:40
  2.7 3.2 %collective-permute-start = (f32[6,4,16,128]{3,2,1,0:T(8,128)}, f32[6,4,16,128]{3,2,1,0:T(8,128)S(1)}, u32[]{:S(2)}, u32[]{:S(2)}) collective-permute-start(f32[6,4,16,128]{3,2,1,0:T(8,128)} %get-tuple-element.22.own_ref), channel_id=1, source_target_pairs={{0,1},{1,2},{2,3},{4,5},{5,6},{6,7},{8,9},{9,10},{10,11},{12,13},{... | collective-permute-start | bytes 589832 | tf_op jit(solution)/shard_map/ppermute | solution.py:388
  5.9 2.1 %collective-permute-start.1 = (f32[6,4,16,128]{3,2,1,0:T(8,128)}, f32[6,4,16,128]{3,2,1,0:T(8,128)S(1)}, u32[]{:S(2)}, u32[]{:S(2)}) collective-permute-start(f32[6,4,16,128]{3,2,1,0:T(8,128)} %get-tuple-element.22.own_ref), channel_id=1, source_target_pairs={{1,0},{2,1},{3,2},{5,4},{6,5},{7,6},{9,8},{10,9},{11,10},{13,12},{... | collective-permute-start | bytes 589832 | tf_op jit(solution)/shard_map/ppermute | solution.py:388
  8.0 19.0 %all-to-all-start = ((f32[128,1,128]{2,1,0:T(1,128)}), f32[128,1,128]{2,1,0:T(1,128)S(1)}, u32[]{:S(2)}, u32[]{:S(2)}) async-start(f32[128,1,128]{2,1,0:T(1,128)} %bitcast.12), calls=%async_computation | async-start | bytes 131072 | tf_op jit(solution)/shard_map/all_to_all | solution.py:408
  27.0 0.0 collective-permute-done.below_ref
  27.0 0.0 collective-permute-done.1.above_ref
  27.0 0.0 copy-start
  27.1 0.9 %copy-done = f32[6,4,16,128]{3,2,1,0:T(8,128)S(1)} copy-done((f32[6,4,16,128]{3,2,1,0:T(8,128)S(1)}, f32[6,4,16,128]{3,2,1,0:T(8,128)}, u32[]{:S(2)}) %copy-start) | copy-done | bytes 196632
  28.0 0.3 shard_map.96
  28.3 3.1 %collective-permute-start.2 = (f32[14,16,128]{2,1,0:T(8,128)S(1)}, f32[14,16,128]{2,1,0:T(8,128)S(1)}, u32[]{:S(2)}, u32[]{:S(2)}) collective-permute-start(f32[14,16,128]{2,1,0:T(8,128)S(1)} %get-tuple-element.23), channel_id=1, source_target_pairs={{0,4},{4,8},{8,12},{1,5},{5,9},{9,13},{2,6},{6,10},{10,14},{3,7},{... | collective-permute-start | bytes 344072 | tf_op jit(solution)/shard_map/ppermute | solution.py:388
  31.4 1.3 %collective-permute-start.3 = (f32[14,16,128]{2,1,0:T(8,128)S(1)}, f32[14,16,128]{2,1,0:T(8,128)S(1)}, u32[]{:S(2)}, u32[]{:S(2)}) collective-permute-start(f32[14,16,128]{2,1,0:T(8,128)S(1)} %get-tuple-element.24), channel_id=1, source_target_pairs={{4,0},{8,4},{12,8},{5,1},{9,5},{13,9},{6,2},{10,6},{14,10},{7,3},{... | collective-permute-start | bytes 344072 | tf_op jit(solution)/shard_map/ppermute | solution.py:388
  32.7 0.8 %collective-permute-done.2.left_ref = f32[14,16,128]{2,1,0:T(8,128)S(1)} collective-permute-done((f32[14,16,128]{2,1,0:T(8,128)S(1)}, f32[14,16,128]{2,1,0:T(8,128)S(1)}, u32[]{:S(2)}, u32[]{:S(2)}) %collective-permute-start.2) | collective-permute-done | bytes 114720 | tf_op jit(solution)/shard_map/ppermute | solution.py:388
  33.5 4.0 %collective-permute-done.3.right_ref = f32[14,16,128]{2,1,0:T(8,128)S(1)} collective-permute-done((f32[14,16,128]{2,1,0:T(8,128)S(1)}, f32[14,16,128]{2,1,0:T(8,128)S(1)}, u32[]{:S(2)}, u32[]{:S(2)}) %collective-permute-start.3) | collective-permute-done | bytes 114720 | tf_op jit(solution)/shard_map/ppermute | solution.py:388
  37.5 0.6 shard_map.97
  38.1 3.7 %collective-permute-start.6 = (f32[5,6,8,128]{3,2,1,0:T(8,128)S(1)}, f32[5,6,8,128]{3,2,1,0:T(8,128)S(1)}, u32[]{:S(2)}, u32[]{:S(2)}) collective-permute-start(f32[5,6,8,128]{3,2,1,0:T(8,128)S(1)} %get-tuple-element.28), channel_id=1, source_target_pairs={{0,16},{16,32},{32,48},{48,64},{64,80},{80,96},{96,112},{112,128},... | collective-permute-start | bytes 368648 | tf_op jit(solution)/shard_map/ppermute | solution.py:388
  41.9 0.0 collective-permute-start.4
  41.9 0.5 collective-permute-start.5
  42.4 0.0 all-to-all-done
  42.4 1.2 %shard_map.99 = (f32[12,2,16,128]{3,2,1,0:T(8,128)S(1)}, f32[12,2,16,128]{3,2,1,0:T(8,128)S(1)}, f32[36,8,128]{2,1,0:T(8,128)S(1)}, f32[36,8,128]{2,1,0:T(8,128)S(1)}) custom-call(f32[12,2,16,128]{3,2,1,0:T(8,128)S(1)} %get-tuple-element.31.state_in, f32[128,128]{1,0:T(8,128)S(1)} %bitcast.9), custom_call_target="tpu_custom_call" | custom-call | flops 20000 | bytes 20000 | tf_op jit(solution)/shard_map/pallas_call | solution.py:40
  43.6 2.5 %collective-permute-start.8 = (f32[36,8,128]{2,1,0:T(8,128)S(1)}, f32[36,8,128]{2,1,0:T(8,128)S(1)}, u32[]{:S(2)}, u32[]{:S(2)}) collective-permute-start(f32[36,8,128]{2,1,0:T(8,128)S(1)} %get-tuple-element.35), channel_id=1, source_target_pairs={{0,16},{16,32},{32,48},{48,64},{64,80},{80,96},{96,112},{112,128},... | collective-permute-start | bytes 442376 | tf_op jit(solution)/shard_map/ppermute | solution.py:388
  46.1 0.0 collective-permute-start.9
  46.1 0.0 collective-permute-done.6.over_side_ref
  46.1 0.0 collective-permute-start.7
  46.1 1.1 %shard_map.100.refs_0_ = f32[2,12,2,16,128]{4,3,2,1,0:T(8,128)S(1)} custom-call(f32[128,128]{1,0:T(8,128)S(1)} %bitcast.10), custom_call_target="tpu_custom_call" | custom-call | flops 20000 | bytes 20000 | tf_op jit(solution)/shard_map/pallas_call | solution.py:40
  47.2 6.0 %collective-permute-done.7.under_side_ref = f32[5,6,8,128]{3,2,1,0:T(8,128)S(1)} collective-permute-done((f32[5,6,8,128]{3,2,1,0:T(8,128)S(1)}, f32[5,6,8,128]{3,2,1,0:T(8,128)S(1)}, u32[]{:S(2)}, u32[]{:S(2)}) %collective-permute-start.7) | collective-permute-done | bytes 122912 | tf_op jit(solution)/shard_map/ppermute | solution.py:388
  53.2 0.0 collective-permute-done.4.over_ref
  53.2 0.0 collective-permute-done.5.under_ref
  53.2 0.0 copy-done.1
  53.2 0.4 shard_map.98
  53.6 0.0 collective-permute-done.8.over_ref
  53.6 0.0 collective-permute-done.9.under_ref
  53.6 2.2 %shard_map.101 = (f32[8,2,16,128]{3,2,1,0:T(8,128)S(1)}, f32[24,8,128]{2,1,0:T(8,128)S(1)}, f32[24,8,128]{2,1,0:T(8,128)S(1)}, f32[4,16,128]{2,1,0:T(8,128)S(1)}) custom-call(f32[2,32,128]{2,1,0:T(8,128)S(1)} %get-tuple-element.30.counts_ref, f32[12,2,16,128]{3,2,1,0:T(8,128)S(1)} %get-tuple-element.33.state_ref, ...), custom_call_target="tpu_custom_call" | custom-call | flops 20000 | bytes 20000 | tf_op jit(solution)/shard_map/pallas_call | solution.py:40
  55.8 0.0 collective-permute-start.10
  55.8 0.5 collective-permute-start.11
  56.3 1.1 %collective-permute-done.10.over_ref = f32[24,8,128]{2,1,0:T(8,128)S(1)} collective-permute-done((f32[24,8,128]{2,1,0:T(8,128)S(1)}, f32[24,8,128]{2,1,0:T(8,128)S(1)}, u32[]{:S(2)}, u32[]{:S(2)}) %collective-permute-start.10) | collective-permute-done | bytes 98336 | tf_op jit(solution)/shard_map/ppermute | solution.py:388
  57.5 3.6 %collective-permute-done.11.under_ref = f32[24,8,128]{2,1,0:T(8,128)S(1)} collective-permute-done((f32[24,8,128]{2,1,0:T(8,128)S(1)}, f32[24,8,128]{2,1,0:T(8,128)S(1)}, u32[]{:S(2)}, u32[]{:S(2)}) %collective-permute-start.11) | collective-permute-done | bytes 98336 | tf_op jit(solution)/shard_map/ppermute | solution.py:388
  61.1 2.0 %shard_map.102 = (f32[4,16,128]{2,1,0:T(8,128)}, f32[4,16,128]{2,1,0:T(8,128)}) custom-call(f32[2,32,128]{2,1,0:T(8,128)S(1)} %get-tuple-element.30.counts_ref, f32[8,2,16,128]{3,2,1,0:T(8,128)S(1)} %get-tuple-element.38.state_ref, f32[5,12,2,32,128]{4,3,2,1,0:T(8,128)S(1)} %get-tuple-element.34.fixed_ref, ...), custom_call_target="tpu_custom_call" | custom-call | flops 20000 | bytes 20000 | tf_op jit(solution)/shard_map/pallas_call | solution.py:40
  (1 shorter events, 0.0 us)
Async XLA Ops:
  0.6 52.5 %copy-start.1 = (s32[32,4]{0,1:T(4,128)S(1)}, s32[32,4]{0,1:T(4,128)}, u32[]{:S(2)}) copy-start(s32[32,4]{0,1:T(4,128)} %param.15) | copy-start | bytes 1540
  2.7 24.3 %collective-permute-start = (f32[6,4,16,128]{3,2,1,0:T(8,128)}, f32[6,4,16,128]{3,2,1,0:T(8,128)S(1)}, u32[]{:S(2)}, u32[]{:S(2)}) collective-permute-start(f32[6,4,16,128]{3,2,1,0:T(8,128)} %get-tuple-element.22.own_ref), channel_id=1, source_target_pairs={{0,1},{1,2},{2,3},{4,5},{5,6},{6,7},{8,9},{9,10},{10,11},{12,13},{... | collective-permute-start | bytes 589832 | tf_op jit(solution)/shard_map/ppermute | solution.py:388
  5.9 21.1 %collective-permute-start.1 = (f32[6,4,16,128]{3,2,1,0:T(8,128)}, f32[6,4,16,128]{3,2,1,0:T(8,128)S(1)}, u32[]{:S(2)}, u32[]{:S(2)}) collective-permute-start(f32[6,4,16,128]{3,2,1,0:T(8,128)} %get-tuple-element.22.own_ref), channel_id=1, source_target_pairs={{1,0},{2,1},{3,2},{5,4},{6,5},{7,6},{9,8},{10,9},{11,10},{13,12},{... | collective-permute-start | bytes 589832 | tf_op jit(solution)/shard_map/ppermute | solution.py:388
  8.0 34.4 %all-to-all-start = ((f32[128,1,128]{2,1,0:T(1,128)}), f32[128,1,128]{2,1,0:T(1,128)S(1)}, u32[]{:S(2)}, u32[]{:S(2)}) async-start(f32[128,1,128]{2,1,0:T(1,128)} %bitcast.12), calls=%async_computation | async-start | bytes 131072 | tf_op jit(solution)/shard_map/all_to_all | solution.py:408
  27.0 0.9 %copy-start = (f32[6,4,16,128]{3,2,1,0:T(8,128)S(1)}, f32[6,4,16,128]{3,2,1,0:T(8,128)}, u32[]{:S(2)}) copy-start(f32[6,4,16,128]{3,2,1,0:T(8,128)} %get-tuple-element.22.own_ref) | copy-start | bytes 589828
  28.3 5.3 %collective-permute-start.2 = (f32[14,16,128]{2,1,0:T(8,128)S(1)}, f32[14,16,128]{2,1,0:T(8,128)S(1)}, u32[]{:S(2)}, u32[]{:S(2)}) collective-permute-start(f32[14,16,128]{2,1,0:T(8,128)S(1)} %get-tuple-element.23), channel_id=1, source_target_pairs={{0,4},{4,8},{8,12},{1,5},{5,9},{9,13},{2,6},{6,10},{10,14},{3,7},{... | collective-permute-start | bytes 344072 | tf_op jit(solution)/shard_map/ppermute | solution.py:388
  31.4 6.1 %collective-permute-start.3 = (f32[14,16,128]{2,1,0:T(8,128)S(1)}, f32[14,16,128]{2,1,0:T(8,128)S(1)}, u32[]{:S(2)}, u32[]{:S(2)}) collective-permute-start(f32[14,16,128]{2,1,0:T(8,128)S(1)} %get-tuple-element.24), channel_id=1, source_target_pairs={{4,0},{8,4},{12,8},{5,1},{9,5},{13,9},{6,2},{10,6},{14,10},{7,3},{... | collective-permute-start | bytes 344072 | tf_op jit(solution)/shard_map/ppermute | solution.py:388
  38.1 7.9 %collective-permute-start.6 = (f32[5,6,8,128]{3,2,1,0:T(8,128)S(1)}, f32[5,6,8,128]{3,2,1,0:T(8,128)S(1)}, u32[]{:S(2)}, u32[]{:S(2)}) collective-permute-start(f32[5,6,8,128]{3,2,1,0:T(8,128)S(1)} %get-tuple-element.28), channel_id=1, source_target_pairs={{0,16},{16,32},{32,48},{48,64},{64,80},{80,96},{96,112},{112,128},... | collective-permute-start | bytes 368648 | tf_op jit(solution)/shard_map/ppermute | solution.py:388
  41.9 11.3 %collective-permute-start.4 = (f32[5,12,8,128]{3,2,1,0:T(8,128)S(1)}, f32[5,12,8,128]{3,2,1,0:T(8,128)S(1)}, u32[]{:S(2)}, u32[]{:S(2)}) collective-permute-start(f32[5,12,8,128]{3,2,1,0:T(8,128)S(1)} %get-tuple-element.26), channel_id=1, source_target_pairs={{0,16},{16,32},{32,48},{48,64},{64,80},{80,96},{96,112},{112,128},... | collective-permute-start | bytes 737288 | tf_op jit(solution)/shard_map/ppermute | solution.py:388
  41.9 11.3 %collective-permute-start.5 = (f32[5,12,8,128]{3,2,1,0:T(8,128)S(1)}, f32[5,12,8,128]{3,2,1,0:T(8,128)S(1)}, u32[]{:S(2)}, u32[]{:S(2)}) collective-permute-start(f32[5,12,8,128]{3,2,1,0:T(8,128)S(1)} %get-tuple-element.27), channel_id=1, source_target_pairs={{0,496},{16,0},{32,16},{48,32},{64,48},{80,64},{96,80},{112,96},{1... | collective-permute-start | bytes 737288 | tf_op jit(solution)/shard_map/ppermute | solution.py:388
  43.6 10.0 %collective-permute-start.8 = (f32[36,8,128]{2,1,0:T(8,128)S(1)}, f32[36,8,128]{2,1,0:T(8,128)S(1)}, u32[]{:S(2)}, u32[]{:S(2)}) collective-permute-start(f32[36,8,128]{2,1,0:T(8,128)S(1)} %get-tuple-element.35), channel_id=1, source_target_pairs={{0,16},{16,32},{32,48},{48,64},{64,80},{80,96},{96,112},{112,128},... | collective-permute-start | bytes 442376 | tf_op jit(solution)/shard_map/ppermute | solution.py:388
  46.1 7.5 %collective-permute-start.9 = (f32[36,8,128]{2,1,0:T(8,128)S(1)}, f32[36,8,128]{2,1,0:T(8,128)S(1)}, u32[]{:S(2)}, u32[]{:S(2)}) collective-permute-start(f32[36,8,128]{2,1,0:T(8,128)S(1)} %get-tuple-element.36), channel_id=1, source_target_pairs={{0,496},{16,0},{32,16},{48,32},{64,48},{80,64},{96,80},{112,96},{1... | collective-permute-start | bytes 442376 | tf_op jit(solution)/shard_map/ppermute | solution.py:388
  46.1 7.1 %collective-permute-start.7 = (f32[5,6,8,128]{3,2,1,0:T(8,128)S(1)}, f32[5,6,8,128]{3,2,1,0:T(8,128)S(1)}, u32[]{:S(2)}, u32[]{:S(2)}) collective-permute-start(f32[5,6,8,128]{3,2,1,0:T(8,128)S(1)} %get-tuple-element.29), channel_id=1, source_target_pairs={{0,496},{16,0},{32,16},{48,32},{64,48},{80,64},{96,80},{112,96},{1... | collective-permute-start | bytes 368648 | tf_op jit(solution)/shard_map/ppermute | solution.py:388
  55.8 1.7 %collective-permute-start.10 = (f32[24,8,128]{2,1,0:T(8,128)S(1)}, f32[24,8,128]{2,1,0:T(8,128)S(1)}, u32[]{:S(2)}, u32[]{:S(2)}) collective-permute-start(f32[24,8,128]{2,1,0:T(8,128)S(1)} %get-tuple-element.39), channel_id=1, source_target_pairs={{0,16},{16,32},{32,48},{48,64},{64,80},{80,96},{96,112},{112,128},... | collective-permute-start | bytes 294920 | tf_op jit(solution)/shard_map/ppermute | solution.py:388
  55.8 5.3 %collective-permute-start.11 = (f32[24,8,128]{2,1,0:T(8,128)S(1)}, f32[24,8,128]{2,1,0:T(8,128)S(1)}, u32[]{:S(2)}, u32[]{:S(2)}) collective-permute-start(f32[24,8,128]{2,1,0:T(8,128)S(1)} %get-tuple-element.40), channel_id=1, source_target_pairs={{0,496},{16,0},{32,16},{48,32},{64,48},{80,64},{96,80},{112,96},{1... | collective-permute-start | bytes 294920 | tf_op jit(solution)/shard_map/ppermute | solution.py:388

commit v7 on v4

--- a/solution.py
+++ b/solution.py
@@ -196,8 +196,17 @@
     for f in range(1, FIELDS):
         values = field(f)
         fixed_ref[f - 1] = values
-        up_ref[f - 1] = fold(values[:, :, :half])
-        down_ref[f - 1] = fold(values[:, :, half:])
+        start, stop, trim = sent(f - 1, layers)
+        values = values[trim : layers - trim]
+        up_ref[start:stop] = fold(values[:, :, :half])
+        down_ref[start:stop] = fold(values[:, :, half:])
+
+
+def sent(field, layers):
+    trims = [0 if f in (2, 3) else 1 for f in range(5)]
+    sizes = [(layers - 2 * trim) * 3 // 2 for trim in trims]
+    start = sum(sizes[:field])
+    return start, start + sizes[field], trims[field]
 
 
 def fold(block):
@@ -235,7 +244,11 @@
         counts_ref[1, at_rows] = jnp.where(lane < LANES // 2, count(x, at_y + 1), count(x, at_y - 1))
 
     def deep(f, masked=False):
-        over, under = unfold(over_ref[f]), unfold(under_ref[f])
+        start, stop, trim = sent(f, own_ref.shape[1])
+        over, under = unfold(over_ref[start:stop]), unfold(under_ref[start:stop])
+        if trim:
+            none = jnp.zeros((trim,) + over.shape[1:], F32)
+            over, under = (jnp.concatenate([none, part, none], axis=0) for part in (over, under))
         if masked:
             over = jnp.where(at_x > 0, over, 0.0)
             under = jnp.where(at_x < n_x - 1, under, 0.0)
@@ -395,7 +408,7 @@
     from_right = shift(to_left, "gy", -1, False)
     block = (layers, 2, rows, LANES)
     halo = (layers + layers // 2, rows // 2, LANES)
-    state, fixed, up, down = call(prepare, [block, (5,) + block, (5,) + halo, (5,) + halo])(
+    state, fixed, up, down = call(prepare, [block, (5,) + block] + [(sent(4, layers)[1],) + halo[1:]] * 2)(
         below, fields, above, from_left, from_right
     )
     over = shift(down, "gx", 1, True)

time: 73.3 us -> 73.3 us (level)
  no operation moved by 1% of the time
where the time goes in v7:
time: 73.3 us; the launch traced here: 73 us
  starting transfers between devices  43 us (59%)
  waiting for transfers between devices  17.4 us (24%)
  Pallas kernels  9.91 us (14%)
  local copies, waits for them, and re-layouts  1.86 us (3%)
  between operations  0.8 us (1%)
    ppermute x10, starting transfers between devices, shift(): return lax.ppermute(cells, axis, pairs)  22.1 us
    all_to_all x1, starting transfers between devices, body(): sensors = lax.all_to_all(message, ('gx', 'gy'), 0, 0, tiled=True)  20.9 us
    all_to_all x1, waiting for transfers between devices, body(): sensors = lax.all_to_all(message, ('gx', 'gy'), 0, 0, tiled=True)  10.4 us
    pallas_call x8, Pallas kernels, run(): pl.pallas_call(kernel, out_shape=[jax.ShapeDtypeStruct(o, F32) for o in o...  9.91 us
    ppermute x10, waiting for transfers between devices, shift(): return lax.ppermute(cells, axis, pairs)  7.05 us
    unnamed x6, local copies, waits for them, and re-layouts  1.85 us
  transfers between devices with their start and end apart: 11, of which 5 were waited for; matrix products, arithmetic and copies ran while one was open for 0% of the time, Pallas kernels for 5%

profile of v7, /device:TPU:8, one launch (start us, length us, event | category | flops | bytes accessed | tf_op | source)
XLA Modules:
  0.0 73.0 jit_solution(14787396442055800467)
XLA Ops:
  0.6 0.0 copy-start.2
  0.6 2.1 %shard_map.95 = (f32[6,4,16,128]{3,2,1,0:T(8,128)}, f32[128,128]{1,0:T(8,128)}) custom-call(f32[4,64]{1,0:T(4,128)} %residual_ref.1, s32[1,64]{1,0:T(1,128)} %bitcast.13, s32[1,64]{1,0:T(1,128)} %bitcast.14, f32[4,16,128]{2,1,0:T(8,128)} %adjoint_ref.1, f32[3,4,16,128]{3,2,1,0:T(8,128)} %conductivity_ref.1, f32[4,16,128]{2,1,0:T(8,128)} %ratio_ref.1, ...), custom_call_target="tpu_custom_call" | custom-call | flops 20000 | bytes 20000 | tf_op jit(solution)/shard_map/pallas_call | solution.py:40
  2.7 3.5 %collective-permute-start = (f32[6,4,16,128]{3,2,1,0:T(8,128)}, f32[6,4,16,128]{3,2,1,0:T(8,128)S(1)}, u32[]{:S(2)}, u32[]{:S(2)}) collective-permute-start(f32[6,4,16,128]{3,2,1,0:T(8,128)} %get-tuple-element.20.own_ref), channel_id=1, source_target_pairs={{0,1},{1,2},{2,3},{4,5},{5,6},{6,7},{8,9},{9,10},{10,11},{12,13},{... | collective-permute-start | bytes 589832 | tf_op jit(solution)/shard_map/ppermute | solution.py:384
  6.2 5.5 %collective-permute-start.1 = (f32[6,4,16,128]{3,2,1,0:T(8,128)}, f32[6,4,16,128]{3,2,1,0:T(8,128)S(1)}, u32[]{:S(2)}, u32[]{:S(2)}) collective-permute-start(f32[6,4,16,128]{3,2,1,0:T(8,128)} %get-tuple-element.20.own_ref), channel_id=1, source_target_pairs={{1,0},{2,1},{3,2},{5,4},{6,5},{7,6},{9,8},{10,9},{11,10},{13,12},{... | collective-permute-start | bytes 589832 | tf_op jit(solution)/shard_map/ppermute | solution.py:384
  11.7 1.9 %collective-permute-done.below_ref = f32[6,4,16,128]{3,2,1,0:T(8,128)S(1)} collective-permute-done((f32[6,4,16,128]{3,2,1,0:T(8,128)}, f32[6,4,16,128]{3,2,1,0:T(8,128)S(1)}, u32[]{:S(2)}, u32[]{:S(2)}) %collective-permute-start) | collective-permute-done | bytes 196640 | tf_op jit(solution)/shard_map/ppermute | solution.py:384
  13.6 1.6 %collective-permute-done.1.above_ref = f32[6,4,16,128]{3,2,1,0:T(8,128)S(1)} collective-permute-done((f32[6,4,16,128]{3,2,1,0:T(8,128)}, f32[6,4,16,128]{3,2,1,0:T(8,128)S(1)}, u32[]{:S(2)}, u32[]{:S(2)}) %collective-permute-start.1) | collective-permute-done | bytes 196640 | tf_op jit(solution)/shard_map/ppermute | solution.py:384
  15.2 0.0 copy-start
  15.2 0.9 %copy-done = f32[6,4,16,128]{3,2,1,0:T(8,128)S(1)} copy-done((f32[6,4,16,128]{3,2,1,0:T(8,128)S(1)}, f32[6,4,16,128]{3,2,1,0:T(8,128)}, u32[]{:S(2)}) %copy-start) | copy-done | bytes 196632
  16.1 0.3 shard_map.96
  16.5 2.9 %collective-permute-start.2 = (f32[14,16,128]{2,1,0:T(8,128)S(1)}, f32[14,16,128]{2,1,0:T(8,128)S(1)}, u32[]{:S(2)}, u32[]{:S(2)}) collective-permute-start(f32[14,16,128]{2,1,0:T(8,128)S(1)} %get-tuple-element.21), channel_id=1, source_target_pairs={{0,4},{4,8},{8,12},{1,5},{5,9},{9,13},{2,6},{6,10},{10,14},{3,7},{... | collective-permute-start | bytes 344072 | tf_op jit(solution)/shard_map/ppermute | solution.py:384
  19.3 1.3 %collective-permute-start.3 = (f32[14,16,128]{2,1,0:T(8,128)S(1)}, f32[14,16,128]{2,1,0:T(8,128)S(1)}, u32[]{:S(2)}, u32[]{:S(2)}) collective-permute-start(f32[14,16,128]{2,1,0:T(8,128)S(1)} %get-tuple-element.22), channel_id=1, source_target_pairs={{4,0},{8,4},{12,8},{5,1},{9,5},{13,9},{6,2},{10,6},{14,10},{7,3},{... | collective-permute-start | bytes 344072 | tf_op jit(solution)/shard_map/ppermute | solution.py:384
  20.6 20.9 %all-to-all-start = ((f32[128,1,128]{2,1,0:T(1,128)}), f32[128,1,128]{2,1,0:T(1,128)S(1)}, u32[]{:S(2)}, u32[]{:S(2)}) async-start(f32[128,1,128]{2,1,0:T(1,128)} %bitcast.12), calls=%async_computation | async-start | bytes 131072 | tf_op jit(solution)/shard_map/all_to_all | solution.py:404
  41.6 0.0 collective-permute-done.2.left_ref
  41.6 0.0 collective-permute-done.3.right_ref
  41.6 0.0 copy-start.1
  41.6 0.9 %copy-done.1 = f32[6,4,16,128]{3,2,1,0:T(8,128)S(1)} copy-done((f32[6,4,16,128]{3,2,1,0:T(8,128)S(1)}, f32[6,4,16,128]{3,2,1,0:T(8,128)}, u32[]{:S(2)}) %copy-start.1) | copy-done | bytes 196632
  42.5 0.6 shard_map.97
  43.2 0.0 collective-permute-start.4
  43.2 2.9 %collective-permute-start.5 = (f32[81,8,128]{2,1,0:T(8,128)S(1)}, f32[81,8,128]{2,1,0:T(8,128)S(1)}, u32[]{:S(2)}, u32[]{:S(2)}) collective-permute-start(f32[81,8,128]{2,1,0:T(8,128)S(1)} %get-tuple-element.25), channel_id=1, source_target_pairs={{0,496},{16,0},{32,16},{48,32},{64,48},{80,64},{96,80},{112,96},{1... | collective-permute-start | bytes 995336 | tf_op jit(solution)/shard_map/ppermute | solution.py:384
  46.1 10.4 %all-to-all-done = f32[128,1,128]{2,1,0:T(1,128)S(1)} async-done(((f32[128,1,128]{2,1,0:T(1,128)}), f32[128,1,128]{2,1,0:T(1,128)S(1)}, u32[]{:S(2)}, u32[]{:S(2)}) %all-to-all-start) | async-done | bytes 65568 | tf_op jit(solution)/shard_map/all_to_all | solution.py:404
  56.5 1.2 %shard_map.99 = (f32[12,2,16,128]{3,2,1,0:T(8,128)S(1)}, f32[12,2,16,128]{3,2,1,0:T(8,128)S(1)}, f32[2,18,8,128]{3,2,1,0:T(8,128)S(1)}, f32[2,18,8,128]{3,2,1,0:T(8,128)S(1)}) custom-call(f32[12,2,16,128]{3,2,1,0:T(8,128)S(1)} %get-tuple-element.27.state_in, f32[128,128]{1,0:T(8,128)S(1)} %bitcast.9), custom_call_target="tpu_custom_call" | custom-call | flops 20000 | bytes 20000 | tf_op jit(solution)/shard_map/pallas_call | solution.py:40
  57.7 0.5 collective-permute-start.6
  58.2 2.5 %collective-permute-start.7 = (f32[2,18,8,128]{3,2,1,0:T(8,128)S(1)}, f32[2,18,8,128]{3,2,1,0:T(8,128)S(1)}, u32[]{:S(2)}, u32[]{:S(2)}) collective-permute-start(f32[2,18,8,128]{3,2,1,0:T(8,128)S(1)} %get-tuple-element.32), channel_id=1, source_target_pairs={{0,496},{16,0},{32,16},{48,32},{64,48},{80,64},{96,80},{112,96},{1... | collective-permute-start | bytes 442376 | tf_op jit(solution)/shard_map/ppermute | solution.py:384
  60.7 1.1 %shard_map.100.refs_0_ = f32[2,12,2,16,128]{4,3,2,1,0:T(8,128)S(1)} custom-call(f32[128,128]{1,0:T(8,128)S(1)} %bitcast.10), custom_call_target="tpu_custom_call" | custom-call | flops 20000 | bytes 20000 | tf_op jit(solution)/shard_map/pallas_call | solution.py:40
  61.8 0.0 collective-permute-done.4.over_ref
  61.8 0.0 collective-permute-done.5.under_ref
  61.8 0.0 copy-done.2
  61.8 0.4 shard_map.98
  62.2 1.3 %collective-permute-done.6.over_ref = f32[2,18,8,128]{3,2,1,0:T(8,128)S(1)} collective-permute-done((f32[2,18,8,128]{3,2,1,0:T(8,128)S(1)}, f32[2,18,8,128]{3,2,1,0:T(8,128)S(1)}, u32[]{:S(2)}, u32[]{:S(2)}) %collective-permute-start.6) | collective-permute-done | bytes 147488 | tf_op jit(solution)/shard_map/ppermute | solution.py:384
  63.5 0.0 collective-permute-done.7.under_ref
  63.5 2.2 %shard_map.101 = (f32[8,2,16,128]{3,2,1,0:T(8,128)S(1)}, f32[2,12,8,128]{3,2,1,0:T(8,128)S(1)}, f32[2,12,8,128]{3,2,1,0:T(8,128)S(1)}, f32[4,16,128]{2,1,0:T(8,128)S(1)}) custom-call(f32[2,32,128]{2,1,0:T(8,128)S(1)} %get-tuple-element.26.counts_ref, f32[12,2,16,128]{3,2,1,0:T(8,128)S(1)} %get-tuple-element.29.state_ref, ...), custom_call_target="tpu_custom_call" | custom-call | flops 20000 | bytes 20000 | tf_op jit(solution)/shard_map/pallas_call | solution.py:40
  65.7 0.0 collective-permute-start.8
  65.7 3.0 %collective-permute-start.9 = (f32[2,12,8,128]{3,2,1,0:T(8,128)S(1)}, f32[2,12,8,128]{3,2,1,0:T(8,128)S(1)}, u32[]{:S(2)}, u32[]{:S(2)}) collective-permute-start(f32[2,12,8,128]{3,2,1,0:T(8,128)S(1)} %get-tuple-element.36), channel_id=1, source_target_pairs={{0,496},{16,0},{32,16},{48,32},{64,48},{80,64},{96,80},{112,96},{1... | collective-permute-start | bytes 294920 | tf_op jit(solution)/shard_map/ppermute | solution.py:384
  68.7 2.3 %collective-permute-done.8.over_ref = f32[2,12,8,128]{3,2,1,0:T(8,128)S(1)} collective-permute-done((f32[2,12,8,128]{3,2,1,0:T(8,128)S(1)}, f32[2,12,8,128]{3,2,1,0:T(8,128)S(1)}, u32[]{:S(2)}, u32[]{:S(2)}) %collective-permute-start.8) | collective-permute-done | bytes 98336 | tf_op jit(solution)/shard_map/ppermute | solution.py:384
  71.0 0.0 collective-permute-done.9.under_ref
  71.0 2.0 %shard_map.102 = (f32[4,16,128]{2,1,0:T(8,128)}, f32[4,16,128]{2,1,0:T(8,128)}) custom-call(f32[2,32,128]{2,1,0:T(8,128)S(1)} %get-tuple-element.26.counts_ref, f32[8,2,16,128]{3,2,1,0:T(8,128)S(1)} %get-tuple-element.34.state_ref, f32[5,12,2,32,128]{4,3,2,1,0:T(8,128)S(1)} %get-tuple-element.30.fixed_ref, ...), custom_call_target="tpu_custom_call" | custom-call | flops 20000 | bytes 20000 | tf_op jit(solution)/shard_map/pallas_call | solution.py:40
  (1 shorter events, 0.0 us)
Async XLA Ops:
  0.6 61.2 %copy-start.2 = (s32[32,4]{0,1:T(4,128)S(1)}, s32[32,4]{0,1:T(4,128)}, u32[]{:S(2)}) copy-start(s32[32,4]{0,1:T(4,128)} %param.15) | copy-start | bytes 1540
  2.7 10.9 %collective-permute-start = (f32[6,4,16,128]{3,2,1,0:T(8,128)}, f32[6,4,16,128]{3,2,1,0:T(8,128)S(1)}, u32[]{:S(2)}, u32[]{:S(2)}) collective-permute-start(f32[6,4,16,128]{3,2,1,0:T(8,128)} %get-tuple-element.20.own_ref), channel_id=1, source_target_pairs={{0,1},{1,2},{2,3},{4,5},{5,6},{6,7},{8,9},{9,10},{10,11},{12,13},{... | collective-permute-start | bytes 589832 | tf_op jit(solution)/shard_map/ppermute | solution.py:384
  6.2 9.0 %collective-permute-start.1 = (f32[6,4,16,128]{3,2,1,0:T(8,128)}, f32[6,4,16,128]{3,2,1,0:T(8,128)S(1)}, u32[]{:S(2)}, u32[]{:S(2)}) collective-permute-start(f32[6,4,16,128]{3,2,1,0:T(8,128)} %get-tuple-element.20.own_ref), channel_id=1, source_target_pairs={{1,0},{2,1},{3,2},{5,4},{6,5},{7,6},{9,8},{10,9},{11,10},{13,12},{... | collective-permute-start | bytes 589832 | tf_op jit(solution)/shard_map/ppermute | solution.py:384
  15.2 0.9 %copy-start = (f32[6,4,16,128]{3,2,1,0:T(8,128)S(1)}, f32[6,4,16,128]{3,2,1,0:T(8,128)}, u32[]{:S(2)}) copy-start(f32[6,4,16,128]{3,2,1,0:T(8,128)} %get-tuple-element.20.own_ref) | copy-start | bytes 589828
  16.5 25.1 %collective-permute-start.2 = (f32[14,16,128]{2,1,0:T(8,128)S(1)}, f32[14,16,128]{2,1,0:T(8,128)S(1)}, u32[]{:S(2)}, u32[]{:S(2)}) collective-permute-start(f32[14,16,128]{2,1,0:T(8,128)S(1)} %get-tuple-element.21), channel_id=1, source_target_pairs={{0,4},{4,8},{8,12},{1,5},{5,9},{9,13},{2,6},{6,10},{10,14},{3,7},{... | collective-permute-start | bytes 344072 | tf_op jit(solution)/shard_map/ppermute | solution.py:384
  19.3 22.3 %collective-permute-start.3 = (f32[14,16,128]{2,1,0:T(8,128)S(1)}, f32[14,16,128]{2,1,0:T(8,128)S(1)}, u32[]{:S(2)}, u32[]{:S(2)}) collective-permute-start(f32[14,16,128]{2,1,0:T(8,128)S(1)} %get-tuple-element.22), channel_id=1, source_target_pairs={{4,0},{8,4},{12,8},{5,1},{9,5},{13,9},{6,2},{10,6},{14,10},{7,3},{... | collective-permute-start | bytes 344072 | tf_op jit(solution)/shard_map/ppermute | solution.py:384
  20.6 35.9 %all-to-all-start = ((f32[128,1,128]{2,1,0:T(1,128)}), f32[128,1,128]{2,1,0:T(1,128)S(1)}, u32[]{:S(2)}, u32[]{:S(2)}) async-start(f32[128,1,128]{2,1,0:T(1,128)} %bitcast.12), calls=%async_computation | async-start | bytes 131072 | tf_op jit(solution)/shard_map/all_to_all | solution.py:404
  41.6 0.9 %copy-start.1 = (f32[6,4,16,128]{3,2,1,0:T(8,128)S(1)}, f32[6,4,16,128]{3,2,1,0:T(8,128)}, u32[]{:S(2)}) copy-start(f32[6,4,16,128]{3,2,1,0:T(8,128)} %get-tuple-element.20.own_ref) | copy-start | bytes 589828
  43.2 18.6 %collective-permute-start.4 = (f32[81,8,128]{2,1,0:T(8,128)S(1)}, f32[81,8,128]{2,1,0:T(8,128)S(1)}, u32[]{:S(2)}, u32[]{:S(2)}) collective-permute-start(f32[81,8,128]{2,1,0:T(8,128)S(1)} %get-tuple-element.24), channel_id=1, source_target_pairs={{0,16},{16,32},{32,48},{48,64},{64,80},{80,96},{96,112},{112,128},... | collective-permute-start | bytes 995336 | tf_op jit(solution)/shard_map/ppermute | solution.py:384
  43.2 18.6 %collective-permute-start.5 = (f32[81,8,128]{2,1,0:T(8,128)S(1)}, f32[81,8,128]{2,1,0:T(8,128)S(1)}, u32[]{:S(2)}, u32[]{:S(2)}) collective-permute-start(f32[81,8,128]{2,1,0:T(8,128)S(1)} %get-tuple-element.25), channel_id=1, source_target_pairs={{0,496},{16,0},{32,16},{48,32},{64,48},{80,64},{96,80},{112,96},{1... | collective-permute-start | bytes 995336 | tf_op jit(solution)/shard_map/ppermute | solution.py:384
  57.7 5.8 %collective-permute-start.6 = (f32[2,18,8,128]{3,2,1,0:T(8,128)S(1)}, f32[2,18,8,128]{3,2,1,0:T(8,128)S(1)}, u32[]{:S(2)}, u32[]{:S(2)}) collective-permute-start(f32[2,18,8,128]{3,2,1,0:T(8,128)S(1)} %get-tuple-element.31), channel_id=1, source_target_pairs={{0,16},{16,32},{32,48},{48,64},{64,80},{80,96},{96,112},{112,128},... | collective-permute-start | bytes 442376 | tf_op jit(solution)/shard_map/ppermute | solution.py:384
  58.2 5.3 %collective-permute-start.7 = (f32[2,18,8,128]{3,2,1,0:T(8,128)S(1)}, f32[2,18,8,128]{3,2,1,0:T(8,128)S(1)}, u32[]{:S(2)}, u32[]{:S(2)}) collective-permute-start(f32[2,18,8,128]{3,2,1,0:T(8,128)S(1)} %get-tuple-element.32), channel_id=1, source_target_pairs={{0,496},{16,0},{32,16},{48,32},{64,48},{80,64},{96,80},{112,96},{1... | collective-permute-start | bytes 442376 | tf_op jit(solution)/shard_map/ppermute | solution.py:384
  65.7 5.3 %collective-permute-start.8 = (f32[2,12,8,128]{3,2,1,0:T(8,128)S(1)}, f32[2,12,8,128]{3,2,1,0:T(8,128)S(1)}, u32[]{:S(2)}, u32[]{:S(2)}) collective-permute-start(f32[2,12,8,128]{3,2,1,0:T(8,128)S(1)} %get-tuple-element.35), channel_id=1, source_target_pairs={{0,16},{16,32},{32,48},{48,64},{64,80},{80,96},{96,112},{112,128},... | collective-permute-start | bytes 294920 | tf_op jit(solution)/shard_map/ppermute | solution.py:384
  65.7 5.2 %collective-permute-start.9 = (f32[2,12,8,128]{3,2,1,0:T(8,128)S(1)}, f32[2,12,8,128]{3,2,1,0:T(8,128)S(1)}, u32[]{:S(2)}, u32[]{:S(2)}) collective-permute-start(f32[2,12,8,128]{3,2,1,0:T(8,128)S(1)} %get-tuple-element.36), channel_id=1, source_target_pairs={{0,496},{16,0},{32,16},{48,32},{64,48},{80,64},{96,80},{112,96},{1... | collective-permute-start | bytes 294920 | tf_op jit(solution)/shard_map/ppermute | solution.py:384
